TPU v7x, 512 devices: a whole 4x8x8 slice. The times are simulated.
512 devices in a mesh: dp: 32 (over y_lo, z, core), mp: 16 (over x, y_hi).
Axes of the slice: x: 4, y: 8 (y_hi: 4, y_lo: 2; y = y_hi * 2 + y_lo), z: 8, core: 2. Of those that a mesh axis runs over, the one named last changes fastest.
Arguments:
- inputs: bfloat16 [4096, 6144], P('dp', 'mp'), may hold values from -6 to 6
- up_weight: bfloat16 [16, 5, 6, 128, 128], P('mp'), may hold values from -0.25 to 0.25
- up_pick: int32 [16, 5, 6], P('mp'), may hold values from 0 to 2
- down_weight: bfloat16 [16, 5, 3, 2, 128, 128], P('mp'), may hold values from -0.15625 to 0.15625
- down_pick: int32 [16, 5, 3, 2], P('mp'), may hold values from 0 to 5
- cotangent: bfloat16 [4096, 6144], P('dp', 'mp'), may hold values from -6 to 6
Outputs:
- output: bfloat16 [4096, 6144], P('dp', 'mp')
- input_grad: bfloat16 [4096, 6144], P('dp', 'mp')
- up_grad: bfloat16 [16, 5, 6, 128, 128], P('mp')
- down_grad: bfloat16 [16, 5, 3, 2, 128, 128], P('mp')
All inputs are finite; a program needn't handle non-finite values.
Results may differ from a plain program's by a relative error of at most 0.005.
Values may be sent and summed in bfloat16 or wider, within the bound.
No kernel may reach another device: no remote copies, remote signals or barrier semaphores. Data moves between devices by JAX's collectives and lax.ppermute only.
A program may use at most 64 MiB of HBM per device.

v0:
```python
import math

import jax
import jax.numpy as jnp
from jax import lax
from jax.sharding import PartitionSpec as P


def from_partner(block, axis, bit):
    count = lax.axis_size(axis)
    route = []
    for low in range(count):
        high = low | 1 << bit
        if high != low and high < count:
            route += [(low, high), (high, low)]
    return lax.ppermute(block, axis, route)


def select_blocks(source, chosen_ids, block_count):
    row_count = source.shape[0]
    blocks = source.reshape(row_count, block_count, -1)
    return jnp.take(blocks, chosen_ids, axis=1)


def place_blocks(partial_terms, chosen_ids, block_count):
    onehot = (chosen_ids[:, None] == jnp.arange(block_count, dtype=jnp.int32)[None, :]).astype(
        jnp.float32
    )
    return jnp.einsum("tmb,mn->tnb", partial_terms, onehot, precision=lax.Precision.HIGHEST)


def gelu_tanh(values_in):
    return jax.nn.gelu(values_in, approximate=True)


def local(inputs, up_weight, up_pick, down_weight, down_pick, cotangent):
    bit_count = lax.axis_size("mp").bit_length() - 1
    levels = bit_count + 1
    tokens, feature_width = inputs.shape
    in_blocks = down_weight.shape[2]
    hid_blocks = up_weight.shape[2]
    per_slot = down_weight.shape[3]
    block_size = up_weight.shape[3]
    grad_scale = 1.0 / math.sqrt(tokens * lax.axis_size("dp"))
    up_local = up_weight[0]
    up_ids = up_pick[0]
    down_local = down_weight[0]
    flat_ids = down_pick[0].reshape(levels, in_blocks * per_slot)
    sources = [inputs] + [from_partner(inputs, "mp", bit_num) for bit_num in range(bit_count)]
    picked_in = jnp.stack(
        [
            select_blocks(sources[level_num], up_ids[level_num], in_blocks)
            for level_num in range(levels)
        ],
        axis=1,
    )
    hidden = jnp.einsum("tlob,lobc->toc", picked_in, up_local, preferred_element_type=jnp.float32)
    activation = gelu_tanh(hidden).astype(jnp.bfloat16)
    act_flat = activation.reshape(tokens, hid_blocks * block_size)
    dy_blocks = cotangent.reshape(tokens, in_blocks, block_size)
    hidden_all = [act_flat] + [
        from_partner(act_flat, "mp", bit_num) for bit_num in range(bit_count)
    ]
    picked_hid = jnp.stack(
        [
            select_blocks(hidden_all[level_num], flat_ids[level_num], hid_blocks).reshape(
                tokens, in_blocks, per_slot, block_size
            )
            for level_num in range(levels)
        ],
        axis=1,
    )
    result = jnp.einsum(
        "tlokb,lokbc->toc", picked_hid, down_local, preferred_element_type=jnp.float32
    )
    down_part = jnp.einsum(
        "tlokb,toc->lokbc", picked_hid, dy_blocks, preferred_element_type=jnp.float32
    )
    back_terms = jnp.einsum(
        "toc,lokbc->tlokb", dy_blocks, down_local, preferred_element_type=jnp.float32
    )
    back_terms = back_terms.reshape(tokens, levels, in_blocks * per_slot, block_size)
    act_grad = place_blocks(back_terms[:, 0], flat_ids[0], hid_blocks)
    for bit_num in range(bit_count):
        placed = place_blocks(back_terms[:, bit_num + 1], flat_ids[bit_num + 1], hid_blocks)
        act_grad = act_grad + from_partner(placed, "mp", bit_num)
    _, gelu_back = jax.vjp(gelu_tanh, hidden)
    hidden_grad = gelu_back(act_grad)[0].astype(jnp.bfloat16)
    up_part = jnp.einsum(
        "tlob,toc->lobc", picked_in, hidden_grad, preferred_element_type=jnp.float32
    )
    in_terms = jnp.einsum(
        "toc,lobc->tlob", hidden_grad, up_local, preferred_element_type=jnp.float32
    )
    grad_inputs = place_blocks(in_terms[:, 0], up_ids[0], in_blocks)
    for bit_num in range(bit_count):
        placed = place_blocks(in_terms[:, bit_num + 1], up_ids[bit_num + 1], in_blocks)
        grad_inputs = grad_inputs + from_partner(placed, "mp", bit_num)
    up_sum, down_sum = lax.psum((up_part, down_part), "dp")
    up_out = (up_sum * grad_scale).astype(jnp.bfloat16)
    down_out = (down_sum * grad_scale).astype(jnp.bfloat16)
    return (
        result.reshape(tokens, feature_width).astype(jnp.bfloat16),
        grad_inputs.reshape(tokens, feature_width).astype(jnp.bfloat16),
        up_out[None],
        down_out[None],
    )


def solution(mesh):
    placed = (
        P("dp", "mp"),
        P("mp", None, None, None, None),
        P("mp", None, None),
        P("mp", None, None, None, None, None),
        P("mp", None, None, None),
        P("dp", "mp"),
    )
    return jax.shard_map(
        local,
        mesh=mesh,
        in_specs=placed,
        out_specs=(
            P("dp", "mp"),
            P("dp", "mp"),
            P("mp", None, None, None, None),
            P("mp", None, None, None, None, None),
        ),
        check_vma=False,
    )
```

profile of v0, /device:TPU:1, one launch (start us, length us, event | category | flops | bytes accessed | tf_op | source)
XLA Modules:
  0.0 394.7 jit_solution(11813904766488361084)
XLA Ops:
  8.3 5.0 %collective-permute-start = (bf16[128,384]{0,1:T(8,128)(2,1)S(1)}, bf16[128,384]{0,1:T(8,128)(2,1)}, u32[]{:S(2)}, u32[]{:S(2)}) collective-permute-start(bf16[128,384]{0,1:T(8,128)(2,1)S(1)} %copy.118), channel_id=1, source_target_pairs={{0,1},{1,0},{2,3},{3,2},{4,5},{5,4},{6,7},{7,6},{8,9},{9,8},{10,11... | collective-permute-start | bytes 294920 | tf_op jit(solution)/shard_map/ppermute | solution.py:16
  13.4 5.7 %collective-permute-start.1 = (bf16[128,384]{0,1:T(8,128)(2,1)S(1)}, bf16[128,384]{0,1:T(8,128)(2,1)}, u32[]{:S(2)}, u32[]{:S(2)}) collective-permute-start(bf16[128,384]{0,1:T(8,128)(2,1)S(1)} %copy.118), channel_id=1, source_target_pairs={{0,2},{2,0},{1,3},{3,1},{4,6},{6,4},{5,7},{7,5},{8,10},{10,8},{9,1... | collective-permute-start | bytes 294920 | tf_op jit(solution)/shard_map/ppermute | solution.py:16
  19.0 3.1 collective-permute-start.2
  22.1 4.4 %collective-permute-start.3 = (bf16[128,384]{0,1:T(8,128)(2,1)S(1)}, bf16[128,384]{0,1:T(8,128)(2,1)}, u32[]{:S(2)}, u32[]{:S(2)}) collective-permute-start(bf16[128,384]{0,1:T(8,128)(2,1)S(1)} %copy.118), channel_id=1, source_target_pairs={{0,8},{8,0},{1,9},{9,1},{2,10},{10,2},{3,11},{11,3},{4,12},{12,4},... | collective-permute-start | bytes 294920 | tf_op jit(solution)/shard_map/ppermute | solution.py:16
  27.5 2.9 convolution_bitcast_fusion.3
  30.4 1.9 copy.142
  34.0 1.6 fusion.13
  36.6 2.4 collective-permute-start.11
  53.9 2.2 collective-permute-start.10
  57.1 3.5 collective-permute-start.9
  61.7 2.2 collective-permute-start.8
  70.8 10.2 %collective-permute-done.9 = f32[128,6,128]{0,2,1:T(8,128)} collective-permute-done((f32[128,6,128]{0,2,1:T(8,128)}, f32[128,6,128]{0,2,1:T(8,128)}, u32[]{:S(2)}, u32[]{:S(2)}) %collective-permute-start.9) | collective-permute-done | bytes 393248 | tf_op jit(solution)/shard_map/ppermute | solution.py:16
  81.0 15.9 %collective-permute-done.8 = f32[128,6,128]{0,2,1:T(8,128)} collective-permute-done((f32[128,6,128]{0,2,1:T(8,128)}, f32[128,6,128]{0,2,1:T(8,128)}, u32[]{:S(2)}, u32[]{:S(2)}) %collective-permute-start.8) | collective-permute-done | bytes 393248 | tf_op jit(solution)/shard_map/ppermute | solution.py:16
  96.9 2.1 fusion.29
  99.1 1.9 collective-permute-start.4
  101.0 6.5 %collective-permute-start.5 = (bf16[128,768]{0,1:T(8,128)(2,1)S(1)}, bf16[128,768]{0,1:T(8,128)(2,1)S(1)}, u32[]{:S(2)}, u32[]{:S(2)}) collective-permute-start(bf16[128,768]{0,1:T(8,128)(2,1)S(1)} %bitcast.234), channel_id=1, source_target_pairs={{0,2},{2,0},{1,3},{3,1},{4,6},{6,4},{5,7},{7,5},{8,10},{10,8},{9,1... | collective-permute-start | bytes 589832 | tf_op jit(solution)/shard_map/ppermute | solution.py:16
  107.5 3.1 collective-permute-start.6
  110.7 4.4 %collective-permute-start.7 = (bf16[128,768]{0,1:T(8,128)(2,1)S(1)}, bf16[128,768]{0,1:T(8,128)(2,1)}, u32[]{:S(2)}, u32[]{:S(2)}) collective-permute-start(bf16[128,768]{0,1:T(8,128)(2,1)S(1)} %bitcast.236), channel_id=1, source_target_pairs={{0,8},{8,0},{1,9},{9,1},{2,10},{10,2},{3,11},{11,3},{4,12},{12,4},... | collective-permute-start | bytes 589832 | tf_op jit(solution)/shard_map/ppermute | solution.py:16
  115.7 1.7 convolution_bitcast_fusion.1
  126.6 1.8 convolution_bitcast_fusion
  130.4 4.3 %collective-permute-start.15 = (f32[128,3,128]{2,1,0:T(4,128)}, f32[128,3,128]{2,1,0:T(4,128)S(1)}, u32[]{:S(2)}, u32[]{:S(2)}) collective-permute-start(f32[128,3,128]{2,1,0:T(4,128)} %convolution_bitcast_fusion.5), channel_id=1, source_target_pairs={{0,8},{8,0},{1,9},{9,1},{2,10},{10,2},{3,11},{11,3},{4,12},{12,4},... | collective-permute-start | bytes 589832 | tf_op jit(solution)/shard_map/ppermute | solution.py:16
  134.7 1.3 convolution_bitcast_fusion.6
  136.0 2.4 collective-permute-start.14
  138.4 1.3 convolution_bitcast_fusion.7
  139.7 5.1 %collective-permute-start.13 = (f32[128,3,128]{2,1,0:T(4,128)}, f32[128,3,128]{2,1,0:T(4,128)S(1)}, u32[]{:S(2)}, u32[]{:S(2)}) collective-permute-start(f32[128,3,128]{2,1,0:T(4,128)} %convolution_bitcast_fusion.7), channel_id=1, source_target_pairs={{0,2},{2,0},{1,3},{3,1},{4,6},{6,4},{5,7},{7,5},{8,10},{10,8},{9,1... | collective-permute-start | bytes 589832 | tf_op jit(solution)/shard_map/ppermute | solution.py:16
  144.8 1.3 convolution_bitcast_fusion.8
  146.1 5.5 %collective-permute-start.12 = (f32[128,3,128]{2,1,0:T(4,128)}, f32[128,3,128]{2,1,0:T(4,128)S(1)}, u32[]{:S(2)}, u32[]{:S(2)}) collective-permute-start(f32[128,3,128]{2,1,0:T(4,128)} %convolution_bitcast_fusion.8), channel_id=1, source_target_pairs={{0,1},{1,0},{2,3},{3,2},{4,5},{5,4},{6,7},{7,6},{8,9},{9,8},{10,11... | collective-permute-start | bytes 589832 | tf_op jit(solution)/shard_map/ppermute | solution.py:16
  152.8 21.2 %collective-permute-done.12 = f32[128,3,128]{2,1,0:T(4,128)S(1)} collective-permute-done((f32[128,3,128]{2,1,0:T(4,128)}, f32[128,3,128]{2,1,0:T(4,128)S(1)}, u32[]{:S(2)}, u32[]{:S(2)}) %collective-permute-start.12) | collective-permute-done | bytes 196640 | tf_op jit(solution)/shard_map/ppermute | solution.py:16
  175.5 206.5 %all-reduce.3.cloned.1.call-done = (f32[5,6,128,128]{2,3,0,1:T(8,128)}, f32[5,3,2,128,128]{4,3,2,0,1:T(8,128)}) async-done(((f32[5,6,128,128]{2,3,0,1:T(8,128)}, f32[5,3,2,128,128]{4,3,2,0,1:T(8,128)}), (f32[5,6,128,128]{2,3,0,1:T(8,128)}, f32[5,3,2,128,128]{4,3,2,0,1:T(8,128)})) %all-reduce.3.cloned.1.call-update) | async-done | bytes 3932176 | tf_op jit(solution)/shard_map/psum | solution.py:99
  382.0 1.8 fusion.6
  383.8 1.3 copy.165
  385.1 1.8 fusion.7
  (137 shorter events, 43.8 us)
Async XLA Ops:
  7.2 89.8 %copy-start = (bf16[1,5,6,128,128]{4,3,2,1,0:T(8,128)(2,1)S(1)}, bf16[1,5,6,128,128]{4,3,2,1,0:T(8,128)(2,1)}, u32[]{:S(2)}) copy-start(bf16[1,5,6,128,128]{4,3,2,1,0:T(8,128)(2,1)} %param.11) | copy-start | bytes 2949124
  7.2 374.8 %all-reduce.3.cloned.1.call-start = ((), (), s32[]{:S(2)}) async-start(), calls=%async_computation | async-start | bytes 7864320 | tf_op jit(solution)/shard_map/psum | solution.py:99
  8.3 45.6 %collective-permute-start = (bf16[128,384]{0,1:T(8,128)(2,1)S(1)}, bf16[128,384]{0,1:T(8,128)(2,1)}, u32[]{:S(2)}, u32[]{:S(2)}) collective-permute-start(bf16[128,384]{0,1:T(8,128)(2,1)S(1)} %copy.118), channel_id=1, source_target_pairs={{0,1},{1,0},{2,3},{3,2},{4,5},{5,4},{6,7},{7,6},{8,9},{9,8},{10,11... | collective-permute-start | bytes 294920 | tf_op jit(solution)/shard_map/ppermute | solution.py:16
  13.4 43.7 %collective-permute-start.1 = (bf16[128,384]{0,1:T(8,128)(2,1)S(1)}, bf16[128,384]{0,1:T(8,128)(2,1)}, u32[]{:S(2)}, u32[]{:S(2)}) collective-permute-start(bf16[128,384]{0,1:T(8,128)(2,1)S(1)} %copy.118), channel_id=1, source_target_pairs={{0,2},{2,0},{1,3},{3,1},{4,6},{6,4},{5,7},{7,5},{8,10},{10,8},{9,1... | collective-permute-start | bytes 294920 | tf_op jit(solution)/shard_map/ppermute | solution.py:16
  19.0 42.6 %collective-permute-start.2 = (bf16[128,384]{0,1:T(8,128)(2,1)S(1)}, bf16[128,384]{0,1:T(8,128)(2,1)}, u32[]{:S(2)}, u32[]{:S(2)}) collective-permute-start(bf16[128,384]{0,1:T(8,128)(2,1)S(1)} %copy.118), channel_id=1, source_target_pairs={{0,4},{4,0},{1,5},{5,1},{2,6},{6,2},{3,7},{7,3},{8,12},{12,8},{9,1... | collective-permute-start | bytes 294920 | tf_op jit(solution)/shard_map/ppermute | solution.py:16
  22.1 42.7 %collective-permute-start.3 = (bf16[128,384]{0,1:T(8,128)(2,1)S(1)}, bf16[128,384]{0,1:T(8,128)(2,1)}, u32[]{:S(2)}, u32[]{:S(2)}) collective-permute-start(bf16[128,384]{0,1:T(8,128)(2,1)S(1)} %copy.118), channel_id=1, source_target_pairs={{0,8},{8,0},{1,9},{9,1},{2,10},{10,2},{3,11},{11,3},{4,12},{12,4},... | collective-permute-start | bytes 294920 | tf_op jit(solution)/shard_map/ppermute | solution.py:16
  33.5 10.3 %copy-start.3 = (f32[128,1,6,128]{3,0,2,1:T(8,128)S(1)}, f32[128,1,6,128]{3,0,2,1:T(8,128)}, u32[]{:S(2)}) copy-start(f32[128,1,6,128]{3,0,2,1:T(8,128)} %get-tuple-element.45) | copy-start | bytes 1179652
  34.0 11.4 %copy-start.2 = (f32[128,1,6,128]{3,0,2,1:T(8,128)S(1)}, f32[128,1,6,128]{3,0,2,1:T(8,128)}, u32[]{:S(2)}) copy-start(f32[128,1,6,128]{3,0,2,1:T(8,128)} %get-tuple-element.46) | copy-start | bytes 1179652
  36.6 34.1 %collective-permute-start.11 = (f32[128,6,128]{0,2,1:T(8,128)}, f32[128,6,128]{0,2,1:T(8,128)}, u32[]{:S(2)}, u32[]{:S(2)}) collective-permute-start(f32[128,6,128]{0,2,1:T(8,128)} %bitcast.64), channel_id=1, source_target_pairs={{0,8},{8,0},{1,9},{9,1},{2,10},{10,2},{3,11},{11,3},{4,12},{12,4},... | collective-permute-start | bytes 1179656 | tf_op jit(solution)/shard_map/ppermute | solution.py:16
  43.9 3.1 copy-start.1
  46.9 3.2 copy-start.9
  46.9 6.2 %copy-start.17 = (s32[6]{0:T(128)S(1)}, s32[6]{0:T(128)}, u32[]{:S(2)}) copy-start(s32[6]{0:T(128)} %compare_select_fusion.2) | copy-start | bytes 76
  46.9 6.2 %copy-start.18 = (s32[6]{0:T(128)S(1)}, s32[6]{0:T(128)}, u32[]{:S(2)}) copy-start(s32[6]{0:T(128)} %compare_select_fusion.1) | copy-start | bytes 76
  47.5 6.4 %copy-start.16 = (s32[6]{0:T(128)S(1)}, s32[6]{0:T(128)}, u32[]{:S(2)}) copy-start(s32[6]{0:T(128)} %compare_select_fusion) | copy-start | bytes 76
  47.5 6.4 %copy-start.5 = (f32[6,128,128]{1,2,0:T(8,128)S(1)}, f32[6,128,128]{1,2,0:T(8,128)}, u32[]{:S(2)}) copy-start(f32[6,128,128]{1,2,0:T(8,128)} %copy.150) | copy-start | bytes 1179652
  53.9 16.9 %collective-permute-start.10 = (f32[128,6,128]{0,2,1:T(8,128)S(1)}, f32[128,6,128]{0,2,1:T(8,128)}, u32[]{:S(2)}, u32[]{:S(2)}) collective-permute-start(f32[128,6,128]{0,2,1:T(8,128)S(1)} %bitcast.230), channel_id=1, source_target_pairs={{0,4},{4,0},{1,5},{5,1},{2,6},{6,2},{3,7},{7,3},{8,12},{12,8},{9,1... | collective-permute-start | bytes 1179656 | tf_op jit(solution)/shard_map/ppermute | solution.py:16
  57.1 23.9 %collective-permute-start.9 = (f32[128,6,128]{0,2,1:T(8,128)}, f32[128,6,128]{0,2,1:T(8,128)}, u32[]{:S(2)}, u32[]{:S(2)}) collective-permute-start(f32[128,6,128]{0,2,1:T(8,128)} %bitcast.58), channel_id=1, source_target_pairs={{0,2},{2,0},{1,3},{3,1},{4,6},{6,4},{5,7},{7,5},{8,10},{10,8},{9,1... | collective-permute-start | bytes 1179656 | tf_op jit(solution)/shard_map/ppermute | solution.py:16
  61.7 35.3 %collective-permute-start.8 = (f32[128,6,128]{0,2,1:T(8,128)}, f32[128,6,128]{0,2,1:T(8,128)}, u32[]{:S(2)}, u32[]{:S(2)}) collective-permute-start(f32[128,6,128]{0,2,1:T(8,128)} %bitcast.55), channel_id=1, source_target_pairs={{0,1},{1,0},{2,3},{3,2},{4,5},{5,4},{6,7},{7,6},{8,9},{9,8},{10,11... | collective-permute-start | bytes 1179656 | tf_op jit(solution)/shard_map/ppermute | solution.py:16
  64.8 3.6 copy-start.10
  99.1 18.4 %copy-start.15 = (pred[6]{0:T(512)(128)(4,1)S(1)}, pred[6]{0:T(512)(128)(4,1)}, u32[]{:S(2)}) copy-start(pred[6]{0:T(512)(128)(4,1)} %compare_and_fusion.4) | copy-start | bytes 22
  99.1 18.7 %collective-permute-start.4 = (bf16[128,768]{0,1:T(8,128)(2,1)S(1)}, bf16[128,768]{0,1:T(8,128)(2,1)S(1)}, u32[]{:S(2)}, u32[]{:S(2)}) collective-permute-start(bf16[128,768]{0,1:T(8,128)(2,1)S(1)} %bitcast.233), channel_id=1, source_target_pairs={{0,1},{1,0},{2,3},{3,2},{4,5},{5,4},{6,7},{7,6},{8,9},{9,8},{10,11... | collective-permute-start | bytes 589832 | tf_op jit(solution)/shard_map/ppermute | solution.py:16
  101.0 18.5 %collective-permute-start.5 = (bf16[128,768]{0,1:T(8,128)(2,1)S(1)}, bf16[128,768]{0,1:T(8,128)(2,1)S(1)}, u32[]{:S(2)}, u32[]{:S(2)}) collective-permute-start(bf16[128,768]{0,1:T(8,128)(2,1)S(1)} %bitcast.234), channel_id=1, source_target_pairs={{0,2},{2,0},{1,3},{3,1},{4,6},{6,4},{5,7},{7,5},{8,10},{10,8},{9,1... | collective-permute-start | bytes 589832 | tf_op jit(solution)/shard_map/ppermute | solution.py:16
  107.5 13.8 %collective-permute-start.6 = (bf16[128,768]{0,1:T(8,128)(2,1)S(1)}, bf16[128,768]{0,1:T(8,128)(2,1)}, u32[]{:S(2)}, u32[]{:S(2)}) collective-permute-start(bf16[128,768]{0,1:T(8,128)(2,1)S(1)} %bitcast.235), channel_id=1, source_target_pairs={{0,4},{4,0},{1,5},{5,1},{2,6},{6,2},{3,7},{7,3},{8,12},{12,8},{9,1... | collective-permute-start | bytes 589832 | tf_op jit(solution)/shard_map/ppermute | solution.py:16
  110.7 11.8 %collective-permute-start.7 = (bf16[128,768]{0,1:T(8,128)(2,1)S(1)}, bf16[128,768]{0,1:T(8,128)(2,1)}, u32[]{:S(2)}, u32[]{:S(2)}) collective-permute-start(bf16[128,768]{0,1:T(8,128)(2,1)S(1)} %bitcast.236), channel_id=1, source_target_pairs={{0,8},{8,0},{1,9},{9,1},{2,10},{10,2},{3,11},{11,3},{4,12},{12,4},... | collective-permute-start | bytes 589832 | tf_op jit(solution)/shard_map/ppermute | solution.py:16
  117.5 6.8 %copy-start.14 = (pred[6]{0:T(512)(128)(4,1)S(1)}, pred[6]{0:T(512)(128)(4,1)}, u32[]{:S(2)}) copy-start(pred[6]{0:T(512)(128)(4,1)} %compare_and_fusion.3) | copy-start | bytes 22
  117.7 7.3 %copy-start.13 = (pred[6]{0:T(512)(128)(4,1)S(1)}, pred[6]{0:T(512)(128)(4,1)}, u32[]{:S(2)}) copy-start(pred[6]{0:T(512)(128)(4,1)} %compare_and_fusion.2) | copy-start | bytes 22
  121.3 4.4 %copy-start.12 = (pred[6]{0:T(512)(128)(4,1)S(1)}, pred[6]{0:T(512)(128)(4,1)}, u32[]{:S(2)}) copy-start(pred[6]{0:T(512)(128)(4,1)} %compare_and_fusion.1) | copy-start | bytes 22
  129.1 22.4 %copy-start.4 = (bf16[1,5,3,2,128,128]{5,4,3,2,1,0:T(8,128)(2,1)S(1)}, bf16[1,5,3,2,128,128]{5,4,3,2,1,0:T(8,128)(2,1)}, u32[]{:S(2)}) copy-start(bf16[1,5,3,2,128,128]{5,4,3,2,1,0:T(8,128)(2,1)} %param.13) | copy-start | bytes 2949124
  130.4 22.4 %collective-permute-start.15 = (f32[128,3,128]{2,1,0:T(4,128)}, f32[128,3,128]{2,1,0:T(4,128)S(1)}, u32[]{:S(2)}, u32[]{:S(2)}) collective-permute-start(f32[128,3,128]{2,1,0:T(4,128)} %convolution_bitcast_fusion.5), channel_id=1, source_target_pairs={{0,8},{8,0},{1,9},{9,1},{2,10},{10,2},{3,11},{11,3},{4,12},{12,4},... | collective-permute-start | bytes 589832 | tf_op jit(solution)/shard_map/ppermute | solution.py:16
  136.0 16.8 %collective-permute-start.14 = (f32[128,3,128]{2,1,0:T(4,128)}, f32[128,3,128]{2,1,0:T(4,128)S(1)}, u32[]{:S(2)}, u32[]{:S(2)}) collective-permute-start(f32[128,3,128]{2,1,0:T(4,128)} %convolution_bitcast_fusion.6), channel_id=1, source_target_pairs={{0,4},{4,0},{1,5},{5,1},{2,6},{6,2},{3,7},{7,3},{8,12},{12,8},{9,1... | collective-permute-start | bytes 589832 | tf_op jit(solution)/shard_map/ppermute | solution.py:16
  139.7 13.1 %collective-permute-start.13 = (f32[128,3,128]{2,1,0:T(4,128)}, f32[128,3,128]{2,1,0:T(4,128)S(1)}, u32[]{:S(2)}, u32[]{:S(2)}) collective-permute-start(f32[128,3,128]{2,1,0:T(4,128)} %convolution_bitcast_fusion.7), channel_id=1, source_target_pairs={{0,2},{2,0},{1,3},{3,1},{4,6},{6,4},{5,7},{7,5},{8,10},{10,8},{9,1... | collective-permute-start | bytes 589832 | tf_op jit(solution)/shard_map/ppermute | solution.py:16
  146.1 27.9 %collective-permute-start.12 = (f32[128,3,128]{2,1,0:T(4,128)}, f32[128,3,128]{2,1,0:T(4,128)S(1)}, u32[]{:S(2)}, u32[]{:S(2)}) collective-permute-start(f32[128,3,128]{2,1,0:T(4,128)} %convolution_bitcast_fusion.8), channel_id=1, source_target_pairs={{0,1},{1,0},{2,3},{3,2},{4,5},{5,4},{6,7},{7,6},{8,9},{9,8},{10,11... | collective-permute-start | bytes 589832 | tf_op jit(solution)/shard_map/ppermute | solution.py:16
  (4 other events, 4.7 us)
Sparse Core Ops, SparseCore 0:
  128.5 253.4 all-reduce.2
where the time goes:
time: 396 us; the launch traced here: 395 us
  waiting for transfers between devices  254 us (64%)
  starting transfers between devices  61.6 us (16%)
  local copies, waits for them, and re-layouts  31.5 us (8%)
  matrix products  19.2 us (5%)
  between operations  14.8 us (4%)
  other arithmetic  13.8 us (3%)
    psum x1, waiting for transfers between devices, local(): up_sum, down_sum = lax.psum((up_part, down_part), 'dp')  206 us
    ppermute x16, starting transfers between devices, from_partner(): return lax.ppermute(block, axis, route)  61.6 us
    ppermute x16, waiting for transfers between devices, from_partner(): return lax.ppermute(block, axis, route)  47.4 us
    dot_general x10, matrix products, place_blocks(): jnp.einsum('tmb,mn->tnb', partial_terms, onehot, precision=lax.Precision....  9.64 us
    reshape x9, local copies, waits for them, and re-layouts, select_blocks(): blocks = source.reshape(row_count, block_count, -1)  8.51 us
  transfers between devices with their start and end apart: 17, of which 4 were waited for; matrix products, arithmetic and copies ran while one was open for 12% of the time, Pallas kernels for 0%

commit v1 on v0

v1 whole, which is shorter than its diff:
```python
import functools
import math

import jax
import jax.numpy as jnp
from jax import lax
from jax.experimental import pallas as pl
from jax.experimental.pallas import tpu as pltpu
from jax.sharding import PartitionSpec as P


F32 = jnp.float32
BF16 = jnp.bfloat16
B = 128
GELU_C = math.sqrt(2.0 / math.pi)
GELU_A = 0.044715


VMEM = pl.BlockSpec(memory_space=pltpu.VMEM)
SMEM = pl.BlockSpec(memory_space=pltpu.SMEM)


def sds(shape, dtype):
    return pltpu.VMEM(shape, dtype)


def call(kernel, outs, in_specs, scratch=()):
    run = pl.pallas_call(
        kernel,
        out_shape=outs,
        in_specs=in_specs,
        out_specs=jax.tree.map(lambda _: VMEM, outs),
        scratch_shapes=list(scratch),
        compiler_params=pltpu.CompilerParams(vmem_limit_bytes=16 << 20),
    )

    def body(*args):
        placed = [
            a if spec is SMEM else pltpu.with_memory_space_constraint(a, pltpu.VMEM)
            for a, spec in zip(args, in_specs)
        ]
        return run(*placed)

    return body


def lanes(index):
    return pl.ds(pl.multiple_of(index * B, B), B)


def dot_nt(a, b):
    return lax.dot_general(a, b, (((1,), (1,)), ((), ())), preferred_element_type=F32)


def dot_tn(a, b):
    return lax.dot_general(a, b, (((0,), (0,)), ((), ())), preferred_element_type=F32)


def back_kernel(levels, db, hb, kd, pick, cot, w, *refs):
    outs, acc = refs[:levels], refs[levels]
    for lvl in range(levels):
        acc[...] = jnp.zeros_like(acc)
        for o in range(db):
            both = jnp.concatenate([w[(lvl * db + o) * kd + k] for k in range(kd)], axis=0)
            term = dot_nt(cot[:, o * B : (o + 1) * B], both)
            for k in range(kd):
                spot = pick[(lvl * db + o) * kd + k]
                acc[spot] += term[:, k * B : (k + 1) * B]
        for h in range(hb):
            outs[lvl][:, h * B : (h + 1) * B] = acc[h].astype(outs[lvl].dtype)


def act_kernel(levels, hb, pick, w, *refs):
    xs, act, slope = refs[:levels], refs[levels], refs[levels + 1]
    for o in range(hb):
        lhs = jnp.concatenate(
            [xs[lvl][:, lanes(pick[lvl * hb + o])] for lvl in range(levels)], axis=1
        )
        rhs = jnp.concatenate([w[lvl * hb + o] for lvl in range(levels)], axis=0)
        v = jnp.dot(lhs, rhs, preferred_element_type=F32)
        sq = v * v
        t = jnp.tanh(GELU_C * (v + GELU_A * (v * sq)))
        half = 0.5 * (1.0 + t)
        act[:, o * B : (o + 1) * B] = (v * half).astype(BF16)
        inner = GELU_C * (1.0 + (3.0 * GELU_A) * sq)
        slope[:, o * B : (o + 1) * B] = half + 0.5 * v * (1.0 - t * t) * inner


def split(core, scr, keep, send):
    half = keep.shape[0]
    keep[...] = scr[pl.ds(core * half, half)]
    send[...] = scr[pl.ds((1 - core) * half, half)].astype(BF16)


def up_kernel(levels, hb, pick, core, slope, *refs):
    back, xs = refs[:levels], refs[levels : 2 * levels]
    hg, keep, send, scr = refs[2 * levels :]
    grad = back[0][...]
    for lvl in range(1, levels):
        grad = grad + back[lvl][...].astype(F32)
    hg[...] = (grad * slope[...]).astype(BF16)
    for o in range(hb):
        right = hg[:, o * B : (o + 1) * B]
        for lvl in range(levels):
            left = xs[lvl][:, lanes(pick[lvl * hb + o])]
            scr[lvl * hb + o] = dot_tn(left, right)
    split(core[0], scr, keep, send)


def in_kernel(levels, db, hb, pick, hg, w, *refs):
    outs, acc = refs[:levels], refs[levels]
    for lvl in range(levels):
        acc[...] = jnp.zeros_like(acc)
        for o in range(hb):
            spot = pick[lvl * hb + o]
            acc[spot] += dot_nt(hg[:, o * B : (o + 1) * B], w[lvl * hb + o])
        for d in range(db):
            outs[lvl][:, d * B : (d + 1) * B] = acc[d].astype(outs[lvl].dtype)


def down_kernel(levels, db, kd, pick, core, cot, *refs):
    acts = refs[:levels]
    keep, send, scr = refs[levels:]
    for o in range(db):
        right = cot[:, o * B : (o + 1) * B]
        for lvl in range(levels):
            for k in range(kd):
                i = (lvl * db + o) * kd + k
                scr[i] = dot_tn(acts[lvl][:, lanes(pick[i])], right)
    split(core[0], scr, keep, send)


def out_kernel(levels, db, kd, pick, w, *refs):
    acts, out = refs[:levels], refs[levels]
    for o in range(db):
        spots = [(lvl * db + o) * kd + k for lvl in range(levels) for k in range(kd)]
        lhs = jnp.concatenate(
            [acts[i // (db * kd)][:, lanes(pick[i])] for i in spots], axis=1
        )
        rhs = jnp.concatenate([w[i] for i in spots], axis=0)
        out[:, o * B : (o + 1) * B] = jnp.dot(lhs, rhs, preferred_element_type=F32).astype(BF16)


def from_partner(block, axis, bit):
    count = lax.axis_size(axis)
    return lax.ppermute(block, axis, [(i, i ^ (1 << bit)) for i in range(count)])


def step(inputs, up_weight, up_pick, down_weight, down_pick, cotangent):
    bits = lax.axis_size("mp").bit_length() - 1
    levels = bits + 1
    tokens = inputs.shape[0]
    db, kd = down_weight.shape[2], down_weight.shape[3]
    hb = up_weight.shape[2]
    dp = lax.axis_size("dp")
    chips = dp // 2
    scale = 1.0 / math.sqrt(tokens * dp)
    n_up, n_down = levels * hb, levels * db * kd
    up_w = up_weight.reshape(n_up, B, B)
    down_w = down_weight.reshape(n_down, B, B)
    up_ids = up_pick.reshape(n_up)
    down_ids = down_pick.reshape(n_down)
    core = lax.rem(lax.axis_index("dp"), 2).reshape(1)
    groups = [[2 * i + c for i in range(chips)] for c in range(2)]

    xs = [inputs] + [from_partner(inputs, "mp", b) for b in range(bits)]

    terms = call(
        functools.partial(back_kernel, levels, db, hb, kd),
        [sds((tokens, hb * B), BF16 if lvl else F32) for lvl in range(levels)],
        [SMEM, VMEM, VMEM],
        [pltpu.VMEM((hb, tokens, B), F32)],
    )(down_ids, cotangent, down_w)
    backs = [terms[0]] + [from_partner(terms[b + 1], "mp", b) for b in range(bits)]

    act, slope = call(
        functools.partial(act_kernel, levels, hb),
        [sds((tokens, hb * B), BF16), sds((tokens, hb * B), F32)],
        [SMEM, VMEM] + [VMEM] * levels,
        (),
    )(up_ids, up_w, *xs)
    acts = [act] + [from_partner(act, "mp", b) for b in range(bits)]

    hg, up_keep, up_send = call(
        functools.partial(up_kernel, levels, hb),
        [
            sds((tokens, hb * B), BF16),
            sds((n_up // 2, B, B), F32),
            sds((n_up // 2, B, B), BF16),
        ],
        [SMEM, SMEM, VMEM] + [VMEM] * (2 * levels),
        [pltpu.VMEM((n_up, B, B), F32)],
    )(up_ids, core, slope, *backs, *xs)

    def exchange(block):
        return lax.all_to_all(
            block, "dp", split_axis=0, concat_axis=0, axis_index_groups=groups, tiled=True
        )

    def reduce_shard(keep, send):
        got = from_partner(send, "dp", 0)
        pair = (keep + got.astype(F32)).astype(BF16)
        parts = exchange(pair.reshape(chips, -1, B))
        return (jnp.sum(parts.astype(F32), axis=0) * scale).astype(BF16)

    def gather(shard):
        wide = lax.optimization_barrier(jnp.broadcast_to(shard[None], (chips,) + shard.shape))
        mine = exchange(wide).reshape(-1, B, B)
        other = from_partner(mine, "dp", 0)
        first = core[0] == 0
        return jnp.concatenate(
            [jnp.where(first, mine, other), jnp.where(first, other, mine)], axis=0
        )

    up_shard = reduce_shard(up_keep, up_send)

    in_terms = call(
        functools.partial(in_kernel, levels, db, hb),
        [sds((tokens, db * B), BF16 if lvl else F32) for lvl in range(levels)],
        [SMEM, VMEM, VMEM],
        [pltpu.VMEM((db, tokens, B), F32)],
    )(up_ids, hg, up_w)
    grad_inputs = in_terms[0]
    for b in range(bits):
        grad_inputs = grad_inputs + from_partner(in_terms[b + 1], "mp", b).astype(F32)

    down_keep, down_send = call(
        functools.partial(down_kernel, levels, db, kd),
        [sds((n_down // 2, B, B), F32), sds((n_down // 2, B, B), BF16)],
        [SMEM, SMEM, VMEM] + [VMEM] * levels,
        [pltpu.VMEM((n_down, B, B), F32)],
    )(down_ids, core, cotangent, *acts)
    down_shard = reduce_shard(down_keep, down_send)

    output = call(
        functools.partial(out_kernel, levels, db, kd),
        sds((tokens, db * B), BF16),
        [SMEM, VMEM] + [VMEM] * levels,
        (),
    )(down_ids, down_w, *acts)

    up_out = gather(up_shard)
    down_out = gather(down_shard)
    return (
        output,
        grad_inputs.astype(BF16),
        up_out.reshape(up_weight.shape),
        down_out.reshape(down_weight.shape),
    )


def solution(mesh):
    placed = (
        P("dp", "mp"),
        P("mp", None, None, None, None),
        P("mp", None, None),
        P("mp", None, None, None, None, None),
        P("mp", None, None, None),
        P("dp", "mp"),
    )
    return jax.shard_map(
        step,
        mesh=mesh,
        in_specs=placed,
        out_specs=(
            P("dp", "mp"),
            P("dp", "mp"),
            P("mp", None, None, None, None),
            P("mp", None, None, None, None, None),
        ),
        check_vma=False,
    )
```

time: 396 us -> 169 us (0.43)
  waiting for transfers between devices: 254 us -> 44.1 us
  starting transfers between devices: 61.6 us -> 100 us
  local copies, waits for them, and re-layouts: 31.5 us -> 6.85 us
  matrix products: 19.2 us -> 0 us
  between operations: 14.8 us -> 1.07 us
  Pallas kernels: 0 us -> 8.08 us
  other arithmetic: 13.8 us -> 6.95 us
    psum x1 -> x0, waiting for transfers between devices: 206 us -> none  [local(): up_sum, down_sum = lax.psum((up_part, down_part), 'dp')]
    all_to_all x0 -> x4, starting transfers between devices: none -> 35.8 us  [exchange(): lax.all_to_all(block, 'dp', split_axis=0, concat_axis=0, axis_index_group...]
    ppermute x16 -> x20, waiting for transfers between devices: 47.4 us -> 19.4 us  [from_partner(): return lax.ppermute(block, axis, [(i, i ^ 1 << bit) for i in range(count)])]
    all_to_all x0 -> x4, waiting for transfers between devices: none -> 24.7 us  [exchange(): lax.all_to_all(block, 'dp', split_axis=0, concat_axis=0, axis_index_group...]
    dot_general x16 -> x0, matrix products: 19.2 us -> none  [the longest x10 9.64 us: place_blocks(): jnp.einsum('tmb,mn->tnb', partial_terms, onehot, precision=lax.Precision....]
    reshape x9 -> x2, local copies, waits for them, and re-layouts: 8.51 us -> 0.17 us  [the longest x1 0.09 us: step(): down_ids = down_pick.reshape(n_down)]
    pallas_call x0 -> x6, Pallas kernels: none -> 8.08 us  [body(): return run(*placed)]
    gather x10 -> x0, local copies, waits for them, and re-layouts: 6.34 us -> none  [select_blocks(): return jnp.take(blocks, chosen_ids, axis=1)]
  transfers between devices with their start and end apart: 17 -> 24, of which waited for: 4 -> 7; matrix products, arithmetic and copies ran while one was open for 12% -> 5% of each run, Pallas kernels for 0% -> 4%
where the time goes in v1:
time: 169 us; the launch traced here: 167 us
  starting transfers between devices  100 us (59%)
  waiting for transfers between devices  44.1 us (26%)
  Pallas kernels  8.08 us (5%)
  other arithmetic  6.95 us (4%)
  local copies, waits for them, and re-layouts  6.85 us (4%)
    ppermute x20, starting transfers between devices, from_partner(): return lax.ppermute(block, axis, [(i, i ^ 1 << bit) for i in range(count)])  64.2 us
    all_to_all x4, starting transfers between devices, exchange(): lax.all_to_all(block, 'dp', split_axis=0, concat_axis=0, axis_index_group...  35.8 us
    all_to_all x4, waiting for transfers between devices, exchange(): lax.all_to_all(block, 'dp', split_axis=0, concat_axis=0, axis_index_group...  24.7 us
    ppermute x20, waiting for transfers between devices, from_partner(): return lax.ppermute(block, axis, [(i, i ^ 1 << bit) for i in range(count)])  19.4 us
    pallas_call x6, Pallas kernels, body(): return run(*placed)  8.08 us
    unnamed x20, local copies, waits for them, and re-layouts  5 us
  transfers between devices with their start and end apart: 24, of which 7 were waited for; matrix products, arithmetic and copies ran while one was open for 5% of the time, Pallas kernels for 4%

profile of v1, /device:TPU:1, one launch (start us, length us, event | category | flops | bytes accessed | tf_op | source)
XLA Modules:
  0.0 167.0 jit_solution(16029957099404372925)
XLA Ops:
  0.6 5.5 %collective-permute-start.3 = (bf16[128,384]{1,0:T(8,128)(2,1)}, bf16[128,384]{1,0:T(8,128)(2,1)S(1)}, u32[]{:S(2)}, u32[]{:S(2)}) collective-permute-start(bf16[128,384]{1,0:T(8,128)(2,1)} %refs_5_.1), channel_id=1, source_target_pairs={{0,8},{1,9},{2,10},{3,11},{4,12},{5,13},{6,14},{7,15},{8,0},{9,1},... | collective-permute-start | bytes 294920 | tf_op jit(solution)/shard_map/ppermute | solution.py:146
  6.1 2.2 %collective-permute-start.2 = (bf16[128,384]{1,0:T(8,128)(2,1)}, bf16[128,384]{1,0:T(8,128)(2,1)S(1)}, u32[]{:S(2)}, u32[]{:S(2)}) collective-permute-start(bf16[128,384]{1,0:T(8,128)(2,1)} %refs_5_.1), channel_id=1, source_target_pairs={{0,4},{1,5},{2,6},{3,7},{4,0},{5,1},{6,2},{7,3},{8,12},{9,13},{10,... | collective-permute-start | bytes 294920 | tf_op jit(solution)/shard_map/ppermute | solution.py:146
  8.3 7.5 %collective-permute-start.1 = (bf16[128,384]{1,0:T(8,128)(2,1)}, bf16[128,384]{1,0:T(8,128)(2,1)S(1)}, u32[]{:S(2)}, u32[]{:S(2)}) collective-permute-start(bf16[128,384]{1,0:T(8,128)(2,1)} %refs_5_.1), channel_id=1, source_target_pairs={{0,2},{1,3},{2,0},{3,1},{4,6},{5,7},{6,4},{7,5},{8,10},{9,11},{10,... | collective-permute-start | bytes 294920 | tf_op jit(solution)/shard_map/ppermute | solution.py:146
  18.8 1.8 %shard_map.95 = (f32[128,768]{1,0:T(8,128)S(1)}, bf16[128,768]{1,0:T(8,128)(2,1)}, bf16[128,768]{1,0:T(8,128)(2,1)S(1)}, bf16[128,768]{1,0:T(8,128)(2,1)S(1)}, bf16[128,768]{1,0:T(8,128)(2,1)S(1)}) custom-call(s32[30]{0:T(128)S(1)} %reshape.49.pick, bf16[128,384]{1,0:T(8,128)(2,1)S(1)} %copy-done.4, bf16[30,128,128]{2,1,0:T(8,128)(2,1)S(1)} %bitcast.9), custom_call_target="tpu_custom_call" | custom-call | tf_op jit(solution)/shard_map/pallas_call | solution.py:42
  20.6 2.4 %collective-permute-start.8 = (bf16[128,768]{1,0:T(8,128)(2,1)}, bf16[128,768]{1,0:T(8,128)(2,1)S(1)}, u32[]{:S(2)}, u32[]{:S(2)}) collective-permute-start(bf16[128,768]{1,0:T(8,128)(2,1)} %get-tuple-element.24), channel_id=1, source_target_pairs={{0,1},{1,0},{2,3},{3,2},{4,5},{5,4},{6,7},{7,6},{8,9},{9,8},{10,11... | collective-permute-start | bytes 589832 | tf_op jit(solution)/shard_map/ppermute | solution.py:146
  23.0 3.5 %collective-permute-start.9 = (bf16[128,768]{1,0:T(8,128)(2,1)S(1)}, bf16[128,768]{1,0:T(8,128)(2,1)S(1)}, u32[]{:S(2)}, u32[]{:S(2)}) collective-permute-start(bf16[128,768]{1,0:T(8,128)(2,1)S(1)} %get-tuple-element.25), channel_id=1, source_target_pairs={{0,2},{1,3},{2,0},{3,1},{4,6},{5,7},{6,4},{7,5},{8,10},{9,11},{10,... | collective-permute-start | bytes 589832 | tf_op jit(solution)/shard_map/ppermute | solution.py:146
  26.6 3.1 %collective-permute-start.10 = (bf16[128,768]{1,0:T(8,128)(2,1)S(1)}, bf16[128,768]{1,0:T(8,128)(2,1)S(1)}, u32[]{:S(2)}, u32[]{:S(2)}) collective-permute-start(bf16[128,768]{1,0:T(8,128)(2,1)S(1)} %get-tuple-element.26), channel_id=1, source_target_pairs={{0,4},{1,5},{2,6},{3,7},{4,0},{5,1},{6,2},{7,3},{8,12},{9,13},{10,... | collective-permute-start | bytes 589832 | tf_op jit(solution)/shard_map/ppermute | solution.py:146
  29.7 2.5 %collective-permute-start.11 = (bf16[128,768]{1,0:T(8,128)(2,1)S(1)}, bf16[128,768]{1,0:T(8,128)(2,1)S(1)}, u32[]{:S(2)}, u32[]{:S(2)}) collective-permute-start(bf16[128,768]{1,0:T(8,128)(2,1)S(1)} %get-tuple-element.27), channel_id=1, source_target_pairs={{0,8},{1,9},{2,10},{3,11},{4,12},{5,13},{6,14},{7,15},{8,0},{9,1},... | collective-permute-start | bytes 589832 | tf_op jit(solution)/shard_map/ppermute | solution.py:146
  32.2 2.1 %collective-permute-start = (bf16[128,384]{1,0:T(8,128)(2,1)S(1)}, bf16[128,384]{1,0:T(8,128)(2,1)S(1)}, u32[]{:S(2)}, u32[]{:S(2)}) collective-permute-start(bf16[128,384]{1,0:T(8,128)(2,1)S(1)} %copy-done.3), channel_id=1, source_target_pairs={{0,1},{1,0},{2,3},{3,2},{4,5},{5,4},{6,7},{7,6},{8,9},{9,8},{10,11... | collective-permute-start | bytes 294920 | tf_op jit(solution)/shard_map/ppermute | solution.py:146
  35.1 12.1 %collective-permute-done.refs_1_.refs_6_ = bf16[128,384]{1,0:T(8,128)(2,1)S(1)} collective-permute-done((bf16[128,384]{1,0:T(8,128)(2,1)S(1)}, bf16[128,384]{1,0:T(8,128)(2,1)S(1)}, u32[]{:S(2)}, u32[]{:S(2)}) %collective-permute-start) | collective-permute-done | bytes 98336 | tf_op jit(solution)/shard_map/ppermute | solution.py:146
  49.5 2.5 %collective-permute-start.16 = (bf16[15,128,128]{2,1,0:T(8,128)(2,1)S(1)}, bf16[15,128,128]{2,1,0:T(8,128)(2,1)S(1)}, u32[]{:S(2)}, u32[]{:S(2)}) collective-permute-start(bf16[15,128,128]{2,1,0:T(8,128)(2,1)S(1)} %get-tuple-element.35), channel_id=1, source_target_pairs={{0,16},{16,0},{32,48},{48,32},{64,80},{80,64},{96,112},{112,96},{1... | collective-permute-start | bytes 1474568 | tf_op jit(solution)/shard_map/ppermute | solution.py:146
  52.0 3.6 %collective-permute-start.7 = (bf16[128,768]{1,0:T(8,128)(2,1)S(1)}, bf16[128,768]{1,0:T(8,128)(2,1)S(1)}, u32[]{:S(2)}, u32[]{:S(2)}) collective-permute-start(bf16[128,768]{1,0:T(8,128)(2,1)S(1)} %get-tuple-element.21.refs_0_), channel_id=1, source_target_pairs={{0,8},{1,9},{2,10},{3,11},{4,12},{5,13},{6,14},{7,15},{8,0},{9,1},... | collective-permute-start | bytes 589832 | tf_op jit(solution)/shard_map/ppermute | solution.py:146
  55.7 1.9 %collective-permute-start.6 = (bf16[128,768]{1,0:T(8,128)(2,1)S(1)}, bf16[128,768]{1,0:T(8,128)(2,1)S(1)}, u32[]{:S(2)}, u32[]{:S(2)}) collective-permute-start(bf16[128,768]{1,0:T(8,128)(2,1)S(1)} %get-tuple-element.21.refs_0_), channel_id=1, source_target_pairs={{0,4},{1,5},{2,6},{3,7},{4,0},{5,1},{6,2},{7,3},{8,12},{9,13},{10,... | collective-permute-start | bytes 589832 | tf_op jit(solution)/shard_map/ppermute | solution.py:146
  57.6 2.6 %collective-permute-start.5 = (bf16[128,768]{1,0:T(8,128)(2,1)S(1)}, bf16[128,768]{1,0:T(8,128)(2,1)S(1)}, u32[]{:S(2)}, u32[]{:S(2)}) collective-permute-start(bf16[128,768]{1,0:T(8,128)(2,1)S(1)} %get-tuple-element.21.refs_0_), channel_id=1, source_target_pairs={{0,2},{1,3},{2,0},{3,1},{4,6},{5,7},{6,4},{7,5},{8,10},{9,11},{10,... | collective-permute-start | bytes 589832 | tf_op jit(solution)/shard_map/ppermute | solution.py:146
  60.2 2.3 %collective-permute-start.4 = (bf16[128,768]{1,0:T(8,128)(2,1)S(1)}, bf16[128,768]{1,0:T(8,128)(2,1)S(1)}, u32[]{:S(2)}, u32[]{:S(2)}) collective-permute-start(bf16[128,768]{1,0:T(8,128)(2,1)S(1)} %get-tuple-element.21.refs_0_), channel_id=1, source_target_pairs={{0,1},{1,0},{2,3},{3,2},{4,5},{5,4},{6,7},{7,6},{8,9},{9,8},{10,11... | collective-permute-start | bytes 589832 | tf_op jit(solution)/shard_map/ppermute | solution.py:146
  63.4 12.3 %all-to-all-start = ((bf16[16,120,128]{2,1,0:T(8,128)(2,1)}), bf16[16,120,128]{2,1,0:T(8,128)(2,1)S(1)}, u32[]{:S(2)}, u32[]{:S(2)}) async-start(bf16[16,120,128]{2,1,0:T(8,128)(2,1)} %bitcast.3), calls=%async_computation | async-start | bytes 983040 | tf_op jit(solution)/shard_map/all_to_all | solution.py:196
  75.7 4.7 %collective-permute-done.4.refs_1_ = bf16[128,768]{1,0:T(8,128)(2,1)S(1)} collective-permute-done((bf16[128,768]{1,0:T(8,128)(2,1)S(1)}, bf16[128,768]{1,0:T(8,128)(2,1)S(1)}, u32[]{:S(2)}, u32[]{:S(2)}) %collective-permute-start.4) | collective-permute-done | bytes 196640 | tf_op jit(solution)/shard_map/ppermute | solution.py:146
  81.5 2.5 %collective-permute-start.18 = (bf16[15,128,128]{2,1,0:T(8,128)(2,1)S(1)}, bf16[15,128,128]{2,1,0:T(8,128)(2,1)S(1)}, u32[]{:S(2)}, u32[]{:S(2)}) collective-permute-start(bf16[15,128,128]{2,1,0:T(8,128)(2,1)S(1)} %get-tuple-element.37), channel_id=1, source_target_pairs={{0,16},{16,0},{32,48},{48,32},{64,80},{80,64},{96,112},{112,96},{1... | collective-permute-start | bytes 1474568 | tf_op jit(solution)/shard_map/ppermute | solution.py:146
  84.0 1.5 collective-permute-done.18
  86.3 3.0 %all-to-all-done = bf16[16,120,128]{2,1,0:T(8,128)(2,1)S(1)} async-done(((bf16[16,120,128]{2,1,0:T(8,128)(2,1)}), bf16[16,120,128]{2,1,0:T(8,128)(2,1)S(1)}, u32[]{:S(2)}, u32[]{:S(2)}) %all-to-all-start) | async-done | bytes 491552 | tf_op jit(solution)/shard_map/all_to_all | solution.py:196
  89.3 7.2 %all-to-all-start.2 = ((bf16[16,120,128]{2,1,0:T(8,128)(2,1)}), bf16[16,120,128]{2,1,0:T(8,128)(2,1)S(1)}, u32[]{:S(2)}, u32[]{:S(2)}) async-start(bf16[16,120,128]{2,1,0:T(8,128)(2,1)} %bitcast.15), calls=%async_computation.2 | async-start | bytes 983040 | tf_op jit(solution)/shard_map/all_to_all | solution.py:196
  97.5 10.9 %all-to-all-done.2 = bf16[16,120,128]{2,1,0:T(8,128)(2,1)S(1)} async-done(((bf16[16,120,128]{2,1,0:T(8,128)(2,1)}), bf16[16,120,128]{2,1,0:T(8,128)(2,1)S(1)}, u32[]{:S(2)}, u32[]{:S(2)}) %all-to-all-start.2) | async-done | bytes 491552 | tf_op jit(solution)/shard_map/all_to_all | solution.py:196
  108.4 8.1 %all-to-all-start.1 = ((bf16[16,120,128]{2,1,0:T(8,128)(2,1)}), bf16[16,120,128]{2,1,0:T(8,128)(2,1)S(1)}, u32[]{:S(2)}, u32[]{:S(2)}) async-start(bf16[16,120,128]{2,1,0:T(8,128)(2,1)} %broadcast_in_dim.4), calls=%async_computation.1 | async-start | bytes 983040 | tf_op jit(solution)/shard_map/all_to_all | solution.py:196
  117.4 10.8 %all-to-all-done.1 = bf16[16,120,128]{2,1,0:T(8,128)(2,1)S(1)} async-done(((bf16[16,120,128]{2,1,0:T(8,128)(2,1)}), bf16[16,120,128]{2,1,0:T(8,128)(2,1)S(1)}, u32[]{:S(2)}, u32[]{:S(2)}) %all-to-all-start.1) | async-done | bytes 491552 | tf_op jit(solution)/shard_map/all_to_all | solution.py:196
  129.0 8.2 %all-to-all-start.3 = ((bf16[16,120,128]{2,1,0:T(8,128)(2,1)}), bf16[16,120,128]{2,1,0:T(8,128)(2,1)}, u32[]{:S(2)}, u32[]{:S(2)}) async-start(bf16[16,120,128]{2,1,0:T(8,128)(2,1)} %broadcast_in_dim.5), calls=%async_computation.3 | async-start | bytes 983040 | tf_op jit(solution)/shard_map/all_to_all | solution.py:196
  137.2 2.9 %collective-permute-start.17 = (bf16[15,128,128]{2,1,0:T(8,128)(2,1)}, bf16[15,128,128]{2,1,0:T(8,128)(2,1)}, u32[]{:S(2)}, u32[]{:S(2)}) collective-permute-start(bf16[15,128,128]{2,1,0:T(8,128)(2,1)} %bitcast.13), channel_id=1, source_target_pairs={{0,16},{16,0},{32,48},{48,32},{64,80},{80,64},{96,112},{112,96},{1... | collective-permute-start | bytes 1474568 | tf_op jit(solution)/shard_map/ppermute | solution.py:146
  140.1 1.9 %shard_map.97 = (f32[128,384]{1,0:T(8,128)S(1)}, bf16[128,384]{1,0:T(8,128)(2,1)}, bf16[128,384]{1,0:T(8,128)(2,1)}, bf16[128,384]{1,0:T(8,128)(2,1)S(1)}, bf16[128,384]{1,0:T(8,128)(2,1)S(1)}) custom-call(s32[30]{0:T(128)S(1)} %reshape.51.pick, bf16[128,768]{1,0:T(8,128)(2,1)S(1)} %get-tuple-element.28.hg, bf16[30,128,128]{2,1,0:T(8,128)(2,1)S(1)} %bitcast.12), custom_call_target="tpu_custom_call" | custom-call | tf_op jit(solution)/shard_map/pallas_call | solution.py:42
  142.1 2.9 %collective-permute-start.12 = (bf16[128,384]{1,0:T(8,128)(2,1)}, bf16[128,384]{1,0:T(8,128)(2,1)S(1)}, u32[]{:S(2)}, u32[]{:S(2)}) collective-permute-start(bf16[128,384]{1,0:T(8,128)(2,1)} %get-tuple-element.30), channel_id=1, source_target_pairs={{0,1},{1,0},{2,3},{3,2},{4,5},{5,4},{6,7},{7,6},{8,9},{9,8},{10,11... | collective-permute-start | bytes 294920 | tf_op jit(solution)/shard_map/ppermute | solution.py:146
  145.0 5.3 %collective-permute-start.13 = (bf16[128,384]{1,0:T(8,128)(2,1)}, bf16[128,384]{1,0:T(8,128)(2,1)S(1)}, u32[]{:S(2)}, u32[]{:S(2)}) collective-permute-start(bf16[128,384]{1,0:T(8,128)(2,1)} %get-tuple-element.31), channel_id=1, source_target_pairs={{0,2},{1,3},{2,0},{3,1},{4,6},{5,7},{6,4},{7,5},{8,10},{9,11},{10,... | collective-permute-start | bytes 294920 | tf_op jit(solution)/shard_map/ppermute | solution.py:146
  150.4 3.2 %collective-permute-start.14 = (bf16[128,384]{1,0:T(8,128)(2,1)S(1)}, bf16[128,384]{1,0:T(8,128)(2,1)S(1)}, u32[]{:S(2)}, u32[]{:S(2)}) collective-permute-start(bf16[128,384]{1,0:T(8,128)(2,1)S(1)} %get-tuple-element.32), channel_id=1, source_target_pairs={{0,4},{1,5},{2,6},{3,7},{4,0},{5,1},{6,2},{7,3},{8,12},{9,13},{10,... | collective-permute-start | bytes 294920 | tf_op jit(solution)/shard_map/ppermute | solution.py:146
  153.5 2.6 %collective-permute-start.15 = (bf16[128,384]{1,0:T(8,128)(2,1)S(1)}, bf16[128,384]{1,0:T(8,128)(2,1)S(1)}, u32[]{:S(2)}, u32[]{:S(2)}) collective-permute-start(bf16[128,384]{1,0:T(8,128)(2,1)S(1)} %get-tuple-element.33), channel_id=1, source_target_pairs={{0,8},{1,9},{2,10},{3,11},{4,12},{5,13},{6,14},{7,15},{8,0},{9,1},... | collective-permute-start | bytes 294920 | tf_op jit(solution)/shard_map/ppermute | solution.py:146
  156.1 3.1 %collective-permute-start.19 = (bf16[15,128,128]{2,1,0:T(8,128)(2,1)}, bf16[15,128,128]{2,1,0:T(8,128)(2,1)S(1)}, u32[]{:S(2)}, u32[]{:S(2)}) collective-permute-start(bf16[15,128,128]{2,1,0:T(8,128)(2,1)} %bitcast.7), channel_id=1, source_target_pairs={{0,16},{16,0},{32,48},{48,32},{64,80},{80,64},{96,112},{112,96},{1... | collective-permute-start | bytes 1474568 | tf_op jit(solution)/shard_map/ppermute | solution.py:146
  (58 shorter events, 19.4 us)
Async XLA Ops:
  0.6 25.9 %collective-permute-start.3 = (bf16[128,384]{1,0:T(8,128)(2,1)}, bf16[128,384]{1,0:T(8,128)(2,1)S(1)}, u32[]{:S(2)}, u32[]{:S(2)}) collective-permute-start(bf16[128,384]{1,0:T(8,128)(2,1)} %refs_5_.1), channel_id=1, source_target_pairs={{0,8},{1,9},{2,10},{3,11},{4,12},{5,13},{6,14},{7,15},{8,0},{9,1},... | collective-permute-start | bytes 294920 | tf_op jit(solution)/shard_map/ppermute | solution.py:146
  6.1 23.5 %collective-permute-start.2 = (bf16[128,384]{1,0:T(8,128)(2,1)}, bf16[128,384]{1,0:T(8,128)(2,1)S(1)}, u32[]{:S(2)}, u32[]{:S(2)}) collective-permute-start(bf16[128,384]{1,0:T(8,128)(2,1)} %refs_5_.1), channel_id=1, source_target_pairs={{0,4},{1,5},{2,6},{3,7},{4,0},{5,1},{6,2},{7,3},{8,12},{9,13},{10,... | collective-permute-start | bytes 294920 | tf_op jit(solution)/shard_map/ppermute | solution.py:146
  8.3 23.8 %collective-permute-start.1 = (bf16[128,384]{1,0:T(8,128)(2,1)}, bf16[128,384]{1,0:T(8,128)(2,1)S(1)}, u32[]{:S(2)}, u32[]{:S(2)}) collective-permute-start(bf16[128,384]{1,0:T(8,128)(2,1)} %refs_5_.1), channel_id=1, source_target_pairs={{0,2},{1,3},{2,0},{3,1},{4,6},{5,7},{6,4},{7,5},{8,10},{9,11},{10,... | collective-permute-start | bytes 294920 | tf_op jit(solution)/shard_map/ppermute | solution.py:146
  16.7 1.2 copy-start
  17.9 0.9 copy-start.4
  18.8 13.4 %copy-start.3 = (bf16[128,384]{1,0:T(8,128)(2,1)S(1)}, bf16[128,384]{1,0:T(8,128)(2,1)}, u32[]{:S(2)}) copy-start(bf16[128,384]{1,0:T(8,128)(2,1)} %refs_5_.1) | copy-start | bytes 294916
  18.8 28.4 %copy-start.2 = (bf16[1,5,6,128,128]{4,3,2,1,0:T(8,128)(2,1)S(1)}, bf16[1,5,6,128,128]{4,3,2,1,0:T(8,128)(2,1)}, u32[]{:S(2)}) copy-start(bf16[1,5,6,128,128]{4,3,2,1,0:T(8,128)(2,1)} %param.7) | copy-start | bytes 2949124
  20.6 27.7 %collective-permute-start.8 = (bf16[128,768]{1,0:T(8,128)(2,1)}, bf16[128,768]{1,0:T(8,128)(2,1)S(1)}, u32[]{:S(2)}, u32[]{:S(2)}) collective-permute-start(bf16[128,768]{1,0:T(8,128)(2,1)} %get-tuple-element.24), channel_id=1, source_target_pairs={{0,1},{1,0},{2,3},{3,2},{4,5},{5,4},{6,7},{7,6},{8,9},{9,8},{10,11... | collective-permute-start | bytes 589832 | tf_op jit(solution)/shard_map/ppermute | solution.py:146
  23.0 25.3 %collective-permute-start.9 = (bf16[128,768]{1,0:T(8,128)(2,1)S(1)}, bf16[128,768]{1,0:T(8,128)(2,1)S(1)}, u32[]{:S(2)}, u32[]{:S(2)}) collective-permute-start(bf16[128,768]{1,0:T(8,128)(2,1)S(1)} %get-tuple-element.25), channel_id=1, source_target_pairs={{0,2},{1,3},{2,0},{3,1},{4,6},{5,7},{6,4},{7,5},{8,10},{9,11},{10,... | collective-permute-start | bytes 589832 | tf_op jit(solution)/shard_map/ppermute | solution.py:146
  26.6 21.7 %collective-permute-start.10 = (bf16[128,768]{1,0:T(8,128)(2,1)S(1)}, bf16[128,768]{1,0:T(8,128)(2,1)S(1)}, u32[]{:S(2)}, u32[]{:S(2)}) collective-permute-start(bf16[128,768]{1,0:T(8,128)(2,1)S(1)} %get-tuple-element.26), channel_id=1, source_target_pairs={{0,4},{1,5},{2,6},{3,7},{4,0},{5,1},{6,2},{7,3},{8,12},{9,13},{10,... | collective-permute-start | bytes 589832 | tf_op jit(solution)/shard_map/ppermute | solution.py:146
  29.7 18.6 %collective-permute-start.11 = (bf16[128,768]{1,0:T(8,128)(2,1)S(1)}, bf16[128,768]{1,0:T(8,128)(2,1)S(1)}, u32[]{:S(2)}, u32[]{:S(2)}) collective-permute-start(bf16[128,768]{1,0:T(8,128)(2,1)S(1)} %get-tuple-element.27), channel_id=1, source_target_pairs={{0,8},{1,9},{2,10},{3,11},{4,12},{5,13},{6,14},{7,15},{8,0},{9,1},... | collective-permute-start | bytes 589832 | tf_op jit(solution)/shard_map/ppermute | solution.py:146
  32.2 15.0 %collective-permute-start = (bf16[128,384]{1,0:T(8,128)(2,1)S(1)}, bf16[128,384]{1,0:T(8,128)(2,1)S(1)}, u32[]{:S(2)}, u32[]{:S(2)}) collective-permute-start(bf16[128,384]{1,0:T(8,128)(2,1)S(1)} %copy-done.3), channel_id=1, source_target_pairs={{0,1},{1,0},{2,3},{3,2},{4,5},{5,4},{6,7},{7,6},{8,9},{9,8},{10,11... | collective-permute-start | bytes 294920 | tf_op jit(solution)/shard_map/ppermute | solution.py:146
  49.5 13.0 %collective-permute-start.16 = (bf16[15,128,128]{2,1,0:T(8,128)(2,1)S(1)}, bf16[15,128,128]{2,1,0:T(8,128)(2,1)S(1)}, u32[]{:S(2)}, u32[]{:S(2)}) collective-permute-start(bf16[15,128,128]{2,1,0:T(8,128)(2,1)S(1)} %get-tuple-element.35), channel_id=1, source_target_pairs={{0,16},{16,0},{32,48},{48,32},{64,80},{80,64},{96,112},{112,96},{1... | collective-permute-start | bytes 1474568 | tf_op jit(solution)/shard_map/ppermute | solution.py:146
  52.0 23.7 %collective-permute-start.7 = (bf16[128,768]{1,0:T(8,128)(2,1)S(1)}, bf16[128,768]{1,0:T(8,128)(2,1)S(1)}, u32[]{:S(2)}, u32[]{:S(2)}) collective-permute-start(bf16[128,768]{1,0:T(8,128)(2,1)S(1)} %get-tuple-element.21.refs_0_), channel_id=1, source_target_pairs={{0,8},{1,9},{2,10},{3,11},{4,12},{5,13},{6,14},{7,15},{8,0},{9,1},... | collective-permute-start | bytes 589832 | tf_op jit(solution)/shard_map/ppermute | solution.py:146
  55.7 20.0 %collective-permute-start.6 = (bf16[128,768]{1,0:T(8,128)(2,1)S(1)}, bf16[128,768]{1,0:T(8,128)(2,1)S(1)}, u32[]{:S(2)}, u32[]{:S(2)}) collective-permute-start(bf16[128,768]{1,0:T(8,128)(2,1)S(1)} %get-tuple-element.21.refs_0_), channel_id=1, source_target_pairs={{0,4},{1,5},{2,6},{3,7},{4,0},{5,1},{6,2},{7,3},{8,12},{9,13},{10,... | collective-permute-start | bytes 589832 | tf_op jit(solution)/shard_map/ppermute | solution.py:146
  57.6 18.1 %collective-permute-start.5 = (bf16[128,768]{1,0:T(8,128)(2,1)S(1)}, bf16[128,768]{1,0:T(8,128)(2,1)S(1)}, u32[]{:S(2)}, u32[]{:S(2)}) collective-permute-start(bf16[128,768]{1,0:T(8,128)(2,1)S(1)} %get-tuple-element.21.refs_0_), channel_id=1, source_target_pairs={{0,2},{1,3},{2,0},{3,1},{4,6},{5,7},{6,4},{7,5},{8,10},{9,11},{10,... | collective-permute-start | bytes 589832 | tf_op jit(solution)/shard_map/ppermute | solution.py:146
  60.2 20.2 %collective-permute-start.4 = (bf16[128,768]{1,0:T(8,128)(2,1)S(1)}, bf16[128,768]{1,0:T(8,128)(2,1)S(1)}, u32[]{:S(2)}, u32[]{:S(2)}) collective-permute-start(bf16[128,768]{1,0:T(8,128)(2,1)S(1)} %get-tuple-element.21.refs_0_), channel_id=1, source_target_pairs={{0,1},{1,0},{2,3},{3,2},{4,5},{5,4},{6,7},{7,6},{8,9},{9,8},{10,11... | collective-permute-start | bytes 589832 | tf_op jit(solution)/shard_map/ppermute | solution.py:146
  63.4 17.0 %copy-start.5 = (bf16[128,384]{1,0:T(8,128)(2,1)S(1)}, bf16[128,384]{1,0:T(8,128)(2,1)}, u32[]{:S(2)}) copy-start(bf16[128,384]{1,0:T(8,128)(2,1)} %cot.3) | copy-start | bytes 294916
  63.4 25.9 %all-to-all-start = ((bf16[16,120,128]{2,1,0:T(8,128)(2,1)}), bf16[16,120,128]{2,1,0:T(8,128)(2,1)S(1)}, u32[]{:S(2)}, u32[]{:S(2)}) async-start(bf16[16,120,128]{2,1,0:T(8,128)(2,1)} %bitcast.3), calls=%async_computation | async-start | bytes 983040 | tf_op jit(solution)/shard_map/all_to_all | solution.py:196
  81.5 3.9 %collective-permute-start.18 = (bf16[15,128,128]{2,1,0:T(8,128)(2,1)S(1)}, bf16[15,128,128]{2,1,0:T(8,128)(2,1)S(1)}, u32[]{:S(2)}, u32[]{:S(2)}) collective-permute-start(bf16[15,128,128]{2,1,0:T(8,128)(2,1)S(1)} %get-tuple-element.37), channel_id=1, source_target_pairs={{0,16},{16,0},{32,48},{48,32},{64,80},{80,64},{96,112},{112,96},{1... | collective-permute-start | bytes 1474568 | tf_op jit(solution)/shard_map/ppermute | solution.py:146
  89.3 19.0 %all-to-all-start.2 = ((bf16[16,120,128]{2,1,0:T(8,128)(2,1)}), bf16[16,120,128]{2,1,0:T(8,128)(2,1)S(1)}, u32[]{:S(2)}, u32[]{:S(2)}) async-start(bf16[16,120,128]{2,1,0:T(8,128)(2,1)} %bitcast.15), calls=%async_computation.2 | async-start | bytes 983040 | tf_op jit(solution)/shard_map/all_to_all | solution.py:196
  108.4 19.8 %all-to-all-start.1 = ((bf16[16,120,128]{2,1,0:T(8,128)(2,1)}), bf16[16,120,128]{2,1,0:T(8,128)(2,1)S(1)}, u32[]{:S(2)}, u32[]{:S(2)}) async-start(bf16[16,120,128]{2,1,0:T(8,128)(2,1)} %broadcast_in_dim.4), calls=%async_computation.1 | async-start | bytes 983040 | tf_op jit(solution)/shard_map/all_to_all | solution.py:196
  128.2 0.8 copy-start.6
  129.0 27.1 %all-to-all-start.3 = ((bf16[16,120,128]{2,1,0:T(8,128)(2,1)}), bf16[16,120,128]{2,1,0:T(8,128)(2,1)}, u32[]{:S(2)}, u32[]{:S(2)}) async-start(bf16[16,120,128]{2,1,0:T(8,128)(2,1)} %broadcast_in_dim.5), calls=%async_computation.3 | async-start | bytes 983040 | tf_op jit(solution)/shard_map/all_to_all | solution.py:196
  137.2 23.9 %copy-start.1 = (bf16[1,5,3,2,128,128]{5,4,3,2,1,0:T(8,128)(2,1)S(1)}, bf16[1,5,3,2,128,128]{5,4,3,2,1,0:T(8,128)(2,1)}, u32[]{:S(2)}) copy-start(bf16[1,5,3,2,128,128]{5,4,3,2,1,0:T(8,128)(2,1)} %param.9) | copy-start | bytes 2949124
  137.2 25.5 %collective-permute-start.17 = (bf16[15,128,128]{2,1,0:T(8,128)(2,1)}, bf16[15,128,128]{2,1,0:T(8,128)(2,1)}, u32[]{:S(2)}, u32[]{:S(2)}) collective-permute-start(bf16[15,128,128]{2,1,0:T(8,128)(2,1)} %bitcast.13), channel_id=1, source_target_pairs={{0,16},{16,0},{32,48},{48,32},{64,80},{80,64},{96,112},{112,96},{1... | collective-permute-start | bytes 1474568 | tf_op jit(solution)/shard_map/ppermute | solution.py:146
  142.1 14.0 %collective-permute-start.12 = (bf16[128,384]{1,0:T(8,128)(2,1)}, bf16[128,384]{1,0:T(8,128)(2,1)S(1)}, u32[]{:S(2)}, u32[]{:S(2)}) collective-permute-start(bf16[128,384]{1,0:T(8,128)(2,1)} %get-tuple-element.30), channel_id=1, source_target_pairs={{0,1},{1,0},{2,3},{3,2},{4,5},{5,4},{6,7},{7,6},{8,9},{9,8},{10,11... | collective-permute-start | bytes 294920 | tf_op jit(solution)/shard_map/ppermute | solution.py:146
  145.0 14.2 %collective-permute-start.13 = (bf16[128,384]{1,0:T(8,128)(2,1)}, bf16[128,384]{1,0:T(8,128)(2,1)S(1)}, u32[]{:S(2)}, u32[]{:S(2)}) collective-permute-start(bf16[128,384]{1,0:T(8,128)(2,1)} %get-tuple-element.31), channel_id=1, source_target_pairs={{0,2},{1,3},{2,0},{3,1},{4,6},{5,7},{6,4},{7,5},{8,10},{9,11},{10,... | collective-permute-start | bytes 294920 | tf_op jit(solution)/shard_map/ppermute | solution.py:146
  150.4 8.8 %collective-permute-start.14 = (bf16[128,384]{1,0:T(8,128)(2,1)S(1)}, bf16[128,384]{1,0:T(8,128)(2,1)S(1)}, u32[]{:S(2)}, u32[]{:S(2)}) collective-permute-start(bf16[128,384]{1,0:T(8,128)(2,1)S(1)} %get-tuple-element.32), channel_id=1, source_target_pairs={{0,4},{1,5},{2,6},{3,7},{4,0},{5,1},{6,2},{7,3},{8,12},{9,13},{10,... | collective-permute-start | bytes 294920 | tf_op jit(solution)/shard_map/ppermute | solution.py:146
  153.5 6.9 %collective-permute-start.15 = (bf16[128,384]{1,0:T(8,128)(2,1)S(1)}, bf16[128,384]{1,0:T(8,128)(2,1)S(1)}, u32[]{:S(2)}, u32[]{:S(2)}) collective-permute-start(bf16[128,384]{1,0:T(8,128)(2,1)S(1)} %get-tuple-element.33), channel_id=1, source_target_pairs={{0,8},{1,9},{2,10},{3,11},{4,12},{5,13},{6,14},{7,15},{8,0},{9,1},... | collective-permute-start | bytes 294920 | tf_op jit(solution)/shard_map/ppermute | solution.py:146
  156.1 8.7 %collective-permute-start.19 = (bf16[15,128,128]{2,1,0:T(8,128)(2,1)}, bf16[15,128,128]{2,1,0:T(8,128)(2,1)S(1)}, u32[]{:S(2)}, u32[]{:S(2)}) collective-permute-start(bf16[15,128,128]{2,1,0:T(8,128)(2,1)} %bitcast.7), channel_id=1, source_target_pairs={{0,16},{16,0},{32,48},{48,32},{64,80},{80,64},{96,112},{112,96},{1... | collective-permute-start | bytes 1474568 | tf_op jit(solution)/shard_map/ppermute | solution.py:146
  161.1 1.6 copy-start.7
  (1 other events, 0.7 us)

commit v2 on v1

v2 whole, which is shorter than its diff:
```python
import functools
import math

import jax
import jax.numpy as jnp
from jax import lax
from jax.experimental import pallas as pl
from jax.experimental.pallas import tpu as pltpu
from jax.sharding import PartitionSpec as P


F32 = jnp.float32
BF16 = jnp.bfloat16
B = 128
GELU_C = math.sqrt(2.0 / math.pi)
GELU_A = 0.044715


VMEM = pl.BlockSpec(memory_space=pltpu.VMEM)
SMEM = pl.BlockSpec(memory_space=pltpu.SMEM)


def sds(shape, dtype):
    return pltpu.VMEM(shape, dtype)


def hbm(shape, dtype):
    return jax.ShapeDtypeStruct(shape, dtype)


def call(kernel, outs, in_specs, scratch=()):
    run = pl.pallas_call(
        kernel,
        out_shape=outs,
        in_specs=in_specs,
        out_specs=jax.tree.map(lambda _: VMEM, outs),
        scratch_shapes=list(scratch),
        compiler_params=pltpu.CompilerParams(vmem_limit_bytes=16 << 20),
    )

    def invoke(*args):
        placed = [
            a if spec is SMEM else pltpu.with_memory_space_constraint(a, pltpu.VMEM)
            for a, spec in zip(args, in_specs)
        ]
        return run(*placed)

    return invoke


def lanes(index):
    return pl.ds(pl.multiple_of(index * B, B), B)


def dot_nt(a, b):
    return lax.dot_general(a, b, (((1,), (1,)), ((), ())), preferred_element_type=F32)


def dot_tn(a, b):
    return lax.dot_general(a, b, (((0,), (0,)), ((), ())), preferred_element_type=F32)


def back_kernel(levels, db, hb, kd, pick, cot, w, x, *refs):
    own, sends, acc = refs[0], refs[1:levels], refs[levels]
    wide = db * B
    for send in sends:
        send[:, :wide] = x[...]
    for lvl in range(levels):
        acc[...] = jnp.zeros_like(acc)
        for o in range(db):
            both = jnp.concatenate([w[(lvl * db + o) * kd + k] for k in range(kd)], axis=0)
            term = dot_nt(cot[:, o * B : (o + 1) * B], both)
            for k in range(kd):
                spot = pick[(lvl * db + o) * kd + k]
                acc[spot] += term[:, k * B : (k + 1) * B]
        for h in range(hb):
            if lvl == 0:
                own[:, h * B : (h + 1) * B] = acc[h]
            else:
                sends[lvl - 1][:, wide + h * B : wide + (h + 1) * B] = acc[h].astype(BF16)


def mid_kernel(levels, db, hb, pick, w, x, own, *refs):
    got = refs[: levels - 1]
    in0, hg, sends, acc = refs[levels - 1], refs[levels], refs[levels + 1 : -1], refs[-1]
    xs = (x,) + got
    wide = db * B
    for o in range(hb):
        here = slice(o * B, (o + 1) * B)
        lhs = jnp.concatenate(
            [xs[lvl][:, lanes(pick[lvl * hb + o])] for lvl in range(levels)], axis=1
        )
        rhs = jnp.concatenate([w[lvl * hb + o] for lvl in range(levels)], axis=0)
        v = jnp.dot(lhs, rhs, preferred_element_type=F32)
        sq = v * v
        t = jnp.tanh(GELU_C * (v + GELU_A * (v * sq)))
        half = 0.5 * (1.0 + t)
        act = (v * half).astype(BF16)
        for send in sends:
            send[:, here] = act
        inner = GELU_C * (1.0 + (3.0 * GELU_A) * sq)
        slope = half + 0.5 * v * (1.0 - t * t) * inner
        grad = own[:, here]
        for ref in got:
            grad = grad + ref[:, wide + o * B : wide + (o + 1) * B].astype(F32)
        hg[:, here] = (grad * slope).astype(BF16)
    base = hb * B
    for lvl in range(levels):
        acc[...] = jnp.zeros_like(acc)
        for o in range(hb):
            spot = pick[lvl * hb + o]
            acc[spot] += dot_nt(hg[:, o * B : (o + 1) * B], w[lvl * hb + o])
        for d in range(db):
            if lvl == 0:
                in0[:, d * B : (d + 1) * B] = acc[d]
            else:
                sends[lvl - 1][:, base + d * B : base + (d + 1) * B] = acc[d].astype(BF16)


def split(core, scr, keep, send):
    half = keep.shape[0]
    keep[...] = scr[pl.ds(core * half, half)]
    send[...] = scr[pl.ds((1 - core) * half, half)].astype(BF16)


def up_kernel(levels, hb, pick, core, hg, *refs):
    xs = refs[:levels]
    keep, send, scr = refs[levels:]
    for o in range(hb):
        right = hg[:, o * B : (o + 1) * B]
        for lvl in range(levels):
            left = xs[lvl][:, lanes(pick[lvl * hb + o])]
            scr[lvl * hb + o] = dot_tn(left, right)
    split(core[0], scr, keep, send)


def down_kernel(levels, db, kd, pick, core, cot, *refs):
    acts = refs[:levels]
    keep, send, scr = refs[levels:]
    for o in range(db):
        right = cot[:, o * B : (o + 1) * B]
        for lvl in range(levels):
            for k in range(kd):
                i = (lvl * db + o) * kd + k
                scr[i] = dot_tn(acts[lvl][:, lanes(pick[i])], right)
    split(core[0], scr, keep, send)


def out_kernel(levels, db, hb, kd, pick, w, in0, *refs):
    acts, out, dx = refs[:levels], refs[levels], refs[levels + 1]
    total = in0[...]
    for ref in acts[1:]:
        total = total + ref[:, hb * B :].astype(F32)
    dx[...] = total.astype(BF16)
    for o in range(db):
        spots = [(lvl * db + o) * kd + k for lvl in range(levels) for k in range(kd)]
        lhs = jnp.concatenate(
            [acts[i // (db * kd)][:, lanes(pick[i])] for i in spots], axis=1
        )
        rhs = jnp.concatenate([w[i] for i in spots], axis=0)
        out[:, o * B : (o + 1) * B] = jnp.dot(lhs, rhs, preferred_element_type=F32).astype(BF16)


def shard_kernel(scale, *refs):
    out = refs[-1]
    at = 0
    for ref in refs[:-1]:
        total = ref[0].astype(F32)
        for i in range(1, ref.shape[0]):
            total = total + ref[i].astype(F32)
        total = (total * scale).astype(BF16)
        rows = ref.shape[1]
        for i in range(out.shape[0]):
            out[i, at : at + rows, :] = total
        at += rows


def join_kernel(core, mine, other, *outs):
    at = 0
    for out in outs:
        rows = out.shape[2]
        out[core[0]] = mine[:, at : at + rows, :]
        out[1 - core[0]] = other[:, at : at + rows, :]
        at += rows


def from_partner(block, axis, bit):
    count = lax.axis_size(axis)
    return lax.ppermute(block, axis, [(i, i ^ (1 << bit)) for i in range(count)])


def step(inputs, up_weight, up_pick, down_weight, down_pick, cotangent):
    bits = lax.axis_size("mp").bit_length() - 1
    levels = bits + 1
    tokens = inputs.shape[0]
    db, kd = down_weight.shape[2], down_weight.shape[3]
    hb = up_weight.shape[2]
    dp = lax.axis_size("dp")
    chips = dp // 2
    scale = 1.0 / math.sqrt(tokens * dp)
    n_up, n_down = levels * hb, levels * db * kd
    up_w = up_weight.reshape(n_up, B, B)
    down_w = down_weight.reshape(n_down, B, B)
    up_ids = up_pick.reshape(n_up)
    down_ids = down_pick.reshape(n_down)
    core = lax.rem(lax.axis_index("dp"), 2).reshape(1)
    groups = [[2 * i + c for i in range(chips)] for c in range(2)]

    def over_mp(blocks):
        return [from_partner(blocks[b], "mp", b) for b in reversed(range(bits))][::-1]

    def exchange(block):
        return lax.all_to_all(
            block, "dp", split_axis=0, concat_axis=0, axis_index_groups=groups, tiled=True
        )

    def partials(keep, send):
        got = from_partner(send, "dp", 0)
        pair = (keep + got.astype(F32)).astype(BF16)
        return exchange(pair.reshape(chips, -1, B))

    wide, deep = db * B, hb * B
    own, *first = call(
        functools.partial(back_kernel, levels, db, hb, kd),
        [sds((tokens, deep), F32)] + [sds((tokens, wide + deep), BF16)] * bits,
        [SMEM, VMEM, VMEM, VMEM],
        [pltpu.VMEM((hb, tokens, B), F32)],
    )(down_ids, cotangent, down_w, inputs)
    got = over_mp(first)

    in0, hg, *second = call(
        functools.partial(mid_kernel, levels, db, hb),
        [sds((tokens, wide), F32), sds((tokens, deep), BF16)]
        + [sds((tokens, deep + wide), BF16)] * bits,
        [SMEM] + [VMEM] * (levels + 2),
        [pltpu.VMEM((db, tokens, B), F32)],
    )(up_ids, up_w, inputs, own, *got)
    acts = [second[0]] + over_mp(second)

    def grad_outs(count):
        return [sds((count // 2, B, B), F32), sds((count // 2, B, B), BF16)]

    up_keep, up_send = call(
        functools.partial(up_kernel, levels, hb),
        grad_outs(n_up),
        [SMEM, SMEM, VMEM] + [VMEM] * levels,
        [pltpu.VMEM((n_up, B, B), F32)],
    )(up_ids, core, hg, inputs, *got)
    up_parts = partials(up_keep, up_send)

    down_keep, down_send = call(
        functools.partial(down_kernel, levels, db, kd),
        grad_outs(n_down),
        [SMEM, SMEM, VMEM] + [VMEM] * levels,
        [pltpu.VMEM((n_down, B, B), F32)],
    )(down_ids, core, cotangent, *acts)
    down_parts = partials(down_keep, down_send)

    output, grad_inputs = call(
        functools.partial(out_kernel, levels, db, hb, kd),
        [hbm((tokens, wide), BF16)] * 2,
        [SMEM, VMEM, VMEM] + [VMEM] * levels,
        (),
    )(down_ids, down_w, in0, *acts)

    rows = [up_parts.shape[1], down_parts.shape[1]]
    shard = call(
        functools.partial(shard_kernel, scale), sds((chips, sum(rows), B), BF16), [VMEM, VMEM], ()
    )(up_parts, down_parts)
    mine = exchange(shard)
    other = from_partner(mine, "dp", 0)
    up_out, down_out = call(
        join_kernel, [hbm((2, chips, r, B), BF16) for r in rows], [SMEM, VMEM, VMEM], ()
    )(core, mine, other)
    return (
        output,
        grad_inputs,
        up_out.reshape(up_weight.shape),
        down_out.reshape(down_weight.shape),
    )


def solution(mesh):
    placed = (
        P("dp", "mp"),
        P("mp", None, None, None, None),
        P("mp", None, None),
        P("mp", None, None, None, None, None),
        P("mp", None, None, None),
        P("dp", "mp"),
    )
    return jax.shard_map(
        step,
        mesh=mesh,
        in_specs=placed,
        out_specs=(
            P("dp", "mp"),
            P("dp", "mp"),
            P("mp", None, None, None, None),
            P("mp", None, None, None, None, None),
        ),
        check_vma=False,
    )
```

time: 169 us -> 145 us (0.86)
  blocking collectives: 0 us -> 45.9 us
  starting transfers between devices: 100 us -> 57.4 us
  waiting for transfers between devices: 44.1 us -> 24.3 us
  other arithmetic: 6.95 us -> 1.07 us
  local copies, waits for them, and re-layouts: 6.85 us -> 4.64 us
  Pallas kernels: 8.08 us -> 10.1 us
    all_to_all x0 -> x2, blocking collectives: none -> 45.9 us  [exchange(): lax.all_to_all(block, 'dp', split_axis=0, concat_axis=0, axis_index_group...]
    all_to_all x4 -> x1, starting transfers between devices: 35.8 us -> 10.9 us  [exchange(): lax.all_to_all(block, 'dp', split_axis=0, concat_axis=0, axis_index_group...]
    ppermute x20 -> x11, starting transfers between devices: 64.2 us -> 46.5 us  [from_partner(): return lax.ppermute(block, axis, [(i, i ^ 1 << bit) for i in range(count)])]
    all_to_all x4 -> x1, waiting for transfers between devices: 24.7 us -> 9.07 us  [exchange(): lax.all_to_all(block, 'dp', split_axis=0, concat_axis=0, axis_index_group...]
    ppermute x20 -> x11, waiting for transfers between devices: 19.4 us -> 15.2 us  [from_partner(): return lax.ppermute(block, axis, [(i, i ^ 1 << bit) for i in range(count)])]
    select_n x2 -> x0, other arithmetic: 2.2 us -> none  [gather(): jnp.where(first, mine, other)]
    concatenate x2 -> x0, other arithmetic: 2.06 us -> none  [gather(): jnp.concatenate([jnp.where(first, mine, other), jnp.where(first, other, m...]
    pallas_call x6 -> x7, Pallas kernels: 8.08 us -> 10.1 us  [invoke(): return run(*placed)]
  transfers between devices with their start and end apart: 24 -> 12, of which waited for: 7 -> 5; matrix products, arithmetic and copies ran while one was open for 5% -> 1% of each run, Pallas kernels for 4% -> 2%
where the time goes in v2:
time: 145 us; the launch traced here: 144 us
  starting transfers between devices  57.4 us (40%)
  blocking collectives  45.9 us (32%)
  waiting for transfers between devices  24.3 us (17%)
  Pallas kernels  10.1 us (7%)
  local copies, waits for them, and re-layouts  4.64 us (3%)
    ppermute x11, starting transfers between devices, from_partner(): return lax.ppermute(block, axis, [(i, i ^ 1 << bit) for i in range(count)])  46.5 us
    all_to_all x2, blocking collectives, exchange(): lax.all_to_all(block, 'dp', split_axis=0, concat_axis=0, axis_index_group...  45.9 us
    ppermute x11, waiting for transfers between devices, from_partner(): return lax.ppermute(block, axis, [(i, i ^ 1 << bit) for i in range(count)])  15.2 us
    all_to_all x1, starting transfers between devices, exchange(): lax.all_to_all(block, 'dp', split_axis=0, concat_axis=0, axis_index_group...  10.9 us
    pallas_call x7, Pallas kernels, invoke(): return run(*placed)  10.1 us
    all_to_all x1, waiting for transfers between devices, exchange(): lax.all_to_all(block, 'dp', split_axis=0, concat_axis=0, axis_index_group...  9.07 us
    unnamed x17, local copies, waits for them, and re-layouts  4.47 us
  transfers between devices with their start and end apart: 12, of which 5 were waited for; matrix products, arithmetic and copies ran while one was open for 1% of the time, Pallas kernels for 2%

profile of v2, /device:TPU:1, one launch (start us, length us, event | category | flops | bytes accessed | tf_op | source)
XLA Modules:
  0.0 144.3 jit_solution(3376363829185484889)
XLA Ops:
  0.6 0.8 copy.11
  1.5 1.2 copy-done
  2.7 0.9 copy-done.3
  3.6 0.9 copy-done.5
  4.5 2.0 %shard_map.93 = (f32[128,768]{1,0:T(8,128)S(1)}, bf16[128,1152]{1,0:T(8,128)(2,1)}, bf16[128,1152]{1,0:T(8,128)(2,1)}, bf16[128,1152]{1,0:T(8,128)(2,1)S(1)}, bf16[128,1152]{1,0:T(8,128)(2,1)S(1)}) custom-call(s32[30]{0:T(128)S(1)} %reshape.35.pick, bf16[128,384]{1,0:T(8,128)(2,1)S(1)} %copy-done.5, bf16[30,128,128]{2,1,0:T(8,128)(2,1)S(1)} %bitcast.7, ...), custom_call_target="tpu_custom_call" | custom-call | tf_op jit(solution)/shard_map/pallas_call | solution.py:46
  6.5 5.0 %collective-permute-start = (bf16[128,1152]{1,0:T(8,128)(2,1)}, bf16[128,1152]{1,0:T(8,128)(2,1)S(1)}, u32[]{:S(2)}, u32[]{:S(2)}) collective-permute-start(bf16[128,1152]{1,0:T(8,128)(2,1)} %get-tuple-element.24), channel_id=1, source_target_pairs={{0,1},{1,0},{2,3},{3,2},{4,5},{5,4},{6,7},{7,6},{8,9},{9,8},{10,11... | collective-permute-start | bytes 884744 | tf_op jit(solution)/shard_map/ppermute | solution.py:189
  11.6 5.6 %collective-permute-start.1 = (bf16[128,1152]{1,0:T(8,128)(2,1)}, bf16[128,1152]{1,0:T(8,128)(2,1)S(1)}, u32[]{:S(2)}, u32[]{:S(2)}) collective-permute-start(bf16[128,1152]{1,0:T(8,128)(2,1)} %get-tuple-element.25), channel_id=1, source_target_pairs={{0,2},{1,3},{2,0},{3,1},{4,6},{5,7},{6,4},{7,5},{8,10},{9,11},{10,... | collective-permute-start | bytes 884744 | tf_op jit(solution)/shard_map/ppermute | solution.py:189
  17.2 3.1 %collective-permute-start.2 = (bf16[128,1152]{1,0:T(8,128)(2,1)S(1)}, bf16[128,1152]{1,0:T(8,128)(2,1)S(1)}, u32[]{:S(2)}, u32[]{:S(2)}) collective-permute-start(bf16[128,1152]{1,0:T(8,128)(2,1)S(1)} %get-tuple-element.26), channel_id=1, source_target_pairs={{0,4},{1,5},{2,6},{3,7},{4,0},{5,1},{6,2},{7,3},{8,12},{9,13},{10,... | collective-permute-start | bytes 884744 | tf_op jit(solution)/shard_map/ppermute | solution.py:189
  20.4 4.4 %collective-permute-start.3 = (bf16[128,1152]{1,0:T(8,128)(2,1)S(1)}, bf16[128,1152]{1,0:T(8,128)(2,1)S(1)}, u32[]{:S(2)}, u32[]{:S(2)}) collective-permute-start(bf16[128,1152]{1,0:T(8,128)(2,1)S(1)} %get-tuple-element.27), channel_id=1, source_target_pairs={{0,8},{1,9},{2,10},{3,11},{4,12},{5,13},{6,14},{7,15},{8,0},{9,1},... | collective-permute-start | bytes 884744 | tf_op jit(solution)/shard_map/ppermute | solution.py:189
  24.7 0.7 copy-done.7
  25.5 11.6 %collective-permute-done.refs_0_.refs_1_ = bf16[128,1152]{1,0:T(8,128)(2,1)S(1)} collective-permute-done((bf16[128,1152]{1,0:T(8,128)(2,1)}, bf16[128,1152]{1,0:T(8,128)(2,1)S(1)}, u32[]{:S(2)}, u32[]{:S(2)}) %collective-permute-start) | collective-permute-done | bytes 294944 | tf_op jit(solution)/shard_map/ppermute | solution.py:189
  37.2 2.7 %shard_map.94 = (f32[128,384]{1,0:T(8,128)S(1)}, bf16[128,768]{1,0:T(8,128)(2,1)S(1)}, bf16[128,1152]{1,0:T(8,128)(2,1)S(1)}, bf16[128,1152]{1,0:T(8,128)(2,1)},...) custom-call(s32[30]{0:T(128)S(1)} %reshape.37.pick, bf16[30,128,128]{2,1,0:T(8,128)(2,1)S(1)} %bitcast.9, ...), custom_call_target="tpu_custom_call" | custom-call | tf_op jit(solution)/shard_map/pallas_call | solution.py:46
  39.8 1.1 shard_map.96
  40.9 3.5 %collective-permute-start.8 = (bf16[15,128,128]{2,1,0:T(8,128)(2,1)S(1)}, bf16[15,128,128]{2,1,0:T(8,128)(2,1)S(1)}, u32[]{:S(2)}, u32[]{:S(2)}) collective-permute-start(bf16[15,128,128]{2,1,0:T(8,128)(2,1)S(1)} %get-tuple-element.37), channel_id=1, source_target_pairs={{0,16},{16,0},{32,48},{48,32},{64,80},{80,64},{96,112},{112,96},{1... | collective-permute-start | bytes 1474568 | tf_op jit(solution)/shard_map/ppermute | solution.py:189
  44.4 2.1 %collective-permute-start.4 = (bf16[128,1152]{1,0:T(8,128)(2,1)S(1)}, bf16[128,1152]{1,0:T(8,128)(2,1)S(1)}, u32[]{:S(2)}, u32[]{:S(2)}) collective-permute-start(bf16[128,1152]{1,0:T(8,128)(2,1)S(1)} %get-tuple-element.29.refs_0_), channel_id=1, source_target_pairs={{0,1},{1,0},{2,3},{3,2},{4,5},{5,4},{6,7},{7,6},{8,9},{9,8},{10,11... | collective-permute-start | bytes 884744 | tf_op jit(solution)/shard_map/ppermute | solution.py:189
  46.5 7.3 %collective-permute-start.5 = (bf16[128,1152]{1,0:T(8,128)(2,1)}, bf16[128,1152]{1,0:T(8,128)(2,1)S(1)}, u32[]{:S(2)}, u32[]{:S(2)}) collective-permute-start(bf16[128,1152]{1,0:T(8,128)(2,1)} %get-tuple-element.30), channel_id=1, source_target_pairs={{0,2},{1,3},{2,0},{3,1},{4,6},{5,7},{6,4},{7,5},{8,10},{9,11},{10,... | collective-permute-start | bytes 884744 | tf_op jit(solution)/shard_map/ppermute | solution.py:189
  53.9 3.1 %collective-permute-start.6 = (bf16[128,1152]{1,0:T(8,128)(2,1)}, bf16[128,1152]{1,0:T(8,128)(2,1)S(1)}, u32[]{:S(2)}, u32[]{:S(2)}) collective-permute-start(bf16[128,1152]{1,0:T(8,128)(2,1)} %get-tuple-element.31), channel_id=1, source_target_pairs={{0,4},{1,5},{2,6},{3,7},{4,0},{5,1},{6,2},{7,3},{8,12},{9,13},{10,... | collective-permute-start | bytes 884744 | tf_op jit(solution)/shard_map/ppermute | solution.py:189
  57.0 4.4 %collective-permute-start.7 = (bf16[128,1152]{1,0:T(8,128)(2,1)S(1)}, bf16[128,1152]{1,0:T(8,128)(2,1)S(1)}, u32[]{:S(2)}, u32[]{:S(2)}) collective-permute-start(bf16[128,1152]{1,0:T(8,128)(2,1)S(1)} %get-tuple-element.32), channel_id=1, source_target_pairs={{0,8},{1,9},{2,10},{3,11},{4,12},{5,13},{6,14},{7,15},{8,0},{9,1},... | collective-permute-start | bytes 884744 | tf_op jit(solution)/shard_map/ppermute | solution.py:189
  61.3 0.9 add_convert_fusion.1
  62.3 10.9 %all-to-all-start = ((bf16[16,120,128]{2,1,0:T(8,128)(2,1)}), bf16[16,120,128]{2,1,0:T(8,128)(2,1)S(1)}, u32[]{:S(2)}, u32[]{:S(2)}) async-start(bf16[16,120,128]{2,1,0:T(8,128)(2,1)} %bitcast.3), calls=%async_computation | async-start | bytes 983040 | tf_op jit(solution)/shard_map/all_to_all | solution.py:213
  73.2 1.6 %collective-permute-done.4.refs_1_ = bf16[128,1152]{1,0:T(8,128)(2,1)S(1)} collective-permute-done((bf16[128,1152]{1,0:T(8,128)(2,1)S(1)}, bf16[128,1152]{1,0:T(8,128)(2,1)S(1)}, u32[]{:S(2)}, u32[]{:S(2)}) %collective-permute-start.4) | collective-permute-done | bytes 294944 | tf_op jit(solution)/shard_map/ppermute | solution.py:189
  74.8 1.1 shard_map.97
  75.9 2.8 %collective-permute-start.9 = (bf16[15,128,128]{2,1,0:T(8,128)(2,1)S(1)}, bf16[15,128,128]{2,1,0:T(8,128)(2,1)S(1)}, u32[]{:S(2)}, u32[]{:S(2)}) collective-permute-start(bf16[15,128,128]{2,1,0:T(8,128)(2,1)S(1)} %get-tuple-element.39), channel_id=1, source_target_pairs={{0,16},{16,0},{32,48},{48,32},{64,80},{80,64},{96,112},{112,96},{1... | collective-permute-start | bytes 1474568 | tf_op jit(solution)/shard_map/ppermute | solution.py:189
  78.7 1.5 %collective-permute-done.9 = bf16[15,128,128]{2,1,0:T(8,128)(2,1)S(1)} collective-permute-done((bf16[15,128,128]{2,1,0:T(8,128)(2,1)S(1)}, bf16[15,128,128]{2,1,0:T(8,128)(2,1)S(1)}, u32[]{:S(2)}, u32[]{:S(2)}) %collective-permute-start.9) | collective-permute-done | bytes 491552 | tf_op jit(solution)/shard_map/ppermute | solution.py:189
  80.3 9.1 %all-to-all-done.refs_0_ = bf16[16,120,128]{2,1,0:T(8,128)(2,1)S(1)} async-done(((bf16[16,120,128]{2,1,0:T(8,128)(2,1)}), bf16[16,120,128]{2,1,0:T(8,128)(2,1)S(1)}, u32[]{:S(2)}, u32[]{:S(2)}) %all-to-all-start) | async-done | bytes 491552 | tf_op jit(solution)/shard_map/all_to_all | solution.py:213
  89.4 15.1 %all_to_all.15.refs_1_ = bf16[16,120,128]{2,1,0:T(8,128)(2,1)S(1)} all-to-all(bf16[16,120,128]{2,1,0:T(8,128)(2,1)S(1)} %bitcast.10), channel_id=1, replica_groups={{0,32,64,96,128,160,192,224,256,288,320,352,384,416,448,480},{16,48,80,..., dimensions={0} | all-to-all | bytes 983040 | tf_op jit(solution)/shard_map/all_to_all | solution.py:213
  104.5 0.1 shard_map.98
  104.6 30.9 %all_to_all.16.mine = bf16[16,240,128]{2,1,0:T(8,128)(2,1)S(1)} all-to-all(bf16[16,240,128]{2,1,0:T(8,128)(2,1)S(1)} %shard_map.98), channel_id=1, replica_groups={{0,32,64,96,128,160,192,224,256,288,320,352,384,416,448,480},{16,48,80,..., dimensions={0} | all-to-all | bytes 1966080 | tf_op jit(solution)/shard_map/all_to_all | solution.py:213
  135.5 5.2 %collective-permute-start.10 = (bf16[16,240,128]{2,1,0:T(8,128)(2,1)S(1)}, bf16[16,240,128]{2,1,0:T(8,128)(2,1)S(1)}, u32[]{:S(2)}, u32[]{:S(2)}) collective-permute-start(bf16[16,240,128]{2,1,0:T(8,128)(2,1)S(1)} %all_to_all.16.mine), channel_id=1, source_target_pairs={{0,16},{16,0},{32,48},{48,32},{64,80},{80,64},{96,112},{112,96},{1... | collective-permute-start | bytes 2949128 | tf_op jit(solution)/shard_map/ppermute | solution.py:189
  140.7 1.7 %shard_map.95 = (bf16[128,384]{1,0:T(8,128)(2,1)}, bf16[128,384]{1,0:T(8,128)(2,1)}) custom-call(s32[30]{0:T(128)S(1)} %reshape.35.pick, bf16[30,128,128]{2,1,0:T(8,128)(2,1)S(1)} %bitcast.8, f32[128,384]{1,0:T(8,128)S(1)} %get-tuple-element.28.in0, bf16[128,1152]{1,0:T(8,128)(2,1)S(1)} %get-tuple-element.29.refs_0_, ...), custom_call_target="tpu_custom_call" | custom-call | tf_op jit(solution)/shard_map/pallas_call | solution.py:46
  142.4 0.5 collective-permute-done.10.other
  142.9 1.4 shard_map.99
  (23 shorter events, 0.4 us)
Async XLA Ops:
  1.5 1.2 copy-start
  2.7 0.9 copy-start.3
  3.6 0.9 copy-start.5
  4.5 32.6 %copy-start.2 = (bf16[1,5,6,128,128]{4,3,2,1,0:T(8,128)(2,1)S(1)}, bf16[1,5,6,128,128]{4,3,2,1,0:T(8,128)(2,1)}, u32[]{:S(2)}) copy-start(bf16[1,5,6,128,128]{4,3,2,1,0:T(8,128)(2,1)} %param.7) | copy-start | bytes 2949124
  4.5 32.7 %copy-start.4 = (bf16[128,384]{1,0:T(8,128)(2,1)S(1)}, bf16[128,384]{1,0:T(8,128)(2,1)}, u32[]{:S(2)}) copy-start(bf16[128,384]{1,0:T(8,128)(2,1)} %refs_0_.1) | copy-start | bytes 294916
  6.5 30.6 %collective-permute-start = (bf16[128,1152]{1,0:T(8,128)(2,1)}, bf16[128,1152]{1,0:T(8,128)(2,1)S(1)}, u32[]{:S(2)}, u32[]{:S(2)}) collective-permute-start(bf16[128,1152]{1,0:T(8,128)(2,1)} %get-tuple-element.24), channel_id=1, source_target_pairs={{0,1},{1,0},{2,3},{3,2},{4,5},{5,4},{6,7},{7,6},{8,9},{9,8},{10,11... | collective-permute-start | bytes 884744 | tf_op jit(solution)/shard_map/ppermute | solution.py:189
  11.6 25.6 %collective-permute-start.1 = (bf16[128,1152]{1,0:T(8,128)(2,1)}, bf16[128,1152]{1,0:T(8,128)(2,1)S(1)}, u32[]{:S(2)}, u32[]{:S(2)}) collective-permute-start(bf16[128,1152]{1,0:T(8,128)(2,1)} %get-tuple-element.25), channel_id=1, source_target_pairs={{0,2},{1,3},{2,0},{3,1},{4,6},{5,7},{6,4},{7,5},{8,10},{9,11},{10,... | collective-permute-start | bytes 884744 | tf_op jit(solution)/shard_map/ppermute | solution.py:189
  17.2 19.9 %collective-permute-start.2 = (bf16[128,1152]{1,0:T(8,128)(2,1)S(1)}, bf16[128,1152]{1,0:T(8,128)(2,1)S(1)}, u32[]{:S(2)}, u32[]{:S(2)}) collective-permute-start(bf16[128,1152]{1,0:T(8,128)(2,1)S(1)} %get-tuple-element.26), channel_id=1, source_target_pairs={{0,4},{1,5},{2,6},{3,7},{4,0},{5,1},{6,2},{7,3},{8,12},{9,13},{10,... | collective-permute-start | bytes 884744 | tf_op jit(solution)/shard_map/ppermute | solution.py:189
  20.4 16.8 %collective-permute-start.3 = (bf16[128,1152]{1,0:T(8,128)(2,1)S(1)}, bf16[128,1152]{1,0:T(8,128)(2,1)S(1)}, u32[]{:S(2)}, u32[]{:S(2)}) collective-permute-start(bf16[128,1152]{1,0:T(8,128)(2,1)S(1)} %get-tuple-element.27), channel_id=1, source_target_pairs={{0,8},{1,9},{2,10},{3,11},{4,12},{5,13},{6,14},{7,15},{8,0},{9,1},... | collective-permute-start | bytes 884744 | tf_op jit(solution)/shard_map/ppermute | solution.py:189
  24.7 0.7 copy-start.7
  40.9 20.4 %collective-permute-start.8 = (bf16[15,128,128]{2,1,0:T(8,128)(2,1)S(1)}, bf16[15,128,128]{2,1,0:T(8,128)(2,1)S(1)}, u32[]{:S(2)}, u32[]{:S(2)}) collective-permute-start(bf16[15,128,128]{2,1,0:T(8,128)(2,1)S(1)} %get-tuple-element.37), channel_id=1, source_target_pairs={{0,16},{16,0},{32,48},{48,32},{64,80},{80,64},{96,112},{112,96},{1... | collective-permute-start | bytes 1474568 | tf_op jit(solution)/shard_map/ppermute | solution.py:189
  44.4 30.4 %collective-permute-start.4 = (bf16[128,1152]{1,0:T(8,128)(2,1)S(1)}, bf16[128,1152]{1,0:T(8,128)(2,1)S(1)}, u32[]{:S(2)}, u32[]{:S(2)}) collective-permute-start(bf16[128,1152]{1,0:T(8,128)(2,1)S(1)} %get-tuple-element.29.refs_0_), channel_id=1, source_target_pairs={{0,1},{1,0},{2,3},{3,2},{4,5},{5,4},{6,7},{7,6},{8,9},{9,8},{10,11... | collective-permute-start | bytes 884744 | tf_op jit(solution)/shard_map/ppermute | solution.py:189
  46.5 28.3 %collective-permute-start.5 = (bf16[128,1152]{1,0:T(8,128)(2,1)}, bf16[128,1152]{1,0:T(8,128)(2,1)S(1)}, u32[]{:S(2)}, u32[]{:S(2)}) collective-permute-start(bf16[128,1152]{1,0:T(8,128)(2,1)} %get-tuple-element.30), channel_id=1, source_target_pairs={{0,2},{1,3},{2,0},{3,1},{4,6},{5,7},{6,4},{7,5},{8,10},{9,11},{10,... | collective-permute-start | bytes 884744 | tf_op jit(solution)/shard_map/ppermute | solution.py:189
  53.9 20.9 %collective-permute-start.6 = (bf16[128,1152]{1,0:T(8,128)(2,1)}, bf16[128,1152]{1,0:T(8,128)(2,1)S(1)}, u32[]{:S(2)}, u32[]{:S(2)}) collective-permute-start(bf16[128,1152]{1,0:T(8,128)(2,1)} %get-tuple-element.31), channel_id=1, source_target_pairs={{0,4},{1,5},{2,6},{3,7},{4,0},{5,1},{6,2},{7,3},{8,12},{9,13},{10,... | collective-permute-start | bytes 884744 | tf_op jit(solution)/shard_map/ppermute | solution.py:189
  57.0 17.8 %collective-permute-start.7 = (bf16[128,1152]{1,0:T(8,128)(2,1)S(1)}, bf16[128,1152]{1,0:T(8,128)(2,1)S(1)}, u32[]{:S(2)}, u32[]{:S(2)}) collective-permute-start(bf16[128,1152]{1,0:T(8,128)(2,1)S(1)} %get-tuple-element.32), channel_id=1, source_target_pairs={{0,8},{1,9},{2,10},{3,11},{4,12},{5,13},{6,14},{7,15},{8,0},{9,1},... | collective-permute-start | bytes 884744 | tf_op jit(solution)/shard_map/ppermute | solution.py:189
  62.3 12.5 %copy-start.6 = (bf16[128,384]{1,0:T(8,128)(2,1)S(1)}, bf16[128,384]{1,0:T(8,128)(2,1)}, u32[]{:S(2)}) copy-start(bf16[128,384]{1,0:T(8,128)(2,1)} %cot.3) | copy-start | bytes 294916
  62.3 27.1 %all-to-all-start = ((bf16[16,120,128]{2,1,0:T(8,128)(2,1)}), bf16[16,120,128]{2,1,0:T(8,128)(2,1)S(1)}, u32[]{:S(2)}, u32[]{:S(2)}) async-start(bf16[16,120,128]{2,1,0:T(8,128)(2,1)} %bitcast.3), calls=%async_computation | async-start | bytes 983040 | tf_op jit(solution)/shard_map/all_to_all | solution.py:213
  75.9 4.3 %collective-permute-start.9 = (bf16[15,128,128]{2,1,0:T(8,128)(2,1)S(1)}, bf16[15,128,128]{2,1,0:T(8,128)(2,1)S(1)}, u32[]{:S(2)}, u32[]{:S(2)}) collective-permute-start(bf16[15,128,128]{2,1,0:T(8,128)(2,1)S(1)} %get-tuple-element.39), channel_id=1, source_target_pairs={{0,16},{16,0},{32,48},{48,32},{64,80},{80,64},{96,112},{112,96},{1... | collective-permute-start | bytes 1474568 | tf_op jit(solution)/shard_map/ppermute | solution.py:189
  104.6 36.1 %copy-start.1 = (bf16[1,5,3,2,128,128]{5,4,3,2,1,0:T(8,128)(2,1)S(1)}, bf16[1,5,3,2,128,128]{5,4,3,2,1,0:T(8,128)(2,1)}, u32[]{:S(2)}) copy-start(bf16[1,5,3,2,128,128]{5,4,3,2,1,0:T(8,128)(2,1)} %param.9) | copy-start | bytes 2949124
  135.5 7.4 %collective-permute-start.10 = (bf16[16,240,128]{2,1,0:T(8,128)(2,1)S(1)}, bf16[16,240,128]{2,1,0:T(8,128)(2,1)S(1)}, u32[]{:S(2)}, u32[]{:S(2)}) collective-permute-start(bf16[16,240,128]{2,1,0:T(8,128)(2,1)S(1)} %all_to_all.16.mine), channel_id=1, source_target_pairs={{0,16},{16,0},{32,48},{48,32},{64,80},{80,64},{96,112},{112,96},{1... | collective-permute-start | bytes 2949128 | tf_op jit(solution)/shard_map/ppermute | solution.py:189

commit v3 on v2

--- a/solution.py
+++ b/solution.py
@@ -17,7 +17,9 @@
 
 
 VMEM = pl.BlockSpec(memory_space=pltpu.VMEM)
+ARG = pl.BlockSpec(memory_space=pltpu.VMEM)
 SMEM = pl.BlockSpec(memory_space=pltpu.SMEM)
+SPACE = {id(VMEM): pltpu.VMEM, id(ARG): pltpu.HBM}
 
 
 def sds(shape, dtype):
@@ -40,7 +42,7 @@
 
     def invoke(*args):
         placed = [
-            a if spec is SMEM else pltpu.with_memory_space_constraint(a, pltpu.VMEM)
+            a if spec is SMEM else pltpu.with_memory_space_constraint(a, SPACE[id(spec)])
             for a, spec in zip(args, in_specs)
         ]
         return run(*placed)
@@ -81,8 +83,7 @@
 
 
 def mid_kernel(levels, db, hb, pick, w, x, own, *refs):
-    got = refs[: levels - 1]
-    in0, hg, sends, acc = refs[levels - 1], refs[levels], refs[levels + 1 : -1], refs[-1]
+    got, hg, act = refs[: levels - 1], refs[levels - 1], refs[levels]
     xs = (x,) + got
     wide = db * B
     for o in range(hb):
@@ -95,26 +96,24 @@
         sq = v * v
         t = jnp.tanh(GELU_C * (v + GELU_A * (v * sq)))
         half = 0.5 * (1.0 + t)
-        act = (v * half).astype(BF16)
-        for send in sends:
-            send[:, here] = act
+        act[:, here] = (v * half).astype(BF16)
         inner = GELU_C * (1.0 + (3.0 * GELU_A) * sq)
         slope = half + 0.5 * v * (1.0 - t * t) * inner
         grad = own[:, here]
         for ref in got:
             grad = grad + ref[:, wide + o * B : wide + (o + 1) * B].astype(F32)
         hg[:, here] = (grad * slope).astype(BF16)
-    base = hb * B
+
+
+def in_kernel(levels, db, hb, pick, hg, w, *refs):
+    outs, acc = refs[:levels], refs[levels]
     for lvl in range(levels):
         acc[...] = jnp.zeros_like(acc)
         for o in range(hb):
             spot = pick[lvl * hb + o]
             acc[spot] += dot_nt(hg[:, o * B : (o + 1) * B], w[lvl * hb + o])
         for d in range(db):
-            if lvl == 0:
-                in0[:, d * B : (d + 1) * B] = acc[d]
-            else:
-                sends[lvl - 1][:, base + d * B : base + (d + 1) * B] = acc[d].astype(BF16)
+            outs[lvl][:, d * B : (d + 1) * B] = acc[d].astype(outs[lvl].dtype)
 
 
 def split(core, scr, keep, send):
@@ -146,12 +145,24 @@
     split(core[0], scr, keep, send)
 
 
-def out_kernel(levels, db, hb, kd, pick, w, in0, *refs):
-    acts, out, dx = refs[:levels], refs[levels], refs[levels + 1]
-    total = in0[...]
-    for ref in acts[1:]:
-        total = total + ref[:, hb * B :].astype(F32)
-    dx[...] = total.astype(BF16)
+def pair_kernel(*refs):
+    out = refs[-1]
+    at = 0
+    for keep, got in zip(refs[0:-1:2], refs[1:-1:2]):
+        rows = keep.shape[1]
+        out[:, at : at + rows, :] = (keep[...] + got[...].astype(F32)).astype(BF16)
+        at += rows
+
+
+def dx_kernel(own, *refs):
+    total = own[...]
+    for ref in refs[:-1]:
+        total = total + ref[...].astype(F32)
+    refs[-1][...] = total.astype(BF16)
+
+
+def out_kernel(levels, db, kd, pick, w, *refs):
+    acts, out = refs[:levels], refs[levels]
     for o in range(db):
         spots = [(lvl * db + o) * kd + k for lvl in range(levels) for k in range(kd)]
         lhs = jnp.concatenate(
@@ -161,18 +172,13 @@
         out[:, o * B : (o + 1) * B] = jnp.dot(lhs, rhs, preferred_element_type=F32).astype(BF16)
 
 
-def shard_kernel(scale, *refs):
-    out = refs[-1]
-    at = 0
-    for ref in refs[:-1]:
-        total = ref[0].astype(F32)
-        for i in range(1, ref.shape[0]):
-            total = total + ref[i].astype(F32)
-        total = (total * scale).astype(BF16)
-        rows = ref.shape[1]
-        for i in range(out.shape[0]):
-            out[i, at : at + rows, :] = total
-        at += rows
+def shard_kernel(scale, parts, out):
+    total = parts[0].astype(F32)
+    for i in range(1, parts.shape[0]):
+        total = total + parts[i].astype(F32)
+    total = (total * scale).astype(BF16)
+    for i in range(out.shape[0]):
+        out[i] = total
 
 
 def join_kernel(core, mine, other, *outs):
@@ -214,28 +220,32 @@
             block, "dp", split_axis=0, concat_axis=0, axis_index_groups=groups, tiled=True
         )
 
-    def partials(keep, send):
-        got = from_partner(send, "dp", 0)
-        pair = (keep + got.astype(F32)).astype(BF16)
-        return exchange(pair.reshape(chips, -1, B))
-
     wide, deep = db * B, hb * B
     own, *first = call(
         functools.partial(back_kernel, levels, db, hb, kd),
         [sds((tokens, deep), F32)] + [sds((tokens, wide + deep), BF16)] * bits,
-        [SMEM, VMEM, VMEM, VMEM],
+        [SMEM, ARG, ARG, ARG],
         [pltpu.VMEM((hb, tokens, B), F32)],
     )(down_ids, cotangent, down_w, inputs)
     got = over_mp(first)
 
-    in0, hg, *second = call(
+    hg, act = call(
         functools.partial(mid_kernel, levels, db, hb),
-        [sds((tokens, wide), F32), sds((tokens, deep), BF16)]
-        + [sds((tokens, deep + wide), BF16)] * bits,
+        [sds((tokens, deep), BF16)] * 2,
         [SMEM] + [VMEM] * (levels + 2),
+        (),
+    )(up_ids, up_w, inputs, own, *got)
+    acts = [act] + over_mp([act] * bits)
+
+    in0, *in_terms = call(
+        functools.partial(in_kernel, levels, db, hb),
+        [sds((tokens, wide), F32)] + [sds((tokens, wide), BF16)] * bits,
+        [SMEM, VMEM, VMEM],
         [pltpu.VMEM((db, tokens, B), F32)],
-    )(up_ids, up_w, inputs, own, *got)
-    acts = [second[0]] + over_mp(second)
+    )(up_ids, hg, up_w)
+    grad_inputs = call(
+        dx_kernel, hbm((tokens, wide), BF16), [VMEM] * levels, ()
+    )(in0, *over_mp(in_terms))
 
     def grad_outs(count):
         return [sds((count // 2, B, B), F32), sds((count // 2, B, B), BF16)]
@@ -246,7 +256,7 @@
         [SMEM, SMEM, VMEM] + [VMEM] * levels,
         [pltpu.VMEM((n_up, B, B), F32)],
     )(up_ids, core, hg, inputs, *got)
-    up_parts = partials(up_keep, up_send)
+    up_got = from_partner(up_send, "dp", 0)
 
     down_keep, down_send = call(
         functools.partial(down_kernel, levels, db, kd),
@@ -254,19 +264,22 @@
         [SMEM, SMEM, VMEM] + [VMEM] * levels,
         [pltpu.VMEM((n_down, B, B), F32)],
     )(down_ids, core, cotangent, *acts)
-    down_parts = partials(down_keep, down_send)
-
-    output, grad_inputs = call(
-        functools.partial(out_kernel, levels, db, hb, kd),
-        [hbm((tokens, wide), BF16)] * 2,
-        [SMEM, VMEM, VMEM] + [VMEM] * levels,
+    down_got = from_partner(down_send, "dp", 0)
+
+    output = call(
+        functools.partial(out_kernel, levels, db, kd),
+        hbm((tokens, wide), BF16),
+        [SMEM, VMEM] + [VMEM] * levels,
         (),
-    )(down_ids, down_w, in0, *acts)
-
-    rows = [up_parts.shape[1], down_parts.shape[1]]
+    )(down_ids, down_w, *acts)
+
+    halves = [a.reshape(chips, -1, B) for a in (up_keep, up_got, down_keep, down_got)]
+    rows = [halves[0].shape[1], halves[2].shape[1]]
+    pair = call(pair_kernel, sds((chips, sum(rows), B), BF16), [VMEM] * 4, ())(*halves)
+    parts = exchange(pair)
     shard = call(
-        functools.partial(shard_kernel, scale), sds((chips, sum(rows), B), BF16), [VMEM, VMEM], ()
-    )(up_parts, down_parts)
+        functools.partial(shard_kernel, scale), sds((chips, sum(rows), B), BF16), [VMEM], ()
+    )(parts)
     mine = exchange(shard)
     other = from_partner(mine, "dp", 0)
     up_out, down_out = call(

time: 145 us -> 167 us (1.15)
  blocking collectives: 45.9 us -> 63 us
  waiting for transfers between devices: 24.3 us -> 29.6 us
  local copies, waits for them, and re-layouts: 4.64 us -> 1.06 us
  starting transfers between devices: 57.4 us -> 59.2 us
    all_to_all x2, blocking collectives: 45.9 us -> 63 us  [exchange(): lax.all_to_all(block, 'dp', split_axis=0, concat_axis=0, axis_index_group...]
    ppermute x11 -> x15, waiting for transfers between devices: 15.2 us -> 29.6 us  [from_partner(): return lax.ppermute(block, axis, [(i, i ^ 1 << bit) for i in range(count)])]
    ppermute x11 -> x15, starting transfers between devices: 46.5 us -> 59.2 us  [from_partner(): return lax.ppermute(block, axis, [(i, i ^ 1 << bit) for i in range(count)])]
    all_to_all x1 -> x0, starting transfers between devices: 10.9 us -> none  [exchange(): lax.all_to_all(block, 'dp', split_axis=0, concat_axis=0, axis_index_group...]
    all_to_all x1 -> x0, waiting for transfers between devices: 9.07 us -> none  [exchange(): lax.all_to_all(block, 'dp', split_axis=0, concat_axis=0, axis_index_group...]
    unnamed x17 -> x11, local copies, waits for them, and re-layouts: 4.47 us -> 0.9 us
    pallas_call x7 -> x10, Pallas kernels: 10.1 us -> 11.6 us  [invoke(): return run(*placed)]
  transfers between devices with their start and end apart: 12 -> 15, of which waited for: 5 -> 6; matrix products, arithmetic and copies ran while one was open for 1% -> 0% of each run, Pallas kernels for 2% -> 4%
where the time goes in v3:
time: 167 us; the launch traced here: 165 us
  blocking collectives  63 us (38%)
  starting transfers between devices  59.2 us (35%)
  waiting for transfers between devices  29.6 us (18%)
  Pallas kernels  11.6 us (7%)
    all_to_all x2, blocking collectives, exchange(): lax.all_to_all(block, 'dp', split_axis=0, concat_axis=0, axis_index_group...  63 us
    ppermute x15, starting transfers between devices, from_partner(): return lax.ppermute(block, axis, [(i, i ^ 1 << bit) for i in range(count)])  59.2 us
    ppermute x15, waiting for transfers between devices, from_partner(): return lax.ppermute(block, axis, [(i, i ^ 1 << bit) for i in range(count)])  29.6 us
    pallas_call x10, Pallas kernels, invoke(): return run(*placed)  11.6 us
  transfers between devices with their start and end apart: 15, of which 6 were waited for; matrix products, arithmetic and copies ran while one was open for 0% of the time, Pallas kernels for 4%

profile of v3, /device:TPU:1, one launch (start us, length us, event | category | flops | bytes accessed | tf_op | source)
XLA Modules:
  0.0 165.4 jit_solution(10944289290545550677)
XLA Ops:
  0.6 0.9 copy.11
  1.6 2.7 %shard_map.93 = (f32[128,768]{1,0:T(8,128)S(1)}, bf16[128,1152]{1,0:T(8,128)(2,1)}, bf16[128,1152]{1,0:T(8,128)(2,1)}, bf16[128,1152]{1,0:T(8,128)(2,1)S(1)}, bf16[128,1152]{1,0:T(8,128)(2,1)S(1)}) custom-call(s32[30]{0:T(128)S(1)} %reshape.41.pick, bf16[128,384]{1,0:T(8,128)(2,1)} %cot.3, bf16[30,128,128]{2,1,0:T(8,128)(2,1)} %bitcast.9, ...), custom_call_target="tpu_custom_call" | custom-call | tf_op jit(solution)/shard_map/pallas_call | solution.py:48
  4.4 5.2 %collective-permute-start = (bf16[128,1152]{1,0:T(8,128)(2,1)}, bf16[128,1152]{1,0:T(8,128)(2,1)S(1)}, u32[]{:S(2)}, u32[]{:S(2)}) collective-permute-start(bf16[128,1152]{1,0:T(8,128)(2,1)} %get-tuple-element.23), channel_id=1, source_target_pairs={{0,1},{1,0},{2,3},{3,2},{4,5},{5,4},{6,7},{7,6},{8,9},{9,8},{10,11... | collective-permute-start | bytes 884744 | tf_op jit(solution)/shard_map/ppermute | solution.py:195
  9.5 5.6 %collective-permute-start.1 = (bf16[128,1152]{1,0:T(8,128)(2,1)}, bf16[128,1152]{1,0:T(8,128)(2,1)S(1)}, u32[]{:S(2)}, u32[]{:S(2)}) collective-permute-start(bf16[128,1152]{1,0:T(8,128)(2,1)} %get-tuple-element.24), channel_id=1, source_target_pairs={{0,2},{1,3},{2,0},{3,1},{4,6},{5,7},{6,4},{7,5},{8,10},{9,11},{10,... | collective-permute-start | bytes 884744 | tf_op jit(solution)/shard_map/ppermute | solution.py:195
  15.2 3.1 %collective-permute-start.2 = (bf16[128,1152]{1,0:T(8,128)(2,1)S(1)}, bf16[128,1152]{1,0:T(8,128)(2,1)S(1)}, u32[]{:S(2)}, u32[]{:S(2)}) collective-permute-start(bf16[128,1152]{1,0:T(8,128)(2,1)S(1)} %get-tuple-element.25), channel_id=1, source_target_pairs={{0,4},{1,5},{2,6},{3,7},{4,0},{5,1},{6,2},{7,3},{8,12},{9,13},{10,... | collective-permute-start | bytes 884744 | tf_op jit(solution)/shard_map/ppermute | solution.py:195
  18.3 4.4 %collective-permute-start.3 = (bf16[128,1152]{1,0:T(8,128)(2,1)S(1)}, bf16[128,1152]{1,0:T(8,128)(2,1)S(1)}, u32[]{:S(2)}, u32[]{:S(2)}) collective-permute-start(bf16[128,1152]{1,0:T(8,128)(2,1)S(1)} %get-tuple-element.26), channel_id=1, source_target_pairs={{0,8},{1,9},{2,10},{3,11},{4,12},{5,13},{6,14},{7,15},{8,0},{9,1},... | collective-permute-start | bytes 884744 | tf_op jit(solution)/shard_map/ppermute | solution.py:195
  22.8 12.3 %collective-permute-done.refs_0_.refs_1_ = bf16[128,1152]{1,0:T(8,128)(2,1)S(1)} collective-permute-done((bf16[128,1152]{1,0:T(8,128)(2,1)}, bf16[128,1152]{1,0:T(8,128)(2,1)S(1)}, u32[]{:S(2)}, u32[]{:S(2)}) %collective-permute-start) | collective-permute-done | bytes 294944 | tf_op jit(solution)/shard_map/ppermute | solution.py:195
  35.1 1.2 shard_map.94
  36.3 4.7 %collective-permute-start.7 = (bf16[128,768]{1,0:T(8,128)(2,1)S(1)}, bf16[128,768]{1,0:T(8,128)(2,1)S(1)}, u32[]{:S(2)}, u32[]{:S(2)}) collective-permute-start(bf16[128,768]{1,0:T(8,128)(2,1)S(1)} %get-tuple-element.27.refs_0_), channel_id=1, source_target_pairs={{0,8},{1,9},{2,10},{3,11},{4,12},{5,13},{6,14},{7,15},{8,0},{9,1},... | collective-permute-start | bytes 589832 | tf_op jit(solution)/shard_map/ppermute | solution.py:195
  41.1 2.2 %collective-permute-start.6 = (bf16[128,768]{1,0:T(8,128)(2,1)S(1)}, bf16[128,768]{1,0:T(8,128)(2,1)S(1)}, u32[]{:S(2)}, u32[]{:S(2)}) collective-permute-start(bf16[128,768]{1,0:T(8,128)(2,1)S(1)} %get-tuple-element.27.refs_0_), channel_id=1, source_target_pairs={{0,4},{1,5},{2,6},{3,7},{4,0},{5,1},{6,2},{7,3},{8,12},{9,13},{10,... | collective-permute-start | bytes 589832 | tf_op jit(solution)/shard_map/ppermute | solution.py:195
  43.3 8.4 %collective-permute-start.5 = (bf16[128,768]{1,0:T(8,128)(2,1)S(1)}, bf16[128,768]{1,0:T(8,128)(2,1)S(1)}, u32[]{:S(2)}, u32[]{:S(2)}) collective-permute-start(bf16[128,768]{1,0:T(8,128)(2,1)S(1)} %get-tuple-element.27.refs_0_), channel_id=1, source_target_pairs={{0,2},{1,3},{2,0},{3,1},{4,6},{5,7},{6,4},{7,5},{8,10},{9,11},{10,... | collective-permute-start | bytes 589832 | tf_op jit(solution)/shard_map/ppermute | solution.py:195
  51.7 1.9 %collective-permute-start.4 = (bf16[128,768]{1,0:T(8,128)(2,1)S(1)}, bf16[128,768]{1,0:T(8,128)(2,1)S(1)}, u32[]{:S(2)}, u32[]{:S(2)}) collective-permute-start(bf16[128,768]{1,0:T(8,128)(2,1)S(1)} %get-tuple-element.27.refs_0_), channel_id=1, source_target_pairs={{0,1},{1,0},{2,3},{3,2},{4,5},{5,4},{6,7},{7,6},{8,9},{9,8},{10,11... | collective-permute-start | bytes 589832 | tf_op jit(solution)/shard_map/ppermute | solution.py:195
  53.6 1.1 shard_map.98
  54.7 3.4 %collective-permute-start.12 = (bf16[15,128,128]{2,1,0:T(8,128)(2,1)S(1)}, bf16[15,128,128]{2,1,0:T(8,128)(2,1)S(1)}, u32[]{:S(2)}, u32[]{:S(2)}) collective-permute-start(bf16[15,128,128]{2,1,0:T(8,128)(2,1)S(1)} %get-tuple-element.35), channel_id=1, source_target_pairs={{0,16},{16,0},{32,48},{48,32},{64,80},{80,64},{96,112},{112,96},{1... | collective-permute-start | bytes 1474568 | tf_op jit(solution)/shard_map/ppermute | solution.py:195
  58.1 0.4 collective-permute-done.5.refs_2_
  58.5 11.1 %collective-permute-done.4.refs_1_ = bf16[128,768]{1,0:T(8,128)(2,1)S(1)} collective-permute-done((bf16[128,768]{1,0:T(8,128)(2,1)S(1)}, bf16[128,768]{1,0:T(8,128)(2,1)S(1)}, u32[]{:S(2)}, u32[]{:S(2)}) %collective-permute-start.4) | collective-permute-done | bytes 196640 | tf_op jit(solution)/shard_map/ppermute | solution.py:195
  69.6 1.1 shard_map.99
  70.7 2.4 %collective-permute-start.13 = (bf16[15,128,128]{2,1,0:T(8,128)(2,1)S(1)}, bf16[15,128,128]{2,1,0:T(8,128)(2,1)S(1)}, u32[]{:S(2)}, u32[]{:S(2)}) collective-permute-start(bf16[15,128,128]{2,1,0:T(8,128)(2,1)S(1)} %get-tuple-element.37), channel_id=1, source_target_pairs={{0,16},{16,0},{32,48},{48,32},{64,80},{80,64},{96,112},{112,96},{1... | collective-permute-start | bytes 1474568 | tf_op jit(solution)/shard_map/ppermute | solution.py:195
  73.1 1.5 collective-permute-done.13
  74.6 0.2 shard_map.100
  74.8 32.6 %all_to_all.10.parts = bf16[16,240,128]{2,1,0:T(8,128)(2,1)S(1)} all-to-all(bf16[16,240,128]{2,1,0:T(8,128)(2,1)S(1)} %shard_map.100), channel_id=1, replica_groups={{0,32,64,96,128,160,192,224,256,288,320,352,384,416,448,480},{16,48,80,..., dimensions={0} | all-to-all | bytes 1966080 | tf_op jit(solution)/shard_map/all_to_all | solution.py:219
  107.5 30.4 %all_to_all.11.mine = bf16[16,240,128]{2,1,0:T(8,128)(2,1)S(1)} all-to-all(bf16[16,240,128]{2,1,0:T(8,128)(2,1)S(1)} %shard_map.101), channel_id=1, replica_groups={{0,32,64,96,128,160,192,224,256,288,320,352,384,416,448,480},{16,48,80,..., dimensions={0} | all-to-all | bytes 1966080 | tf_op jit(solution)/shard_map/all_to_all | solution.py:219
  138.0 5.2 %collective-permute-start.14 = (bf16[16,240,128]{2,1,0:T(8,128)(2,1)S(1)}, bf16[16,240,128]{2,1,0:T(8,128)(2,1)S(1)}, u32[]{:S(2)}, u32[]{:S(2)}) collective-permute-start(bf16[16,240,128]{2,1,0:T(8,128)(2,1)S(1)} %all_to_all.11.mine), channel_id=1, source_target_pairs={{0,16},{16,0},{32,48},{48,32},{64,80},{80,64},{96,112},{112,96},{1... | collective-permute-start | bytes 2949128 | tf_op jit(solution)/shard_map/ppermute | solution.py:195
  143.2 1.4 shard_map.96
  144.6 2.5 %collective-permute-start.8 = (bf16[128,384]{1,0:T(8,128)(2,1)S(1)}, bf16[128,384]{1,0:T(8,128)(2,1)S(1)}, u32[]{:S(2)}, u32[]{:S(2)}) collective-permute-start(bf16[128,384]{1,0:T(8,128)(2,1)S(1)} %get-tuple-element.30), channel_id=1, source_target_pairs={{0,1},{1,0},{2,3},{3,2},{4,5},{5,4},{6,7},{7,6},{8,9},{9,8},{10,11... | collective-permute-start | bytes 294920 | tf_op jit(solution)/shard_map/ppermute | solution.py:195
  147.0 4.7 %collective-permute-start.9 = (bf16[128,384]{1,0:T(8,128)(2,1)S(1)}, bf16[128,384]{1,0:T(8,128)(2,1)S(1)}, u32[]{:S(2)}, u32[]{:S(2)}) collective-permute-start(bf16[128,384]{1,0:T(8,128)(2,1)S(1)} %get-tuple-element.31), channel_id=1, source_target_pairs={{0,2},{1,3},{2,0},{3,1},{4,6},{5,7},{6,4},{7,5},{8,10},{9,11},{10,... | collective-permute-start | bytes 294920 | tf_op jit(solution)/shard_map/ppermute | solution.py:195
  151.8 3.1 %collective-permute-start.10 = (bf16[128,384]{1,0:T(8,128)(2,1)S(1)}, bf16[128,384]{1,0:T(8,128)(2,1)S(1)}, u32[]{:S(2)}, u32[]{:S(2)}) collective-permute-start(bf16[128,384]{1,0:T(8,128)(2,1)S(1)} %get-tuple-element.32), channel_id=1, source_target_pairs={{0,4},{1,5},{2,6},{3,7},{4,0},{5,1},{6,2},{7,3},{8,12},{9,13},{10,... | collective-permute-start | bytes 294920 | tf_op jit(solution)/shard_map/ppermute | solution.py:195
  154.8 2.5 %collective-permute-start.11 = (bf16[128,384]{1,0:T(8,128)(2,1)S(1)}, bf16[128,384]{1,0:T(8,128)(2,1)S(1)}, u32[]{:S(2)}, u32[]{:S(2)}) collective-permute-start(bf16[128,384]{1,0:T(8,128)(2,1)S(1)} %get-tuple-element.33), channel_id=1, source_target_pairs={{0,8},{1,9},{2,10},{3,11},{4,12},{5,13},{6,14},{7,15},{8,0},{9,1},... | collective-permute-start | bytes 294920 | tf_op jit(solution)/shard_map/ppermute | solution.py:195
  157.4 4.3 %collective-permute-done.11.refs_3_ = bf16[128,384]{1,0:T(8,128)(2,1)S(1)} collective-permute-done((bf16[128,384]{1,0:T(8,128)(2,1)S(1)}, bf16[128,384]{1,0:T(8,128)(2,1)S(1)}, u32[]{:S(2)}, u32[]{:S(2)}) %collective-permute-start.11) | collective-permute-done | bytes 98336 | tf_op jit(solution)/shard_map/ppermute | solution.py:195
  161.7 0.7 shard_map.97
  162.4 1.6 shard_map.95
  164.0 1.4 shard_map.102
  (24 shorter events, 0.5 us)
Async XLA Ops:
  0.6 34.5 %copy-start.1 = (bf16[1,5,6,128,128]{4,3,2,1,0:T(8,128)(2,1)S(1)}, bf16[1,5,6,128,128]{4,3,2,1,0:T(8,128)(2,1)}, u32[]{:S(2)}) copy-start(bf16[1,5,6,128,128]{4,3,2,1,0:T(8,128)(2,1)} %param.7) | copy-start | bytes 2949124
  1.6 33.5 %copy-start.2 = (bf16[128,384]{1,0:T(8,128)(2,1)S(1)}, bf16[128,384]{1,0:T(8,128)(2,1)}, u32[]{:S(2)}) copy-start(bf16[128,384]{1,0:T(8,128)(2,1)} %refs_0_.1) | copy-start | bytes 294916
  4.4 18.3 %copy-start.4 = (s32[1,5,6]{2,0,1:T(1,128)S(1)}, s32[1,5,6]{2,0,1:T(1,128)}, u32[]{:S(2)}) copy-start(s32[1,5,6]{2,0,1:T(1,128)} %param.8) | copy-start | bytes 364
  4.4 30.7 %collective-permute-start = (bf16[128,1152]{1,0:T(8,128)(2,1)}, bf16[128,1152]{1,0:T(8,128)(2,1)S(1)}, u32[]{:S(2)}, u32[]{:S(2)}) collective-permute-start(bf16[128,1152]{1,0:T(8,128)(2,1)} %get-tuple-element.23), channel_id=1, source_target_pairs={{0,1},{1,0},{2,3},{3,2},{4,5},{5,4},{6,7},{7,6},{8,9},{9,8},{10,11... | collective-permute-start | bytes 884744 | tf_op jit(solution)/shard_map/ppermute | solution.py:195
  9.5 25.6 %collective-permute-start.1 = (bf16[128,1152]{1,0:T(8,128)(2,1)}, bf16[128,1152]{1,0:T(8,128)(2,1)S(1)}, u32[]{:S(2)}, u32[]{:S(2)}) collective-permute-start(bf16[128,1152]{1,0:T(8,128)(2,1)} %get-tuple-element.24), channel_id=1, source_target_pairs={{0,2},{1,3},{2,0},{3,1},{4,6},{5,7},{6,4},{7,5},{8,10},{9,11},{10,... | collective-permute-start | bytes 884744 | tf_op jit(solution)/shard_map/ppermute | solution.py:195
  15.2 19.9 %collective-permute-start.2 = (bf16[128,1152]{1,0:T(8,128)(2,1)S(1)}, bf16[128,1152]{1,0:T(8,128)(2,1)S(1)}, u32[]{:S(2)}, u32[]{:S(2)}) collective-permute-start(bf16[128,1152]{1,0:T(8,128)(2,1)S(1)} %get-tuple-element.25), channel_id=1, source_target_pairs={{0,4},{1,5},{2,6},{3,7},{4,0},{5,1},{6,2},{7,3},{8,12},{9,13},{10,... | collective-permute-start | bytes 884744 | tf_op jit(solution)/shard_map/ppermute | solution.py:195
  18.3 16.8 %collective-permute-start.3 = (bf16[128,1152]{1,0:T(8,128)(2,1)S(1)}, bf16[128,1152]{1,0:T(8,128)(2,1)S(1)}, u32[]{:S(2)}, u32[]{:S(2)}) collective-permute-start(bf16[128,1152]{1,0:T(8,128)(2,1)S(1)} %get-tuple-element.26), channel_id=1, source_target_pairs={{0,8},{1,9},{2,10},{3,11},{4,12},{5,13},{6,14},{7,15},{8,0},{9,1},... | collective-permute-start | bytes 884744 | tf_op jit(solution)/shard_map/ppermute | solution.py:195
  36.3 21.8 %collective-permute-start.7 = (bf16[128,768]{1,0:T(8,128)(2,1)S(1)}, bf16[128,768]{1,0:T(8,128)(2,1)S(1)}, u32[]{:S(2)}, u32[]{:S(2)}) collective-permute-start(bf16[128,768]{1,0:T(8,128)(2,1)S(1)} %get-tuple-element.27.refs_0_), channel_id=1, source_target_pairs={{0,8},{1,9},{2,10},{3,11},{4,12},{5,13},{6,14},{7,15},{8,0},{9,1},... | collective-permute-start | bytes 589832 | tf_op jit(solution)/shard_map/ppermute | solution.py:195
  41.1 17.0 %collective-permute-start.6 = (bf16[128,768]{1,0:T(8,128)(2,1)S(1)}, bf16[128,768]{1,0:T(8,128)(2,1)S(1)}, u32[]{:S(2)}, u32[]{:S(2)}) collective-permute-start(bf16[128,768]{1,0:T(8,128)(2,1)S(1)} %get-tuple-element.27.refs_0_), channel_id=1, source_target_pairs={{0,4},{1,5},{2,6},{3,7},{4,0},{5,1},{6,2},{7,3},{8,12},{9,13},{10,... | collective-permute-start | bytes 589832 | tf_op jit(solution)/shard_map/ppermute | solution.py:195
  43.3 15.2 %collective-permute-start.5 = (bf16[128,768]{1,0:T(8,128)(2,1)S(1)}, bf16[128,768]{1,0:T(8,128)(2,1)S(1)}, u32[]{:S(2)}, u32[]{:S(2)}) collective-permute-start(bf16[128,768]{1,0:T(8,128)(2,1)S(1)} %get-tuple-element.27.refs_0_), channel_id=1, source_target_pairs={{0,2},{1,3},{2,0},{3,1},{4,6},{5,7},{6,4},{7,5},{8,10},{9,11},{10,... | collective-permute-start | bytes 589832 | tf_op jit(solution)/shard_map/ppermute | solution.py:195
  51.7 17.9 %collective-permute-start.4 = (bf16[128,768]{1,0:T(8,128)(2,1)S(1)}, bf16[128,768]{1,0:T(8,128)(2,1)S(1)}, u32[]{:S(2)}, u32[]{:S(2)}) collective-permute-start(bf16[128,768]{1,0:T(8,128)(2,1)S(1)} %get-tuple-element.27.refs_0_), channel_id=1, source_target_pairs={{0,1},{1,0},{2,3},{3,2},{4,5},{5,4},{6,7},{7,6},{8,9},{9,8},{10,11... | collective-permute-start | bytes 589832 | tf_op jit(solution)/shard_map/ppermute | solution.py:195
  53.6 16.0 %copy-start.3 = (bf16[128,384]{1,0:T(8,128)(2,1)S(1)}, bf16[128,384]{1,0:T(8,128)(2,1)}, u32[]{:S(2)}) copy-start(bf16[128,384]{1,0:T(8,128)(2,1)} %cot.3) | copy-start | bytes 294916
  54.7 18.4 %collective-permute-start.12 = (bf16[15,128,128]{2,1,0:T(8,128)(2,1)S(1)}, bf16[15,128,128]{2,1,0:T(8,128)(2,1)S(1)}, u32[]{:S(2)}, u32[]{:S(2)}) collective-permute-start(bf16[15,128,128]{2,1,0:T(8,128)(2,1)S(1)} %get-tuple-element.35), channel_id=1, source_target_pairs={{0,16},{16,0},{32,48},{48,32},{64,80},{80,64},{96,112},{112,96},{1... | collective-permute-start | bytes 1474568 | tf_op jit(solution)/shard_map/ppermute | solution.py:195
  70.7 3.9 %collective-permute-start.13 = (bf16[15,128,128]{2,1,0:T(8,128)(2,1)S(1)}, bf16[15,128,128]{2,1,0:T(8,128)(2,1)S(1)}, u32[]{:S(2)}, u32[]{:S(2)}) collective-permute-start(bf16[15,128,128]{2,1,0:T(8,128)(2,1)S(1)} %get-tuple-element.37), channel_id=1, source_target_pairs={{0,16},{16,0},{32,48},{48,32},{64,80},{80,64},{96,112},{112,96},{1... | collective-permute-start | bytes 1474568 | tf_op jit(solution)/shard_map/ppermute | solution.py:195
  138.0 24.4 %copy-start = (bf16[1,5,3,2,128,128]{5,4,3,2,1,0:T(8,128)(2,1)S(1)}, bf16[1,5,3,2,128,128]{5,4,3,2,1,0:T(8,128)(2,1)}, u32[]{:S(2)}) copy-start(bf16[1,5,3,2,128,128]{5,4,3,2,1,0:T(8,128)(2,1)} %param.9) | copy-start | bytes 2949124
  138.0 26.1 %collective-permute-start.14 = (bf16[16,240,128]{2,1,0:T(8,128)(2,1)S(1)}, bf16[16,240,128]{2,1,0:T(8,128)(2,1)S(1)}, u32[]{:S(2)}, u32[]{:S(2)}) collective-permute-start(bf16[16,240,128]{2,1,0:T(8,128)(2,1)S(1)} %all_to_all.11.mine), channel_id=1, source_target_pairs={{0,16},{16,0},{32,48},{48,32},{64,80},{80,64},{96,112},{112,96},{1... | collective-permute-start | bytes 2949128 | tf_op jit(solution)/shard_map/ppermute | solution.py:195
  144.6 12.8 %collective-permute-start.8 = (bf16[128,384]{1,0:T(8,128)(2,1)S(1)}, bf16[128,384]{1,0:T(8,128)(2,1)S(1)}, u32[]{:S(2)}, u32[]{:S(2)}) collective-permute-start(bf16[128,384]{1,0:T(8,128)(2,1)S(1)} %get-tuple-element.30), channel_id=1, source_target_pairs={{0,1},{1,0},{2,3},{3,2},{4,5},{5,4},{6,7},{7,6},{8,9},{9,8},{10,11... | collective-permute-start | bytes 294920 | tf_op jit(solution)/shard_map/ppermute | solution.py:195
  147.0 10.3 %collective-permute-start.9 = (bf16[128,384]{1,0:T(8,128)(2,1)S(1)}, bf16[128,384]{1,0:T(8,128)(2,1)S(1)}, u32[]{:S(2)}, u32[]{:S(2)}) collective-permute-start(bf16[128,384]{1,0:T(8,128)(2,1)S(1)} %get-tuple-element.31), channel_id=1, source_target_pairs={{0,2},{1,3},{2,0},{3,1},{4,6},{5,7},{6,4},{7,5},{8,10},{9,11},{10,... | collective-permute-start | bytes 294920 | tf_op jit(solution)/shard_map/ppermute | solution.py:195
  151.8 5.7 %collective-permute-start.10 = (bf16[128,384]{1,0:T(8,128)(2,1)S(1)}, bf16[128,384]{1,0:T(8,128)(2,1)S(1)}, u32[]{:S(2)}, u32[]{:S(2)}) collective-permute-start(bf16[128,384]{1,0:T(8,128)(2,1)S(1)} %get-tuple-element.32), channel_id=1, source_target_pairs={{0,4},{1,5},{2,6},{3,7},{4,0},{5,1},{6,2},{7,3},{8,12},{9,13},{10,... | collective-permute-start | bytes 294920 | tf_op jit(solution)/shard_map/ppermute | solution.py:195
  154.8 6.9 %collective-permute-start.11 = (bf16[128,384]{1,0:T(8,128)(2,1)S(1)}, bf16[128,384]{1,0:T(8,128)(2,1)S(1)}, u32[]{:S(2)}, u32[]{:S(2)}) collective-permute-start(bf16[128,384]{1,0:T(8,128)(2,1)S(1)} %get-tuple-element.33), channel_id=1, source_target_pairs={{0,8},{1,9},{2,10},{3,11},{4,12},{5,13},{6,14},{7,15},{8,0},{9,1},... | collective-permute-start | bytes 294920 | tf_op jit(solution)/shard_map/ppermute | solution.py:195

commit v4 on v3

--- a/solution.py
+++ b/solution.py
@@ -213,7 +213,7 @@
     groups = [[2 * i + c for i in range(chips)] for c in range(2)]
 
     def over_mp(blocks):
-        return [from_partner(blocks[b], "mp", b) for b in reversed(range(bits))][::-1]
+        return [from_partner(blocks[b], "mp", b) for b in range(bits)]
 
     def exchange(block):
         return lax.all_to_all(
@@ -278,7 +278,10 @@
     pair = call(pair_kernel, sds((chips, sum(rows), B), BF16), [VMEM] * 4, ())(*halves)
     parts = exchange(pair)
     shard = call(
-        functools.partial(shard_kernel, scale), sds((chips, sum(rows), B), BF16), [VMEM], ()
+        functools.partial(shard_kernel, scale),
+        sds((chips, sum(rows), B), BF16),
+        [VMEM],
+        (),
     )(parts)
     mine = exchange(shard)
     other = from_partner(mine, "dp", 0)

time: 167 us -> 167 us (level)
  no operation moved by 1% of the time
where the time goes in v4:
time: 167 us; the launch traced here: 165 us
  blocking collectives  63 us (38%)
  starting transfers between devices  59.2 us (35%)
  waiting for transfers between devices  29.6 us (18%)
  Pallas kernels  11.6 us (7%)
    all_to_all x2, blocking collectives, exchange(): lax.all_to_all(block, 'dp', split_axis=0, concat_axis=0, axis_index_group...  63 us
    ppermute x15, starting transfers between devices, from_partner(): return lax.ppermute(block, axis, [(i, i ^ 1 << bit) for i in range(count)])  59.2 us
    ppermute x15, waiting for transfers between devices, from_partner(): return lax.ppermute(block, axis, [(i, i ^ 1 << bit) for i in range(count)])  29.6 us
    pallas_call x10, Pallas kernels, invoke(): return run(*placed)  11.6 us
  transfers between devices with their start and end apart: 15, of which 6 were waited for; matrix products, arithmetic and copies ran while one was open for 0% of the time, Pallas kernels for 4%

profile of v4, /device:TPU:1, one launch (start us, length us, event | category | flops | bytes accessed | tf_op | source)
XLA Modules:
  0.0 165.4 jit_solution(10944289290545550677)
XLA Ops:
  0.6 0.9 copy.11
  1.6 2.7 %shard_map.93 = (f32[128,768]{1,0:T(8,128)S(1)}, bf16[128,1152]{1,0:T(8,128)(2,1)}, bf16[128,1152]{1,0:T(8,128)(2,1)}, bf16[128,1152]{1,0:T(8,128)(2,1)S(1)}, bf16[128,1152]{1,0:T(8,128)(2,1)S(1)}) custom-call(s32[30]{0:T(128)S(1)} %reshape.41.pick, bf16[128,384]{1,0:T(8,128)(2,1)} %cot.3, bf16[30,128,128]{2,1,0:T(8,128)(2,1)} %bitcast.9, ...), custom_call_target="tpu_custom_call" | custom-call | tf_op jit(solution)/shard_map/pallas_call | solution.py:48
  4.4 5.2 %collective-permute-start = (bf16[128,1152]{1,0:T(8,128)(2,1)}, bf16[128,1152]{1,0:T(8,128)(2,1)S(1)}, u32[]{:S(2)}, u32[]{:S(2)}) collective-permute-start(bf16[128,1152]{1,0:T(8,128)(2,1)} %get-tuple-element.23), channel_id=1, source_target_pairs={{0,1},{1,0},{2,3},{3,2},{4,5},{5,4},{6,7},{7,6},{8,9},{9,8},{10,11... | collective-permute-start | bytes 884744 | tf_op jit(solution)/shard_map/ppermute | solution.py:195
  9.5 5.6 %collective-permute-start.1 = (bf16[128,1152]{1,0:T(8,128)(2,1)}, bf16[128,1152]{1,0:T(8,128)(2,1)S(1)}, u32[]{:S(2)}, u32[]{:S(2)}) collective-permute-start(bf16[128,1152]{1,0:T(8,128)(2,1)} %get-tuple-element.24), channel_id=1, source_target_pairs={{0,2},{1,3},{2,0},{3,1},{4,6},{5,7},{6,4},{7,5},{8,10},{9,11},{10,... | collective-permute-start | bytes 884744 | tf_op jit(solution)/shard_map/ppermute | solution.py:195
  15.2 3.1 %collective-permute-start.2 = (bf16[128,1152]{1,0:T(8,128)(2,1)S(1)}, bf16[128,1152]{1,0:T(8,128)(2,1)S(1)}, u32[]{:S(2)}, u32[]{:S(2)}) collective-permute-start(bf16[128,1152]{1,0:T(8,128)(2,1)S(1)} %get-tuple-element.25), channel_id=1, source_target_pairs={{0,4},{1,5},{2,6},{3,7},{4,0},{5,1},{6,2},{7,3},{8,12},{9,13},{10,... | collective-permute-start | bytes 884744 | tf_op jit(solution)/shard_map/ppermute | solution.py:195
  18.3 4.4 %collective-permute-start.3 = (bf16[128,1152]{1,0:T(8,128)(2,1)S(1)}, bf16[128,1152]{1,0:T(8,128)(2,1)S(1)}, u32[]{:S(2)}, u32[]{:S(2)}) collective-permute-start(bf16[128,1152]{1,0:T(8,128)(2,1)S(1)} %get-tuple-element.26), channel_id=1, source_target_pairs={{0,8},{1,9},{2,10},{3,11},{4,12},{5,13},{6,14},{7,15},{8,0},{9,1},... | collective-permute-start | bytes 884744 | tf_op jit(solution)/shard_map/ppermute | solution.py:195
  22.8 12.3 %collective-permute-done.refs_0_.refs_1_ = bf16[128,1152]{1,0:T(8,128)(2,1)S(1)} collective-permute-done((bf16[128,1152]{1,0:T(8,128)(2,1)}, bf16[128,1152]{1,0:T(8,128)(2,1)S(1)}, u32[]{:S(2)}, u32[]{:S(2)}) %collective-permute-start) | collective-permute-done | bytes 294944 | tf_op jit(solution)/shard_map/ppermute | solution.py:195
  35.1 1.2 shard_map.94
  36.3 4.7 %collective-permute-start.7 = (bf16[128,768]{1,0:T(8,128)(2,1)S(1)}, bf16[128,768]{1,0:T(8,128)(2,1)S(1)}, u32[]{:S(2)}, u32[]{:S(2)}) collective-permute-start(bf16[128,768]{1,0:T(8,128)(2,1)S(1)} %get-tuple-element.27.refs_0_), channel_id=1, source_target_pairs={{0,8},{1,9},{2,10},{3,11},{4,12},{5,13},{6,14},{7,15},{8,0},{9,1},... | collective-permute-start | bytes 589832 | tf_op jit(solution)/shard_map/ppermute | solution.py:195
  41.1 2.2 %collective-permute-start.6 = (bf16[128,768]{1,0:T(8,128)(2,1)S(1)}, bf16[128,768]{1,0:T(8,128)(2,1)S(1)}, u32[]{:S(2)}, u32[]{:S(2)}) collective-permute-start(bf16[128,768]{1,0:T(8,128)(2,1)S(1)} %get-tuple-element.27.refs_0_), channel_id=1, source_target_pairs={{0,4},{1,5},{2,6},{3,7},{4,0},{5,1},{6,2},{7,3},{8,12},{9,13},{10,... | collective-permute-start | bytes 589832 | tf_op jit(solution)/shard_map/ppermute | solution.py:195
  43.3 8.4 %collective-permute-start.5 = (bf16[128,768]{1,0:T(8,128)(2,1)S(1)}, bf16[128,768]{1,0:T(8,128)(2,1)S(1)}, u32[]{:S(2)}, u32[]{:S(2)}) collective-permute-start(bf16[128,768]{1,0:T(8,128)(2,1)S(1)} %get-tuple-element.27.refs_0_), channel_id=1, source_target_pairs={{0,2},{1,3},{2,0},{3,1},{4,6},{5,7},{6,4},{7,5},{8,10},{9,11},{10,... | collective-permute-start | bytes 589832 | tf_op jit(solution)/shard_map/ppermute | solution.py:195
  51.7 1.9 %collective-permute-start.4 = (bf16[128,768]{1,0:T(8,128)(2,1)S(1)}, bf16[128,768]{1,0:T(8,128)(2,1)S(1)}, u32[]{:S(2)}, u32[]{:S(2)}) collective-permute-start(bf16[128,768]{1,0:T(8,128)(2,1)S(1)} %get-tuple-element.27.refs_0_), channel_id=1, source_target_pairs={{0,1},{1,0},{2,3},{3,2},{4,5},{5,4},{6,7},{7,6},{8,9},{9,8},{10,11... | collective-permute-start | bytes 589832 | tf_op jit(solution)/shard_map/ppermute | solution.py:195
  53.6 1.1 shard_map.98
  54.7 3.4 %collective-permute-start.12 = (bf16[15,128,128]{2,1,0:T(8,128)(2,1)S(1)}, bf16[15,128,128]{2,1,0:T(8,128)(2,1)S(1)}, u32[]{:S(2)}, u32[]{:S(2)}) collective-permute-start(bf16[15,128,128]{2,1,0:T(8,128)(2,1)S(1)} %get-tuple-element.35), channel_id=1, source_target_pairs={{0,16},{16,0},{32,48},{48,32},{64,80},{80,64},{96,112},{112,96},{1... | collective-permute-start | bytes 1474568 | tf_op jit(solution)/shard_map/ppermute | solution.py:195
  58.1 0.4 collective-permute-done.5.refs_2_
  58.5 11.1 %collective-permute-done.4.refs_1_ = bf16[128,768]{1,0:T(8,128)(2,1)S(1)} collective-permute-done((bf16[128,768]{1,0:T(8,128)(2,1)S(1)}, bf16[128,768]{1,0:T(8,128)(2,1)S(1)}, u32[]{:S(2)}, u32[]{:S(2)}) %collective-permute-start.4) | collective-permute-done | bytes 196640 | tf_op jit(solution)/shard_map/ppermute | solution.py:195
  69.6 1.1 shard_map.99
  70.7 2.4 %collective-permute-start.13 = (bf16[15,128,128]{2,1,0:T(8,128)(2,1)S(1)}, bf16[15,128,128]{2,1,0:T(8,128)(2,1)S(1)}, u32[]{:S(2)}, u32[]{:S(2)}) collective-permute-start(bf16[15,128,128]{2,1,0:T(8,128)(2,1)S(1)} %get-tuple-element.37), channel_id=1, source_target_pairs={{0,16},{16,0},{32,48},{48,32},{64,80},{80,64},{96,112},{112,96},{1... | collective-permute-start | bytes 1474568 | tf_op jit(solution)/shard_map/ppermute | solution.py:195
  73.1 1.5 collective-permute-done.13
  74.6 0.2 shard_map.100
  74.8 32.6 %all_to_all.10.parts = bf16[16,240,128]{2,1,0:T(8,128)(2,1)S(1)} all-to-all(bf16[16,240,128]{2,1,0:T(8,128)(2,1)S(1)} %shard_map.100), channel_id=1, replica_groups={{0,32,64,96,128,160,192,224,256,288,320,352,384,416,448,480},{16,48,80,..., dimensions={0} | all-to-all | bytes 1966080 | tf_op jit(solution)/shard_map/all_to_all | solution.py:219
  107.5 30.4 %all_to_all.11.mine = bf16[16,240,128]{2,1,0:T(8,128)(2,1)S(1)} all-to-all(bf16[16,240,128]{2,1,0:T(8,128)(2,1)S(1)} %shard_map.101), channel_id=1, replica_groups={{0,32,64,96,128,160,192,224,256,288,320,352,384,416,448,480},{16,48,80,..., dimensions={0} | all-to-all | bytes 1966080 | tf_op jit(solution)/shard_map/all_to_all | solution.py:219
  138.0 5.2 %collective-permute-start.14 = (bf16[16,240,128]{2,1,0:T(8,128)(2,1)S(1)}, bf16[16,240,128]{2,1,0:T(8,128)(2,1)S(1)}, u32[]{:S(2)}, u32[]{:S(2)}) collective-permute-start(bf16[16,240,128]{2,1,0:T(8,128)(2,1)S(1)} %all_to_all.11.mine), channel_id=1, source_target_pairs={{0,16},{16,0},{32,48},{48,32},{64,80},{80,64},{96,112},{112,96},{1... | collective-permute-start | bytes 2949128 | tf_op jit(solution)/shard_map/ppermute | solution.py:195
  143.2 1.4 shard_map.96
  144.6 2.5 %collective-permute-start.8 = (bf16[128,384]{1,0:T(8,128)(2,1)S(1)}, bf16[128,384]{1,0:T(8,128)(2,1)S(1)}, u32[]{:S(2)}, u32[]{:S(2)}) collective-permute-start(bf16[128,384]{1,0:T(8,128)(2,1)S(1)} %get-tuple-element.30), channel_id=1, source_target_pairs={{0,1},{1,0},{2,3},{3,2},{4,5},{5,4},{6,7},{7,6},{8,9},{9,8},{10,11... | collective-permute-start | bytes 294920 | tf_op jit(solution)/shard_map/ppermute | solution.py:195
  147.0 4.7 %collective-permute-start.9 = (bf16[128,384]{1,0:T(8,128)(2,1)S(1)}, bf16[128,384]{1,0:T(8,128)(2,1)S(1)}, u32[]{:S(2)}, u32[]{:S(2)}) collective-permute-start(bf16[128,384]{1,0:T(8,128)(2,1)S(1)} %get-tuple-element.31), channel_id=1, source_target_pairs={{0,2},{1,3},{2,0},{3,1},{4,6},{5,7},{6,4},{7,5},{8,10},{9,11},{10,... | collective-permute-start | bytes 294920 | tf_op jit(solution)/shard_map/ppermute | solution.py:195
  151.8 3.1 %collective-permute-start.10 = (bf16[128,384]{1,0:T(8,128)(2,1)S(1)}, bf16[128,384]{1,0:T(8,128)(2,1)S(1)}, u32[]{:S(2)}, u32[]{:S(2)}) collective-permute-start(bf16[128,384]{1,0:T(8,128)(2,1)S(1)} %get-tuple-element.32), channel_id=1, source_target_pairs={{0,4},{1,5},{2,6},{3,7},{4,0},{5,1},{6,2},{7,3},{8,12},{9,13},{10,... | collective-permute-start | bytes 294920 | tf_op jit(solution)/shard_map/ppermute | solution.py:195
  154.8 2.5 %collective-permute-start.11 = (bf16[128,384]{1,0:T(8,128)(2,1)S(1)}, bf16[128,384]{1,0:T(8,128)(2,1)S(1)}, u32[]{:S(2)}, u32[]{:S(2)}) collective-permute-start(bf16[128,384]{1,0:T(8,128)(2,1)S(1)} %get-tuple-element.33), channel_id=1, source_target_pairs={{0,8},{1,9},{2,10},{3,11},{4,12},{5,13},{6,14},{7,15},{8,0},{9,1},... | collective-permute-start | bytes 294920 | tf_op jit(solution)/shard_map/ppermute | solution.py:195
  157.4 4.3 %collective-permute-done.11.refs_3_ = bf16[128,384]{1,0:T(8,128)(2,1)S(1)} collective-permute-done((bf16[128,384]{1,0:T(8,128)(2,1)S(1)}, bf16[128,384]{1,0:T(8,128)(2,1)S(1)}, u32[]{:S(2)}, u32[]{:S(2)}) %collective-permute-start.11) | collective-permute-done | bytes 98336 | tf_op jit(solution)/shard_map/ppermute | solution.py:195
  161.7 0.7 shard_map.97
  162.4 1.6 shard_map.95
  164.0 1.4 shard_map.102
  (24 shorter events, 0.5 us)
Async XLA Ops:
  0.6 34.5 %copy-start.1 = (bf16[1,5,6,128,128]{4,3,2,1,0:T(8,128)(2,1)S(1)}, bf16[1,5,6,128,128]{4,3,2,1,0:T(8,128)(2,1)}, u32[]{:S(2)}) copy-start(bf16[1,5,6,128,128]{4,3,2,1,0:T(8,128)(2,1)} %param.7) | copy-start | bytes 2949124
  1.6 33.5 %copy-start.2 = (bf16[128,384]{1,0:T(8,128)(2,1)S(1)}, bf16[128,384]{1,0:T(8,128)(2,1)}, u32[]{:S(2)}) copy-start(bf16[128,384]{1,0:T(8,128)(2,1)} %refs_0_.1) | copy-start | bytes 294916
  4.4 18.3 %copy-start.4 = (s32[1,5,6]{2,0,1:T(1,128)S(1)}, s32[1,5,6]{2,0,1:T(1,128)}, u32[]{:S(2)}) copy-start(s32[1,5,6]{2,0,1:T(1,128)} %param.8) | copy-start | bytes 364
  4.4 30.7 %collective-permute-start = (bf16[128,1152]{1,0:T(8,128)(2,1)}, bf16[128,1152]{1,0:T(8,128)(2,1)S(1)}, u32[]{:S(2)}, u32[]{:S(2)}) collective-permute-start(bf16[128,1152]{1,0:T(8,128)(2,1)} %get-tuple-element.23), channel_id=1, source_target_pairs={{0,1},{1,0},{2,3},{3,2},{4,5},{5,4},{6,7},{7,6},{8,9},{9,8},{10,11... | collective-permute-start | bytes 884744 | tf_op jit(solution)/shard_map/ppermute | solution.py:195
  9.5 25.6 %collective-permute-start.1 = (bf16[128,1152]{1,0:T(8,128)(2,1)}, bf16[128,1152]{1,0:T(8,128)(2,1)S(1)}, u32[]{:S(2)}, u32[]{:S(2)}) collective-permute-start(bf16[128,1152]{1,0:T(8,128)(2,1)} %get-tuple-element.24), channel_id=1, source_target_pairs={{0,2},{1,3},{2,0},{3,1},{4,6},{5,7},{6,4},{7,5},{8,10},{9,11},{10,... | collective-permute-start | bytes 884744 | tf_op jit(solution)/shard_map/ppermute | solution.py:195
  15.2 19.9 %collective-permute-start.2 = (bf16[128,1152]{1,0:T(8,128)(2,1)S(1)}, bf16[128,1152]{1,0:T(8,128)(2,1)S(1)}, u32[]{:S(2)}, u32[]{:S(2)}) collective-permute-start(bf16[128,1152]{1,0:T(8,128)(2,1)S(1)} %get-tuple-element.25), channel_id=1, source_target_pairs={{0,4},{1,5},{2,6},{3,7},{4,0},{5,1},{6,2},{7,3},{8,12},{9,13},{10,... | collective-permute-start | bytes 884744 | tf_op jit(solution)/shard_map/ppermute | solution.py:195
  18.3 16.8 %collective-permute-start.3 = (bf16[128,1152]{1,0:T(8,128)(2,1)S(1)}, bf16[128,1152]{1,0:T(8,128)(2,1)S(1)}, u32[]{:S(2)}, u32[]{:S(2)}) collective-permute-start(bf16[128,1152]{1,0:T(8,128)(2,1)S(1)} %get-tuple-element.26), channel_id=1, source_target_pairs={{0,8},{1,9},{2,10},{3,11},{4,12},{5,13},{6,14},{7,15},{8,0},{9,1},... | collective-permute-start | bytes 884744 | tf_op jit(solution)/shard_map/ppermute | solution.py:195
  36.3 21.8 %collective-permute-start.7 = (bf16[128,768]{1,0:T(8,128)(2,1)S(1)}, bf16[128,768]{1,0:T(8,128)(2,1)S(1)}, u32[]{:S(2)}, u32[]{:S(2)}) collective-permute-start(bf16[128,768]{1,0:T(8,128)(2,1)S(1)} %get-tuple-element.27.refs_0_), channel_id=1, source_target_pairs={{0,8},{1,9},{2,10},{3,11},{4,12},{5,13},{6,14},{7,15},{8,0},{9,1},... | collective-permute-start | bytes 589832 | tf_op jit(solution)/shard_map/ppermute | solution.py:195
  41.1 17.0 %collective-permute-start.6 = (bf16[128,768]{1,0:T(8,128)(2,1)S(1)}, bf16[128,768]{1,0:T(8,128)(2,1)S(1)}, u32[]{:S(2)}, u32[]{:S(2)}) collective-permute-start(bf16[128,768]{1,0:T(8,128)(2,1)S(1)} %get-tuple-element.27.refs_0_), channel_id=1, source_target_pairs={{0,4},{1,5},{2,6},{3,7},{4,0},{5,1},{6,2},{7,3},{8,12},{9,13},{10,... | collective-permute-start | bytes 589832 | tf_op jit(solution)/shard_map/ppermute | solution.py:195
  43.3 15.2 %collective-permute-start.5 = (bf16[128,768]{1,0:T(8,128)(2,1)S(1)}, bf16[128,768]{1,0:T(8,128)(2,1)S(1)}, u32[]{:S(2)}, u32[]{:S(2)}) collective-permute-start(bf16[128,768]{1,0:T(8,128)(2,1)S(1)} %get-tuple-element.27.refs_0_), channel_id=1, source_target_pairs={{0,2},{1,3},{2,0},{3,1},{4,6},{5,7},{6,4},{7,5},{8,10},{9,11},{10,... | collective-permute-start | bytes 589832 | tf_op jit(solution)/shard_map/ppermute | solution.py:195
  51.7 17.9 %collective-permute-start.4 = (bf16[128,768]{1,0:T(8,128)(2,1)S(1)}, bf16[128,768]{1,0:T(8,128)(2,1)S(1)}, u32[]{:S(2)}, u32[]{:S(2)}) collective-permute-start(bf16[128,768]{1,0:T(8,128)(2,1)S(1)} %get-tuple-element.27.refs_0_), channel_id=1, source_target_pairs={{0,1},{1,0},{2,3},{3,2},{4,5},{5,4},{6,7},{7,6},{8,9},{9,8},{10,11... | collective-permute-start | bytes 589832 | tf_op jit(solution)/shard_map/ppermute | solution.py:195
  53.6 16.0 %copy-start.3 = (bf16[128,384]{1,0:T(8,128)(2,1)S(1)}, bf16[128,384]{1,0:T(8,128)(2,1)}, u32[]{:S(2)}) copy-start(bf16[128,384]{1,0:T(8,128)(2,1)} %cot.3) | copy-start | bytes 294916
  54.7 18.4 %collective-permute-start.12 = (bf16[15,128,128]{2,1,0:T(8,128)(2,1)S(1)}, bf16[15,128,128]{2,1,0:T(8,128)(2,1)S(1)}, u32[]{:S(2)}, u32[]{:S(2)}) collective-permute-start(bf16[15,128,128]{2,1,0:T(8,128)(2,1)S(1)} %get-tuple-element.35), channel_id=1, source_target_pairs={{0,16},{16,0},{32,48},{48,32},{64,80},{80,64},{96,112},{112,96},{1... | collective-permute-start | bytes 1474568 | tf_op jit(solution)/shard_map/ppermute | solution.py:195
  70.7 3.9 %collective-permute-start.13 = (bf16[15,128,128]{2,1,0:T(8,128)(2,1)S(1)}, bf16[15,128,128]{2,1,0:T(8,128)(2,1)S(1)}, u32[]{:S(2)}, u32[]{:S(2)}) collective-permute-start(bf16[15,128,128]{2,1,0:T(8,128)(2,1)S(1)} %get-tuple-element.37), channel_id=1, source_target_pairs={{0,16},{16,0},{32,48},{48,32},{64,80},{80,64},{96,112},{112,96},{1... | collective-permute-start | bytes 1474568 | tf_op jit(solution)/shard_map/ppermute | solution.py:195
  138.0 24.4 %copy-start = (bf16[1,5,3,2,128,128]{5,4,3,2,1,0:T(8,128)(2,1)S(1)}, bf16[1,5,3,2,128,128]{5,4,3,2,1,0:T(8,128)(2,1)}, u32[]{:S(2)}) copy-start(bf16[1,5,3,2,128,128]{5,4,3,2,1,0:T(8,128)(2,1)} %param.9) | copy-start | bytes 2949124
  138.0 26.1 %collective-permute-start.14 = (bf16[16,240,128]{2,1,0:T(8,128)(2,1)S(1)}, bf16[16,240,128]{2,1,0:T(8,128)(2,1)S(1)}, u32[]{:S(2)}, u32[]{:S(2)}) collective-permute-start(bf16[16,240,128]{2,1,0:T(8,128)(2,1)S(1)} %all_to_all.11.mine), channel_id=1, source_target_pairs={{0,16},{16,0},{32,48},{48,32},{64,80},{80,64},{96,112},{112,96},{1... | collective-permute-start | bytes 2949128 | tf_op jit(solution)/shard_map/ppermute | solution.py:195
  144.6 12.8 %collective-permute-start.8 = (bf16[128,384]{1,0:T(8,128)(2,1)S(1)}, bf16[128,384]{1,0:T(8,128)(2,1)S(1)}, u32[]{:S(2)}, u32[]{:S(2)}) collective-permute-start(bf16[128,384]{1,0:T(8,128)(2,1)S(1)} %get-tuple-element.30), channel_id=1, source_target_pairs={{0,1},{1,0},{2,3},{3,2},{4,5},{5,4},{6,7},{7,6},{8,9},{9,8},{10,11... | collective-permute-start | bytes 294920 | tf_op jit(solution)/shard_map/ppermute | solution.py:195
  147.0 10.3 %collective-permute-start.9 = (bf16[128,384]{1,0:T(8,128)(2,1)S(1)}, bf16[128,384]{1,0:T(8,128)(2,1)S(1)}, u32[]{:S(2)}, u32[]{:S(2)}) collective-permute-start(bf16[128,384]{1,0:T(8,128)(2,1)S(1)} %get-tuple-element.31), channel_id=1, source_target_pairs={{0,2},{1,3},{2,0},{3,1},{4,6},{5,7},{6,4},{7,5},{8,10},{9,11},{10,... | collective-permute-start | bytes 294920 | tf_op jit(solution)/shard_map/ppermute | solution.py:195
  151.8 5.7 %collective-permute-start.10 = (bf16[128,384]{1,0:T(8,128)(2,1)S(1)}, bf16[128,384]{1,0:T(8,128)(2,1)S(1)}, u32[]{:S(2)}, u32[]{:S(2)}) collective-permute-start(bf16[128,384]{1,0:T(8,128)(2,1)S(1)} %get-tuple-element.32), channel_id=1, source_target_pairs={{0,4},{1,5},{2,6},{3,7},{4,0},{5,1},{6,2},{7,3},{8,12},{9,13},{10,... | collective-permute-start | bytes 294920 | tf_op jit(solution)/shard_map/ppermute | solution.py:195
  154.8 6.9 %collective-permute-start.11 = (bf16[128,384]{1,0:T(8,128)(2,1)S(1)}, bf16[128,384]{1,0:T(8,128)(2,1)S(1)}, u32[]{:S(2)}, u32[]{:S(2)}) collective-permute-start(bf16[128,384]{1,0:T(8,128)(2,1)S(1)} %get-tuple-element.33), channel_id=1, source_target_pairs={{0,8},{1,9},{2,10},{3,11},{4,12},{5,13},{6,14},{7,15},{8,0},{9,1},... | collective-permute-start | bytes 294920 | tf_op jit(solution)/shard_map/ppermute | solution.py:195

commit v5 on v4

--- a/solution.py
+++ b/solution.py
@@ -73,7 +73,7 @@
             both = jnp.concatenate([w[(lvl * db + o) * kd + k] for k in range(kd)], axis=0)
             term = dot_nt(cot[:, o * B : (o + 1) * B], both)
             for k in range(kd):
-                spot = pick[(lvl * db + o) * kd + k]
+                spot = pick[o, k, lvl]
                 acc[spot] += term[:, k * B : (k + 1) * B]
         for h in range(hb):
             if lvl == 0:
@@ -89,7 +89,7 @@
     for o in range(hb):
         here = slice(o * B, (o + 1) * B)
         lhs = jnp.concatenate(
-            [xs[lvl][:, lanes(pick[lvl * hb + o])] for lvl in range(levels)], axis=1
+            [xs[lvl][:, lanes(pick[lvl, 0, o])] for lvl in range(levels)], axis=1
         )
         rhs = jnp.concatenate([w[lvl * hb + o] for lvl in range(levels)], axis=0)
         v = jnp.dot(lhs, rhs, preferred_element_type=F32)
@@ -110,7 +110,7 @@
     for lvl in range(levels):
         acc[...] = jnp.zeros_like(acc)
         for o in range(hb):
-            spot = pick[lvl * hb + o]
+            spot = pick[lvl, 0, o]
             acc[spot] += dot_nt(hg[:, o * B : (o + 1) * B], w[lvl * hb + o])
         for d in range(db):
             outs[lvl][:, d * B : (d + 1) * B] = acc[d].astype(outs[lvl].dtype)
@@ -128,7 +128,7 @@
     for o in range(hb):
         right = hg[:, o * B : (o + 1) * B]
         for lvl in range(levels):
-            left = xs[lvl][:, lanes(pick[lvl * hb + o])]
+            left = xs[lvl][:, lanes(pick[lvl, 0, o])]
             scr[lvl * hb + o] = dot_tn(left, right)
     split(core[0], scr, keep, send)
 
@@ -141,17 +141,12 @@
         for lvl in range(levels):
             for k in range(kd):
                 i = (lvl * db + o) * kd + k
-                scr[i] = dot_tn(acts[lvl][:, lanes(pick[i])], right)
+                scr[i] = dot_tn(acts[lvl][:, lanes(pick[o, k, lvl])], right)
     split(core[0], scr, keep, send)
 
 
-def pair_kernel(*refs):
-    out = refs[-1]
-    at = 0
-    for keep, got in zip(refs[0:-1:2], refs[1:-1:2]):
-        rows = keep.shape[1]
-        out[:, at : at + rows, :] = (keep[...] + got[...].astype(F32)).astype(BF16)
-        at += rows
+def pair_kernel(keep, got, out):
+    out[...] = (keep[...] + got[...].astype(F32)).astype(BF16)
 
 
 def dx_kernel(own, *refs):
@@ -164,21 +159,26 @@
 def out_kernel(levels, db, kd, pick, w, *refs):
     acts, out = refs[:levels], refs[levels]
     for o in range(db):
-        spots = [(lvl * db + o) * kd + k for lvl in range(levels) for k in range(kd)]
+        slots = [(lvl, k) for lvl in range(levels) for k in range(kd)]
         lhs = jnp.concatenate(
-            [acts[i // (db * kd)][:, lanes(pick[i])] for i in spots], axis=1
+            [acts[lvl][:, lanes(pick[o, k, lvl])] for lvl, k in slots], axis=1
         )
-        rhs = jnp.concatenate([w[i] for i in spots], axis=0)
+        rhs = jnp.concatenate([w[(lvl * db + o) * kd + k] for lvl, k in slots], axis=0)
         out[:, o * B : (o + 1) * B] = jnp.dot(lhs, rhs, preferred_element_type=F32).astype(BF16)
 
 
-def shard_kernel(scale, parts, out):
-    total = parts[0].astype(F32)
-    for i in range(1, parts.shape[0]):
-        total = total + parts[i].astype(F32)
-    total = (total * scale).astype(BF16)
-    for i in range(out.shape[0]):
-        out[i] = total
+def shard_kernel(scale, *refs):
+    out = refs[-1]
+    at = 0
+    for parts in refs[:-1]:
+        total = parts[0].astype(F32)
+        for i in range(1, parts.shape[0]):
+            total = total + parts[i].astype(F32)
+        total = (total * scale).astype(BF16)
+        rows = parts.shape[1]
+        for i in range(out.shape[0]):
+            out[i, at : at + rows, :] = total
+        at += rows
 
 
 def join_kernel(core, mine, other, *outs):
@@ -207,8 +207,8 @@
     n_up, n_down = levels * hb, levels * db * kd
     up_w = up_weight.reshape(n_up, B, B)
     down_w = down_weight.reshape(n_down, B, B)
-    up_ids = up_pick.reshape(n_up)
-    down_ids = down_pick.reshape(n_down)
+    up_ids = up_pick.transpose(1, 0, 2)
+    down_ids = down_pick[0].transpose(1, 2, 0)
     core = lax.rem(lax.axis_index("dp"), 2).reshape(1)
     groups = [[2 * i + c for i in range(chips)] for c in range(2)]
 
@@ -219,6 +219,13 @@
         return lax.all_to_all(
             block, "dp", split_axis=0, concat_axis=0, axis_index_groups=groups, tiled=True
         )
+
+    def partials(keep, send):
+        got = from_partner(send, "dp", 0)
+        pair = call(
+            pair_kernel, sds((chips, keep.size // (chips * B), B), BF16), [VMEM] * 2, ()
+        )(keep.reshape(chips, -1, B), got.reshape(chips, -1, B))
+        return exchange(pair)
 
     wide, deep = db * B, hb * B
     own, *first = call(
@@ -256,7 +263,7 @@
         [SMEM, SMEM, VMEM] + [VMEM] * levels,
         [pltpu.VMEM((n_up, B, B), F32)],
     )(up_ids, core, hg, inputs, *got)
-    up_got = from_partner(up_send, "dp", 0)
+    up_parts = partials(up_keep, up_send)
 
     down_keep, down_send = call(
         functools.partial(down_kernel, levels, db, kd),
@@ -264,7 +271,7 @@
         [SMEM, SMEM, VMEM] + [VMEM] * levels,
         [pltpu.VMEM((n_down, B, B), F32)],
     )(down_ids, core, cotangent, *acts)
-    down_got = from_partner(down_send, "dp", 0)
+    down_parts = partials(down_keep, down_send)
 
     output = call(
         functools.partial(out_kernel, levels, db, kd),
@@ -273,16 +280,13 @@
         (),
     )(down_ids, down_w, *acts)
 
-    halves = [a.reshape(chips, -1, B) for a in (up_keep, up_got, down_keep, down_got)]
-    rows = [halves[0].shape[1], halves[2].shape[1]]
-    pair = call(pair_kernel, sds((chips, sum(rows), B), BF16), [VMEM] * 4, ())(*halves)
-    parts = exchange(pair)
+    rows = [up_parts.shape[1], down_parts.shape[1]]
     shard = call(
         functools.partial(shard_kernel, scale),
         sds((chips, sum(rows), B), BF16),
-        [VMEM],
+        [VMEM] * 2,
         (),
-    )(parts)
+    )(up_parts, down_parts)
     mine = exchange(shard)
     other = from_partner(mine, "dp", 0)
     up_out, down_out = call(

time: 167 us -> 169 us (1.012)
  blocking collectives: 63 us -> 48.7 us
  starting transfers between devices: 59.2 us -> 68.9 us
  waiting for transfers between devices: 29.6 us -> 36.6 us
    all_to_all x2, blocking collectives: 63 us -> 48.7 us  [exchange(): lax.all_to_all(block, 'dp', split_axis=0, concat_axis=0, axis_index_group...]
    all_to_all x0 -> x1, starting transfers between devices: none -> 10.5 us  [exchange(): lax.all_to_all(block, 'dp', split_axis=0, concat_axis=0, axis_index_group...]
    ppermute x15, waiting for transfers between devices: 29.6 us -> 36.6 us  [from_partner(): return lax.ppermute(block, axis, [(i, i ^ 1 << bit) for i in range(count)])]
    pallas_call x10 -> x11, Pallas kernels: 11.6 us -> 12.6 us  [invoke(): return run(*placed)]
  transfers between devices with their start and end apart: 15 -> 16, of which waited for: 6 -> 7; matrix products, arithmetic and copies ran while one was open for 0% -> 0% of each run, Pallas kernels for 4% -> 3%
where the time goes in v5:
time: 169 us; the launch traced here: 168 us
  starting transfers between devices  68.9 us (41%)
  blocking collectives  48.7 us (29%)
  waiting for transfers between devices  36.6 us (22%)
  Pallas kernels  12.6 us (7%)
    ppermute x15, starting transfers between devices, from_partner(): return lax.ppermute(block, axis, [(i, i ^ 1 << bit) for i in range(count)])  58.4 us
    all_to_all x2, blocking collectives, exchange(): lax.all_to_all(block, 'dp', split_axis=0, concat_axis=0, axis_index_group...  48.7 us
    ppermute x15, waiting for transfers between devices, from_partner(): return lax.ppermute(block, axis, [(i, i ^ 1 << bit) for i in range(count)])  36.6 us
    pallas_call x11, Pallas kernels, invoke(): return run(*placed)  12.6 us
    all_to_all x1, starting transfers between devices, exchange(): lax.all_to_all(block, 'dp', split_axis=0, concat_axis=0, axis_index_group...  10.5 us
  transfers between devices with their start and end apart: 16, of which 7 were waited for; matrix products, arithmetic and copies ran while one was open for 0% of the time, Pallas kernels for 3%

profile of v5, /device:TPU:1, one launch (start us, length us, event | category | flops | bytes accessed | tf_op | source)
XLA Modules:
  0.0 168.4 jit_solution(5935593394833184687)
XLA Ops:
  1.3 2.7 %shard_map.93 = (f32[128,768]{1,0:T(8,128)S(1)}, bf16[128,1152]{1,0:T(8,128)(2,1)}, bf16[128,1152]{1,0:T(8,128)(2,1)}, bf16[128,1152]{1,0:T(8,128)(2,1)S(1)}, bf16[128,1152]{1,0:T(8,128)(2,1)S(1)}) custom-call(s32[3,2,5]{2,1,0:T(2,128)S(1)} %bitcast.21, bf16[128,384]{1,0:T(8,128)(2,1)} %cot.3, bf16[30,128,128]{2,1,0:T(8,128)(2,1)} %bitcast.15, ...), custom_call_target="tpu_custom_call" | custom-call | tf_op jit(solution)/shard_map/pallas_call | solution.py:48
  4.1 5.0 %collective-permute-start = (bf16[128,1152]{1,0:T(8,128)(2,1)}, bf16[128,1152]{1,0:T(8,128)(2,1)S(1)}, u32[]{:S(2)}, u32[]{:S(2)}) collective-permute-start(bf16[128,1152]{1,0:T(8,128)(2,1)} %get-tuple-element.23), channel_id=1, source_target_pairs={{0,1},{1,0},{2,3},{3,2},{4,5},{5,4},{6,7},{7,6},{8,9},{9,8},{10,11... | collective-permute-start | bytes 884744 | tf_op jit(solution)/shard_map/ppermute | solution.py:195
  9.1 5.6 %collective-permute-start.1 = (bf16[128,1152]{1,0:T(8,128)(2,1)}, bf16[128,1152]{1,0:T(8,128)(2,1)S(1)}, u32[]{:S(2)}, u32[]{:S(2)}) collective-permute-start(bf16[128,1152]{1,0:T(8,128)(2,1)} %get-tuple-element.24), channel_id=1, source_target_pairs={{0,2},{1,3},{2,0},{3,1},{4,6},{5,7},{6,4},{7,5},{8,10},{9,11},{10,... | collective-permute-start | bytes 884744 | tf_op jit(solution)/shard_map/ppermute | solution.py:195
  14.7 3.1 %collective-permute-start.2 = (bf16[128,1152]{1,0:T(8,128)(2,1)S(1)}, bf16[128,1152]{1,0:T(8,128)(2,1)S(1)}, u32[]{:S(2)}, u32[]{:S(2)}) collective-permute-start(bf16[128,1152]{1,0:T(8,128)(2,1)S(1)} %get-tuple-element.25), channel_id=1, source_target_pairs={{0,4},{1,5},{2,6},{3,7},{4,0},{5,1},{6,2},{7,3},{8,12},{9,13},{10,... | collective-permute-start | bytes 884744 | tf_op jit(solution)/shard_map/ppermute | solution.py:195
  17.9 4.4 %collective-permute-start.3 = (bf16[128,1152]{1,0:T(8,128)(2,1)S(1)}, bf16[128,1152]{1,0:T(8,128)(2,1)S(1)}, u32[]{:S(2)}, u32[]{:S(2)}) collective-permute-start(bf16[128,1152]{1,0:T(8,128)(2,1)S(1)} %get-tuple-element.26), channel_id=1, source_target_pairs={{0,8},{1,9},{2,10},{3,11},{4,12},{5,13},{6,14},{7,15},{8,0},{9,1},... | collective-permute-start | bytes 884744 | tf_op jit(solution)/shard_map/ppermute | solution.py:195
  22.3 12.4 %collective-permute-done.refs_0_.refs_1_ = bf16[128,1152]{1,0:T(8,128)(2,1)S(1)} collective-permute-done((bf16[128,1152]{1,0:T(8,128)(2,1)}, bf16[128,1152]{1,0:T(8,128)(2,1)S(1)}, u32[]{:S(2)}, u32[]{:S(2)}) %collective-permute-start) | collective-permute-done | bytes 294944 | tf_op jit(solution)/shard_map/ppermute | solution.py:195
  34.7 1.2 shard_map.94
  35.9 1.1 shard_map.98
  37.1 3.5 %collective-permute-start.12 = (bf16[15,128,128]{2,1,0:T(8,128)(2,1)S(1)}, bf16[15,128,128]{2,1,0:T(8,128)(2,1)S(1)}, u32[]{:S(2)}, u32[]{:S(2)}) collective-permute-start(bf16[15,128,128]{2,1,0:T(8,128)(2,1)S(1)} %get-tuple-element.35), channel_id=1, source_target_pairs={{0,16},{16,0},{32,48},{48,32},{64,80},{80,64},{96,112},{112,96},{1... | collective-permute-start | bytes 1474568 | tf_op jit(solution)/shard_map/ppermute | solution.py:195
  40.6 1.5 collective-permute-done.12
  42.9 10.5 %all-to-all-start = ((bf16[16,120,128]{2,1,0:T(8,128)(2,1)}), bf16[16,120,128]{2,1,0:T(8,128)(2,1)S(1)}, u32[]{:S(2)}, u32[]{:S(2)}) async-start(bf16[16,120,128]{2,1,0:T(8,128)(2,1)} %shard_map.99), calls=%async_computation | async-start | bytes 983040 | tf_op jit(solution)/shard_map/all_to_all | solution.py:219
  53.5 4.6 %collective-permute-start.7 = (bf16[128,768]{1,0:T(8,128)(2,1)S(1)}, bf16[128,768]{1,0:T(8,128)(2,1)S(1)}, u32[]{:S(2)}, u32[]{:S(2)}) collective-permute-start(bf16[128,768]{1,0:T(8,128)(2,1)S(1)} %get-tuple-element.27.refs_0_), channel_id=1, source_target_pairs={{0,8},{1,9},{2,10},{3,11},{4,12},{5,13},{6,14},{7,15},{8,0},{9,1},... | collective-permute-start | bytes 589832 | tf_op jit(solution)/shard_map/ppermute | solution.py:195
  58.1 2.2 %collective-permute-start.6 = (bf16[128,768]{1,0:T(8,128)(2,1)S(1)}, bf16[128,768]{1,0:T(8,128)(2,1)S(1)}, u32[]{:S(2)}, u32[]{:S(2)}) collective-permute-start(bf16[128,768]{1,0:T(8,128)(2,1)S(1)} %get-tuple-element.27.refs_0_), channel_id=1, source_target_pairs={{0,4},{1,5},{2,6},{3,7},{4,0},{5,1},{6,2},{7,3},{8,12},{9,13},{10,... | collective-permute-start | bytes 589832 | tf_op jit(solution)/shard_map/ppermute | solution.py:195
  60.3 7.2 %collective-permute-start.5 = (bf16[128,768]{1,0:T(8,128)(2,1)S(1)}, bf16[128,768]{1,0:T(8,128)(2,1)S(1)}, u32[]{:S(2)}, u32[]{:S(2)}) collective-permute-start(bf16[128,768]{1,0:T(8,128)(2,1)S(1)} %get-tuple-element.27.refs_0_), channel_id=1, source_target_pairs={{0,2},{1,3},{2,0},{3,1},{4,6},{5,7},{6,4},{7,5},{8,10},{9,11},{10,... | collective-permute-start | bytes 589832 | tf_op jit(solution)/shard_map/ppermute | solution.py:195
  67.6 2.5 %collective-permute-start.4 = (bf16[128,768]{1,0:T(8,128)(2,1)S(1)}, bf16[128,768]{1,0:T(8,128)(2,1)S(1)}, u32[]{:S(2)}, u32[]{:S(2)}) collective-permute-start(bf16[128,768]{1,0:T(8,128)(2,1)S(1)} %get-tuple-element.27.refs_0_), channel_id=1, source_target_pairs={{0,1},{1,0},{2,3},{3,2},{4,5},{5,4},{6,7},{7,6},{8,9},{9,8},{10,11... | collective-permute-start | bytes 589832 | tf_op jit(solution)/shard_map/ppermute | solution.py:195
  70.2 1.2 collective-permute-done.5.refs_2_
  71.4 15.4 %collective-permute-done.4.refs_1_ = bf16[128,768]{1,0:T(8,128)(2,1)S(1)} collective-permute-done((bf16[128,768]{1,0:T(8,128)(2,1)S(1)}, bf16[128,768]{1,0:T(8,128)(2,1)S(1)}, u32[]{:S(2)}, u32[]{:S(2)}) %collective-permute-start.4) | collective-permute-done | bytes 196640 | tf_op jit(solution)/shard_map/ppermute | solution.py:195
  86.8 1.1 shard_map.100
  87.9 2.4 %collective-permute-start.13 = (bf16[15,128,128]{2,1,0:T(8,128)(2,1)S(1)}, bf16[15,128,128]{2,1,0:T(8,128)(2,1)S(1)}, u32[]{:S(2)}, u32[]{:S(2)}) collective-permute-start(bf16[15,128,128]{2,1,0:T(8,128)(2,1)S(1)} %get-tuple-element.37), channel_id=1, source_target_pairs={{0,16},{16,0},{32,48},{48,32},{64,80},{80,64},{96,112},{112,96},{1... | collective-permute-start | bytes 1474568 | tf_op jit(solution)/shard_map/ppermute | solution.py:195
  90.3 1.5 collective-permute-done.13
  91.9 18.1 %all_to_all.15.refs_1_ = bf16[16,120,128]{2,1,0:T(8,128)(2,1)S(1)} all-to-all(bf16[16,120,128]{2,1,0:T(8,128)(2,1)S(1)} %shard_map.101), channel_id=1, replica_groups={{0,32,64,96,128,160,192,224,256,288,320,352,384,416,448,480},{16,48,80,..., dimensions={0} | all-to-all | bytes 983040 | tf_op jit(solution)/shard_map/all_to_all | solution.py:219
  110.1 30.6 %all_to_all.16.mine = bf16[16,240,128]{2,1,0:T(8,128)(2,1)S(1)} all-to-all(bf16[16,240,128]{2,1,0:T(8,128)(2,1)S(1)} %shard_map.102), channel_id=1, replica_groups={{0,32,64,96,128,160,192,224,256,288,320,352,384,416,448,480},{16,48,80,..., dimensions={0} | all-to-all | bytes 1966080 | tf_op jit(solution)/shard_map/all_to_all | solution.py:219
  140.8 5.3 %collective-permute-start.14 = (bf16[16,240,128]{2,1,0:T(8,128)(2,1)S(1)}, bf16[16,240,128]{2,1,0:T(8,128)(2,1)S(1)}, u32[]{:S(2)}, u32[]{:S(2)}) collective-permute-start(bf16[16,240,128]{2,1,0:T(8,128)(2,1)S(1)} %all_to_all.16.mine), channel_id=1, source_target_pairs={{0,16},{16,0},{32,48},{48,32},{64,80},{80,64},{96,112},{112,96},{1... | collective-permute-start | bytes 2949128 | tf_op jit(solution)/shard_map/ppermute | solution.py:195
  146.1 1.4 shard_map.96
  147.6 4.2 %collective-permute-start.8 = (bf16[128,384]{1,0:T(8,128)(2,1)S(1)}, bf16[128,384]{1,0:T(8,128)(2,1)S(1)}, u32[]{:S(2)}, u32[]{:S(2)}) collective-permute-start(bf16[128,384]{1,0:T(8,128)(2,1)S(1)} %get-tuple-element.30), channel_id=1, source_target_pairs={{0,1},{1,0},{2,3},{3,2},{4,5},{5,4},{6,7},{7,6},{8,9},{9,8},{10,11... | collective-permute-start | bytes 294920 | tf_op jit(solution)/shard_map/ppermute | solution.py:195
  151.7 2.6 %collective-permute-start.9 = (bf16[128,384]{1,0:T(8,128)(2,1)S(1)}, bf16[128,384]{1,0:T(8,128)(2,1)S(1)}, u32[]{:S(2)}, u32[]{:S(2)}) collective-permute-start(bf16[128,384]{1,0:T(8,128)(2,1)S(1)} %get-tuple-element.31), channel_id=1, source_target_pairs={{0,2},{1,3},{2,0},{3,1},{4,6},{5,7},{6,4},{7,5},{8,10},{9,11},{10,... | collective-permute-start | bytes 294920 | tf_op jit(solution)/shard_map/ppermute | solution.py:195
  154.4 3.1 %collective-permute-start.10 = (bf16[128,384]{1,0:T(8,128)(2,1)S(1)}, bf16[128,384]{1,0:T(8,128)(2,1)S(1)}, u32[]{:S(2)}, u32[]{:S(2)}) collective-permute-start(bf16[128,384]{1,0:T(8,128)(2,1)S(1)} %get-tuple-element.32), channel_id=1, source_target_pairs={{0,4},{1,5},{2,6},{3,7},{4,0},{5,1},{6,2},{7,3},{8,12},{9,13},{10,... | collective-permute-start | bytes 294920 | tf_op jit(solution)/shard_map/ppermute | solution.py:195
  157.4 2.5 %collective-permute-start.11 = (bf16[128,384]{1,0:T(8,128)(2,1)S(1)}, bf16[128,384]{1,0:T(8,128)(2,1)S(1)}, u32[]{:S(2)}, u32[]{:S(2)}) collective-permute-start(bf16[128,384]{1,0:T(8,128)(2,1)S(1)} %get-tuple-element.33), channel_id=1, source_target_pairs={{0,8},{1,9},{2,10},{3,11},{4,12},{5,13},{6,14},{7,15},{8,0},{9,1},... | collective-permute-start | bytes 294920 | tf_op jit(solution)/shard_map/ppermute | solution.py:195
  160.0 1.7 collective-permute-done.9.refs_1_
  161.7 2.9 %collective-permute-done.11.refs_3_ = bf16[128,384]{1,0:T(8,128)(2,1)S(1)} collective-permute-done((bf16[128,384]{1,0:T(8,128)(2,1)S(1)}, bf16[128,384]{1,0:T(8,128)(2,1)S(1)}, u32[]{:S(2)}, u32[]{:S(2)}) %collective-permute-start.11) | collective-permute-done | bytes 98336 | tf_op jit(solution)/shard_map/ppermute | solution.py:195
  165.3 1.7 shard_map.95
  167.0 1.4 shard_map.103
  (25 shorter events, 2.6 us)
Async XLA Ops:
  0.6 0.7 copy-start.4
  0.6 34.0 %copy-start = (bf16[1,5,6,128,128]{4,3,2,1,0:T(8,128)(2,1)S(1)}, bf16[1,5,6,128,128]{4,3,2,1,0:T(8,128)(2,1)}, u32[]{:S(2)}) copy-start(bf16[1,5,6,128,128]{4,3,2,1,0:T(8,128)(2,1)} %param.7) | copy-start | bytes 2949124
  1.3 33.4 %copy-start.2 = (bf16[128,384]{1,0:T(8,128)(2,1)S(1)}, bf16[128,384]{1,0:T(8,128)(2,1)}, u32[]{:S(2)}) copy-start(bf16[128,384]{1,0:T(8,128)(2,1)} %refs_0_.1) | copy-start | bytes 294916
  4.1 30.6 %collective-permute-start = (bf16[128,1152]{1,0:T(8,128)(2,1)}, bf16[128,1152]{1,0:T(8,128)(2,1)S(1)}, u32[]{:S(2)}, u32[]{:S(2)}) collective-permute-start(bf16[128,1152]{1,0:T(8,128)(2,1)} %get-tuple-element.23), channel_id=1, source_target_pairs={{0,1},{1,0},{2,3},{3,2},{4,5},{5,4},{6,7},{7,6},{8,9},{9,8},{10,11... | collective-permute-start | bytes 884744 | tf_op jit(solution)/shard_map/ppermute | solution.py:195
  9.1 25.6 %collective-permute-start.1 = (bf16[128,1152]{1,0:T(8,128)(2,1)}, bf16[128,1152]{1,0:T(8,128)(2,1)S(1)}, u32[]{:S(2)}, u32[]{:S(2)}) collective-permute-start(bf16[128,1152]{1,0:T(8,128)(2,1)} %get-tuple-element.24), channel_id=1, source_target_pairs={{0,2},{1,3},{2,0},{3,1},{4,6},{5,7},{6,4},{7,5},{8,10},{9,11},{10,... | collective-permute-start | bytes 884744 | tf_op jit(solution)/shard_map/ppermute | solution.py:195
  14.7 19.9 %collective-permute-start.2 = (bf16[128,1152]{1,0:T(8,128)(2,1)S(1)}, bf16[128,1152]{1,0:T(8,128)(2,1)S(1)}, u32[]{:S(2)}, u32[]{:S(2)}) collective-permute-start(bf16[128,1152]{1,0:T(8,128)(2,1)S(1)} %get-tuple-element.25), channel_id=1, source_target_pairs={{0,4},{1,5},{2,6},{3,7},{4,0},{5,1},{6,2},{7,3},{8,12},{9,13},{10,... | collective-permute-start | bytes 884744 | tf_op jit(solution)/shard_map/ppermute | solution.py:195
  17.9 16.8 %collective-permute-start.3 = (bf16[128,1152]{1,0:T(8,128)(2,1)S(1)}, bf16[128,1152]{1,0:T(8,128)(2,1)S(1)}, u32[]{:S(2)}, u32[]{:S(2)}) collective-permute-start(bf16[128,1152]{1,0:T(8,128)(2,1)S(1)} %get-tuple-element.26), channel_id=1, source_target_pairs={{0,8},{1,9},{2,10},{3,11},{4,12},{5,13},{6,14},{7,15},{8,0},{9,1},... | collective-permute-start | bytes 884744 | tf_op jit(solution)/shard_map/ppermute | solution.py:195
  22.3 12.4 %copy-start.5 = (s32[1,5,6]{2,0,1:T(1,128)S(1)}, s32[1,5,6]{2,0,1:T(1,128)}, u32[]{:S(2)}) copy-start(s32[1,5,6]{2,0,1:T(1,128)} %param.8) | copy-start | bytes 364
  37.1 4.9 %collective-permute-start.12 = (bf16[15,128,128]{2,1,0:T(8,128)(2,1)S(1)}, bf16[15,128,128]{2,1,0:T(8,128)(2,1)S(1)}, u32[]{:S(2)}, u32[]{:S(2)}) collective-permute-start(bf16[15,128,128]{2,1,0:T(8,128)(2,1)S(1)} %get-tuple-element.35), channel_id=1, source_target_pairs={{0,16},{16,0},{32,48},{48,32},{64,80},{80,64},{96,112},{112,96},{1... | collective-permute-start | bytes 1474568 | tf_op jit(solution)/shard_map/ppermute | solution.py:195
  42.9 43.8 %copy-start.3 = (bf16[128,384]{1,0:T(8,128)(2,1)S(1)}, bf16[128,384]{1,0:T(8,128)(2,1)}, u32[]{:S(2)}) copy-start(bf16[128,384]{1,0:T(8,128)(2,1)} %cot.3) | copy-start | bytes 294916
  42.9 49.0 %all-to-all-start = ((bf16[16,120,128]{2,1,0:T(8,128)(2,1)}), bf16[16,120,128]{2,1,0:T(8,128)(2,1)S(1)}, u32[]{:S(2)}, u32[]{:S(2)}) async-start(bf16[16,120,128]{2,1,0:T(8,128)(2,1)} %shard_map.99), calls=%async_computation | async-start | bytes 983040 | tf_op jit(solution)/shard_map/all_to_all | solution.py:219
  53.5 16.7 %collective-permute-start.7 = (bf16[128,768]{1,0:T(8,128)(2,1)S(1)}, bf16[128,768]{1,0:T(8,128)(2,1)S(1)}, u32[]{:S(2)}, u32[]{:S(2)}) collective-permute-start(bf16[128,768]{1,0:T(8,128)(2,1)S(1)} %get-tuple-element.27.refs_0_), channel_id=1, source_target_pairs={{0,8},{1,9},{2,10},{3,11},{4,12},{5,13},{6,14},{7,15},{8,0},{9,1},... | collective-permute-start | bytes 589832 | tf_op jit(solution)/shard_map/ppermute | solution.py:195
  58.1 12.0 %collective-permute-start.6 = (bf16[128,768]{1,0:T(8,128)(2,1)S(1)}, bf16[128,768]{1,0:T(8,128)(2,1)S(1)}, u32[]{:S(2)}, u32[]{:S(2)}) collective-permute-start(bf16[128,768]{1,0:T(8,128)(2,1)S(1)} %get-tuple-element.27.refs_0_), channel_id=1, source_target_pairs={{0,4},{1,5},{2,6},{3,7},{4,0},{5,1},{6,2},{7,3},{8,12},{9,13},{10,... | collective-permute-start | bytes 589832 | tf_op jit(solution)/shard_map/ppermute | solution.py:195
  60.3 11.0 %collective-permute-start.5 = (bf16[128,768]{1,0:T(8,128)(2,1)S(1)}, bf16[128,768]{1,0:T(8,128)(2,1)S(1)}, u32[]{:S(2)}, u32[]{:S(2)}) collective-permute-start(bf16[128,768]{1,0:T(8,128)(2,1)S(1)} %get-tuple-element.27.refs_0_), channel_id=1, source_target_pairs={{0,2},{1,3},{2,0},{3,1},{4,6},{5,7},{6,4},{7,5},{8,10},{9,11},{10,... | collective-permute-start | bytes 589832 | tf_op jit(solution)/shard_map/ppermute | solution.py:195
  67.6 19.2 %collective-permute-start.4 = (bf16[128,768]{1,0:T(8,128)(2,1)S(1)}, bf16[128,768]{1,0:T(8,128)(2,1)S(1)}, u32[]{:S(2)}, u32[]{:S(2)}) collective-permute-start(bf16[128,768]{1,0:T(8,128)(2,1)S(1)} %get-tuple-element.27.refs_0_), channel_id=1, source_target_pairs={{0,1},{1,0},{2,3},{3,2},{4,5},{5,4},{6,7},{7,6},{8,9},{9,8},{10,11... | collective-permute-start | bytes 589832 | tf_op jit(solution)/shard_map/ppermute | solution.py:195
  87.9 3.9 %collective-permute-start.13 = (bf16[15,128,128]{2,1,0:T(8,128)(2,1)S(1)}, bf16[15,128,128]{2,1,0:T(8,128)(2,1)S(1)}, u32[]{:S(2)}, u32[]{:S(2)}) collective-permute-start(bf16[15,128,128]{2,1,0:T(8,128)(2,1)S(1)} %get-tuple-element.37), channel_id=1, source_target_pairs={{0,16},{16,0},{32,48},{48,32},{64,80},{80,64},{96,112},{112,96},{1... | collective-permute-start | bytes 1474568 | tf_op jit(solution)/shard_map/ppermute | solution.py:195
  140.8 24.5 %copy-start.1 = (bf16[1,5,3,2,128,128]{5,4,3,2,1,0:T(8,128)(2,1)S(1)}, bf16[1,5,3,2,128,128]{5,4,3,2,1,0:T(8,128)(2,1)}, u32[]{:S(2)}) copy-start(bf16[1,5,3,2,128,128]{5,4,3,2,1,0:T(8,128)(2,1)} %param.9) | copy-start | bytes 2949124
  140.8 26.2 %collective-permute-start.14 = (bf16[16,240,128]{2,1,0:T(8,128)(2,1)S(1)}, bf16[16,240,128]{2,1,0:T(8,128)(2,1)S(1)}, u32[]{:S(2)}, u32[]{:S(2)}) collective-permute-start(bf16[16,240,128]{2,1,0:T(8,128)(2,1)S(1)} %all_to_all.16.mine), channel_id=1, source_target_pairs={{0,16},{16,0},{32,48},{48,32},{64,80},{80,64},{96,112},{112,96},{1... | collective-permute-start | bytes 2949128 | tf_op jit(solution)/shard_map/ppermute | solution.py:195
  147.6 12.4 %collective-permute-start.8 = (bf16[128,384]{1,0:T(8,128)(2,1)S(1)}, bf16[128,384]{1,0:T(8,128)(2,1)S(1)}, u32[]{:S(2)}, u32[]{:S(2)}) collective-permute-start(bf16[128,384]{1,0:T(8,128)(2,1)S(1)} %get-tuple-element.30), channel_id=1, source_target_pairs={{0,1},{1,0},{2,3},{3,2},{4,5},{5,4},{6,7},{7,6},{8,9},{9,8},{10,11... | collective-permute-start | bytes 294920 | tf_op jit(solution)/shard_map/ppermute | solution.py:195
  151.7 9.9 %collective-permute-start.9 = (bf16[128,384]{1,0:T(8,128)(2,1)S(1)}, bf16[128,384]{1,0:T(8,128)(2,1)S(1)}, u32[]{:S(2)}, u32[]{:S(2)}) collective-permute-start(bf16[128,384]{1,0:T(8,128)(2,1)S(1)} %get-tuple-element.31), channel_id=1, source_target_pairs={{0,2},{1,3},{2,0},{3,1},{4,6},{5,7},{6,4},{7,5},{8,10},{9,11},{10,... | collective-permute-start | bytes 294920 | tf_op jit(solution)/shard_map/ppermute | solution.py:195
  154.4 7.3 %collective-permute-start.10 = (bf16[128,384]{1,0:T(8,128)(2,1)S(1)}, bf16[128,384]{1,0:T(8,128)(2,1)S(1)}, u32[]{:S(2)}, u32[]{:S(2)}) collective-permute-start(bf16[128,384]{1,0:T(8,128)(2,1)S(1)} %get-tuple-element.32), channel_id=1, source_target_pairs={{0,4},{1,5},{2,6},{3,7},{4,0},{5,1},{6,2},{7,3},{8,12},{9,13},{10,... | collective-permute-start | bytes 294920 | tf_op jit(solution)/shard_map/ppermute | solution.py:195
  157.4 7.2 %collective-permute-start.11 = (bf16[128,384]{1,0:T(8,128)(2,1)S(1)}, bf16[128,384]{1,0:T(8,128)(2,1)S(1)}, u32[]{:S(2)}, u32[]{:S(2)}) collective-permute-start(bf16[128,384]{1,0:T(8,128)(2,1)S(1)} %get-tuple-element.33), channel_id=1, source_target_pairs={{0,8},{1,9},{2,10},{3,11},{4,12},{5,13},{6,14},{7,15},{8,0},{9,1},... | collective-permute-start | bytes 294920 | tf_op jit(solution)/shard_map/ppermute | solution.py:195

commit v6 on v4

--- a/solution.py
+++ b/solution.py
@@ -73,7 +73,7 @@
             both = jnp.concatenate([w[(lvl * db + o) * kd + k] for k in range(kd)], axis=0)
             term = dot_nt(cot[:, o * B : (o + 1) * B], both)
             for k in range(kd):
-                spot = pick[(lvl * db + o) * kd + k]
+                spot = pick[o, k, lvl]
                 acc[spot] += term[:, k * B : (k + 1) * B]
         for h in range(hb):
             if lvl == 0:
@@ -89,7 +89,7 @@
     for o in range(hb):
         here = slice(o * B, (o + 1) * B)
         lhs = jnp.concatenate(
-            [xs[lvl][:, lanes(pick[lvl * hb + o])] for lvl in range(levels)], axis=1
+            [xs[lvl][:, lanes(pick[lvl, 0, o])] for lvl in range(levels)], axis=1
         )
         rhs = jnp.concatenate([w[lvl * hb + o] for lvl in range(levels)], axis=0)
         v = jnp.dot(lhs, rhs, preferred_element_type=F32)
@@ -110,7 +110,7 @@
     for lvl in range(levels):
         acc[...] = jnp.zeros_like(acc)
         for o in range(hb):
-            spot = pick[lvl * hb + o]
+            spot = pick[lvl, 0, o]
             acc[spot] += dot_nt(hg[:, o * B : (o + 1) * B], w[lvl * hb + o])
         for d in range(db):
             outs[lvl][:, d * B : (d + 1) * B] = acc[d].astype(outs[lvl].dtype)
@@ -128,7 +128,7 @@
     for o in range(hb):
         right = hg[:, o * B : (o + 1) * B]
         for lvl in range(levels):
-            left = xs[lvl][:, lanes(pick[lvl * hb + o])]
+            left = xs[lvl][:, lanes(pick[lvl, 0, o])]
             scr[lvl * hb + o] = dot_tn(left, right)
     split(core[0], scr, keep, send)
 
@@ -141,11 +141,17 @@
         for lvl in range(levels):
             for k in range(kd):
                 i = (lvl * db + o) * kd + k
-                scr[i] = dot_tn(acts[lvl][:, lanes(pick[i])], right)
+                scr[i] = dot_tn(acts[lvl][:, lanes(pick[o, k, lvl])], right)
     split(core[0], scr, keep, send)
 
 
-def pair_kernel(*refs):
+def pair_kernel(row, keep, got, keep_y, send_y):
+    mine, other = row[0], 1 - row[0]
+    keep_y[...] = keep[mine] + got[mine].astype(F32)
+    send_y[...] = (keep[other] + got[other].astype(F32)).astype(BF16)
+
+
+def column_kernel(*refs):
     out = refs[-1]
     at = 0
     for keep, got in zip(refs[0:-1:2], refs[1:-1:2]):
@@ -164,11 +170,11 @@
 def out_kernel(levels, db, kd, pick, w, *refs):
     acts, out = refs[:levels], refs[levels]
     for o in range(db):
-        spots = [(lvl * db + o) * kd + k for lvl in range(levels) for k in range(kd)]
+        slots = [(lvl, k) for lvl in range(levels) for k in range(kd)]
         lhs = jnp.concatenate(
-            [acts[i // (db * kd)][:, lanes(pick[i])] for i in spots], axis=1
+            [acts[lvl][:, lanes(pick[o, k, lvl])] for lvl, k in slots], axis=1
         )
-        rhs = jnp.concatenate([w[i] for i in spots], axis=0)
+        rhs = jnp.concatenate([w[(lvl * db + o) * kd + k] for lvl, k in slots], axis=0)
         out[:, o * B : (o + 1) * B] = jnp.dot(lhs, rhs, preferred_element_type=F32).astype(BF16)
 
 
@@ -207,18 +213,36 @@
     n_up, n_down = levels * hb, levels * db * kd
     up_w = up_weight.reshape(n_up, B, B)
     down_w = down_weight.reshape(n_down, B, B)
-    up_ids = up_pick.reshape(n_up)
-    down_ids = down_pick.reshape(n_down)
+    up_ids = up_pick.transpose(1, 0, 2)
+    down_ids = down_pick[0].transpose(1, 2, 0)
     core = lax.rem(lax.axis_index("dp"), 2).reshape(1)
-    groups = [[2 * i + c for i in range(chips)] for c in range(2)]
+    row = lax.div(lax.axis_index("dp"), chips).reshape(1)
+    deep_z = chips // 2
+    chip_groups = [[2 * i + c for i in range(chips)] for c in range(2)]
+    column_groups = [
+        [chips * r + 2 * i + c for i in range(deep_z)] for r in range(2) for c in range(2)
+    ]
+    row_bit = dp.bit_length() - 2
 
     def over_mp(blocks):
         return [from_partner(blocks[b], "mp", b) for b in range(bits)]
 
-    def exchange(block):
+    def exchange(block, groups):
         return lax.all_to_all(
             block, "dp", split_axis=0, concat_axis=0, axis_index_groups=groups, tiled=True
         )
+
+    def partials(keep, send):
+        got = from_partner(send, "dp", 0)
+        view = (2, deep_z, -1, B)
+        rows = keep.size // (chips * B)
+        keep_y, send_y = call(
+            pair_kernel,
+            [sds((deep_z, rows, B), F32), sds((deep_z, rows, B), BF16)],
+            [SMEM, VMEM, VMEM],
+            (),
+        )(row, keep.reshape(view), got.reshape(view))
+        return keep_y, from_partner(send_y, "dp", row_bit)
 
     wide, deep = db * B, hb * B
     own, *first = call(
@@ -256,7 +280,7 @@
         [SMEM, SMEM, VMEM] + [VMEM] * levels,
         [pltpu.VMEM((n_up, B, B), F32)],
     )(up_ids, core, hg, inputs, *got)
-    up_got = from_partner(up_send, "dp", 0)
+    up_parts = partials(up_keep, up_send)
 
     down_keep, down_send = call(
         functools.partial(down_kernel, levels, db, kd),
@@ -264,7 +288,7 @@
         [SMEM, SMEM, VMEM] + [VMEM] * levels,
         [pltpu.VMEM((n_down, B, B), F32)],
     )(down_ids, core, cotangent, *acts)
-    down_got = from_partner(down_send, "dp", 0)
+    down_parts = partials(down_keep, down_send)
 
     output = call(
         functools.partial(out_kernel, levels, db, kd),
@@ -273,17 +297,18 @@
         (),
     )(down_ids, down_w, *acts)
 
-    halves = [a.reshape(chips, -1, B) for a in (up_keep, up_got, down_keep, down_got)]
-    rows = [halves[0].shape[1], halves[2].shape[1]]
-    pair = call(pair_kernel, sds((chips, sum(rows), B), BF16), [VMEM] * 4, ())(*halves)
-    parts = exchange(pair)
+    rows = [up_parts[0].shape[1], down_parts[0].shape[1]]
+    column = call(
+        column_kernel, sds((deep_z, sum(rows), B), BF16), [VMEM] * 4, ()
+    )(*up_parts, *down_parts)
+    parts = exchange(column, column_groups)
     shard = call(
         functools.partial(shard_kernel, scale),
         sds((chips, sum(rows), B), BF16),
         [VMEM],
         (),
     )(parts)
-    mine = exchange(shard)
+    mine = exchange(shard, chip_groups)
     other = from_partner(mine, "dp", 0)
     up_out, down_out = call(
         join_kernel, [hbm((2, chips, r, B), BF16) for r in rows], [SMEM, VMEM, VMEM], ()

time: 167 us -> 163 us (0.976)
  blocking collectives: 63 us -> 51.2 us
  starting transfers between devices: 59.2 us -> 66.9 us
  waiting for transfers between devices: 29.6 us -> 23.2 us
  Pallas kernels: 11.6 us -> 15.9 us
    all_to_all x2, blocking collectives: 63 us -> 51.2 us  [exchange(): lax.all_to_all(block, 'dp', split_axis=0, concat_axis=0, axis_index_group...]
    ppermute x15 -> x17, starting transfers between devices: 59.2 us -> 66.9 us  [from_partner(): return lax.ppermute(block, axis, [(i, i ^ 1 << bit) for i in range(count)])]
    ppermute x15 -> x17, waiting for transfers between devices: 29.6 us -> 23.2 us  [from_partner(): return lax.ppermute(block, axis, [(i, i ^ 1 << bit) for i in range(count)])]
    pallas_call x10 -> x12, Pallas kernels: 11.6 us -> 15.9 us  [invoke(): return run(*placed)]
  transfers between devices with their start and end apart: 15 -> 17, of which waited for: 6 -> 5; matrix products, arithmetic and copies ran while one was open for 0% -> 0% of each run, Pallas kernels for 4% -> 7%
where the time goes in v6:
time: 163 us; the launch traced here: 160 us
  starting transfers between devices  66.9 us (41%)
  blocking collectives  51.2 us (31%)
  waiting for transfers between devices  23.2 us (14%)
  Pallas kernels  15.9 us (10%)
  local copies, waits for them, and re-layouts  2.28 us (1%)
    ppermute x17, starting transfers between devices, from_partner(): return lax.ppermute(block, axis, [(i, i ^ 1 << bit) for i in range(count)])  66.9 us
    all_to_all x2, blocking collectives, exchange(): lax.all_to_all(block, 'dp', split_axis=0, concat_axis=0, axis_index_group...  51.2 us
    ppermute x17, waiting for transfers between devices, from_partner(): return lax.ppermute(block, axis, [(i, i ^ 1 << bit) for i in range(count)])  23.2 us
    pallas_call x12, Pallas kernels, invoke(): return run(*placed)  15.9 us
  transfers between devices with their start and end apart: 17, of which 5 were waited for; matrix products, arithmetic and copies ran while one was open for 0% of the time, Pallas kernels for 7%

profile of v6, /device:TPU:1, one launch (start us, length us, event | category | flops | bytes accessed | tf_op | source)
XLA Modules:
  0.0 160.4 jit_solution(7065827302884730579)
XLA Ops:
  1.3 2.0 %shard_map.93 = (f32[128,768]{1,0:T(8,128)S(1)}, bf16[128,1152]{1,0:T(8,128)(2,1)S(1)}, bf16[128,1152]{1,0:T(8,128)(2,1)S(1)}, bf16[128,1152]{1,0:T(8,128)(2,1)S(1)}, bf16[128,1152]{1,0:T(8,128)(2,1)S(1)}) custom-call(s32[3,2,5]{2,1,0:T(2,128)S(1)} %bitcast.20, bf16[128,384]{1,0:T(8,128)(2,1)} %cot.3, bf16[30,128,128]{2,1,0:T(8,128)(2,1)} %bitcast.16, ...), custom_call_target="tpu_custom_call" | custom-call | tf_op jit(solution)/shard_map/pallas_call | solution.py:48
  3.3 5.0 %collective-permute-start = (bf16[128,1152]{1,0:T(8,128)(2,1)S(1)}, bf16[128,1152]{1,0:T(8,128)(2,1)S(1)}, u32[]{:S(2)}, u32[]{:S(2)}) collective-permute-start(bf16[128,1152]{1,0:T(8,128)(2,1)S(1)} %get-tuple-element.27), channel_id=1, source_target_pairs={{0,1},{1,0},{2,3},{3,2},{4,5},{5,4},{6,7},{7,6},{8,9},{9,8},{10,11... | collective-permute-start | bytes 884744 | tf_op jit(solution)/shard_map/ppermute | solution.py:201
  8.3 5.7 %collective-permute-start.1 = (bf16[128,1152]{1,0:T(8,128)(2,1)S(1)}, bf16[128,1152]{1,0:T(8,128)(2,1)S(1)}, u32[]{:S(2)}, u32[]{:S(2)}) collective-permute-start(bf16[128,1152]{1,0:T(8,128)(2,1)S(1)} %get-tuple-element.28), channel_id=1, source_target_pairs={{0,2},{1,3},{2,0},{3,1},{4,6},{5,7},{6,4},{7,5},{8,10},{9,11},{10,... | collective-permute-start | bytes 884744 | tf_op jit(solution)/shard_map/ppermute | solution.py:201
  14.0 3.1 %collective-permute-start.2 = (bf16[128,1152]{1,0:T(8,128)(2,1)S(1)}, bf16[128,1152]{1,0:T(8,128)(2,1)S(1)}, u32[]{:S(2)}, u32[]{:S(2)}) collective-permute-start(bf16[128,1152]{1,0:T(8,128)(2,1)S(1)} %get-tuple-element.29), channel_id=1, source_target_pairs={{0,4},{1,5},{2,6},{3,7},{4,0},{5,1},{6,2},{7,3},{8,12},{9,13},{10,... | collective-permute-start | bytes 884744 | tf_op jit(solution)/shard_map/ppermute | solution.py:201
  17.1 4.4 %collective-permute-start.3 = (bf16[128,1152]{1,0:T(8,128)(2,1)S(1)}, bf16[128,1152]{1,0:T(8,128)(2,1)S(1)}, u32[]{:S(2)}, u32[]{:S(2)}) collective-permute-start(bf16[128,1152]{1,0:T(8,128)(2,1)S(1)} %get-tuple-element.30), channel_id=1, source_target_pairs={{0,8},{1,9},{2,10},{3,11},{4,12},{5,13},{6,14},{7,15},{8,0},{9,1},... | collective-permute-start | bytes 884744 | tf_op jit(solution)/shard_map/ppermute | solution.py:201
  21.5 12.2 %collective-permute-done.refs_0_.refs_1_ = bf16[128,1152]{1,0:T(8,128)(2,1)S(1)} collective-permute-done((bf16[128,1152]{1,0:T(8,128)(2,1)S(1)}, bf16[128,1152]{1,0:T(8,128)(2,1)S(1)}, u32[]{:S(2)}, u32[]{:S(2)}) %collective-permute-start) | collective-permute-done | bytes 294944 | tf_op jit(solution)/shard_map/ppermute | solution.py:201
  33.7 1.2 shard_map.94
  35.7 1.9 %collective-permute-start.4 = (bf16[128,768]{1,0:T(8,128)(2,1)S(1)}, bf16[128,768]{1,0:T(8,128)(2,1)}, u32[]{:S(2)}, u32[]{:S(2)}) collective-permute-start(bf16[128,768]{1,0:T(8,128)(2,1)S(1)} %get-tuple-element.31.refs_0_), channel_id=1, source_target_pairs={{0,1},{1,0},{2,3},{3,2},{4,5},{5,4},{6,7},{7,6},{8,9},{9,8},{10,11... | collective-permute-start | bytes 589832 | tf_op jit(solution)/shard_map/ppermute | solution.py:201
  37.6 8.4 %collective-permute-start.5 = (bf16[128,768]{1,0:T(8,128)(2,1)S(1)}, bf16[128,768]{1,0:T(8,128)(2,1)}, u32[]{:S(2)}, u32[]{:S(2)}) collective-permute-start(bf16[128,768]{1,0:T(8,128)(2,1)S(1)} %get-tuple-element.31.refs_0_), channel_id=1, source_target_pairs={{0,2},{1,3},{2,0},{3,1},{4,6},{5,7},{6,4},{7,5},{8,10},{9,11},{10,... | collective-permute-start | bytes 589832 | tf_op jit(solution)/shard_map/ppermute | solution.py:201
  46.0 3.1 %collective-permute-start.6 = (bf16[128,768]{1,0:T(8,128)(2,1)S(1)}, bf16[128,768]{1,0:T(8,128)(2,1)}, u32[]{:S(2)}, u32[]{:S(2)}) collective-permute-start(bf16[128,768]{1,0:T(8,128)(2,1)S(1)} %get-tuple-element.31.refs_0_), channel_id=1, source_target_pairs={{0,4},{1,5},{2,6},{3,7},{4,0},{5,1},{6,2},{7,3},{8,12},{9,13},{10,... | collective-permute-start | bytes 589832 | tf_op jit(solution)/shard_map/ppermute | solution.py:201
  49.2 4.4 %collective-permute-start.7 = (bf16[128,768]{1,0:T(8,128)(2,1)S(1)}, bf16[128,768]{1,0:T(8,128)(2,1)}, u32[]{:S(2)}, u32[]{:S(2)}) collective-permute-start(bf16[128,768]{1,0:T(8,128)(2,1)S(1)} %get-tuple-element.31.refs_0_), channel_id=1, source_target_pairs={{0,8},{1,9},{2,10},{3,11},{4,12},{5,13},{6,14},{7,15},{8,0},{9,1},... | collective-permute-start | bytes 589832 | tf_op jit(solution)/shard_map/ppermute | solution.py:201
  54.5 1.9 %shard_map.98 = (f32[15,128,128]{2,1,0:T(8,128)S(1)}, bf16[15,128,128]{2,1,0:T(8,128)(2,1)}) custom-call(s32[5,1,6]{2,1,0:T(1,128)S(1)} %bitcast.24, s32[1]{0:T(128)} %bitcast.6.core, bf16[128,768]{1,0:T(8,128)(2,1)S(1)} %copy-done.4, bf16[128,384]{1,0:T(8,128)(2,1)S(1)} %copy-done.2, bf16[128,1152]{1,0:T(8,128)(2,1)S(1)} %collective-permute-done.refs_0_.refs_1_, ...), custom_call_target="tpu_custom_call" | custom-call | tf_op jit(solution)/shard_map/pallas_call | solution.py:48
  56.4 3.3 %collective-permute-start.12 = (bf16[15,128,128]{2,1,0:T(8,128)(2,1)}, bf16[15,128,128]{2,1,0:T(8,128)(2,1)}, u32[]{:S(2)}, u32[]{:S(2)}) collective-permute-start(bf16[15,128,128]{2,1,0:T(8,128)(2,1)} %get-tuple-element.39), channel_id=1, source_target_pairs={{0,16},{16,0},{32,48},{48,32},{64,80},{80,64},{96,112},{112,96},{1... | collective-permute-start | bytes 1474568 | tf_op jit(solution)/shard_map/ppermute | solution.py:201
  60.0 2.6 %shard_map.100 = (f32[15,128,128]{2,1,0:T(8,128)S(1)}, bf16[15,128,128]{2,1,0:T(8,128)(2,1)}) custom-call(s32[3,2,5]{2,1,0:T(2,128)S(1)} %bitcast.21, s32[1]{0:T(128)} %bitcast.6.core, bf16[128,384]{1,0:T(8,128)(2,1)S(1)} %copy-done.6, bf16[128,768]{1,0:T(8,128)(2,1)S(1)} %get-tuple-element.31.refs_0_, bf16[128,768]{1,0:T(8,128)(2,1)} %collective-permute-done.4.refs_1_, ...), custom_call_target="tpu_custom_call" | custom-call | tf_op jit(solution)/shard_map/pallas_call | solution.py:48
  62.6 3.6 %collective-permute-start.14 = (bf16[15,128,128]{2,1,0:T(8,128)(2,1)}, bf16[15,128,128]{2,1,0:T(8,128)(2,1)}, u32[]{:S(2)}, u32[]{:S(2)}) collective-permute-start(bf16[15,128,128]{2,1,0:T(8,128)(2,1)} %get-tuple-element.43), channel_id=1, source_target_pairs={{0,16},{16,0},{32,48},{48,32},{64,80},{80,64},{96,112},{112,96},{1... | collective-permute-start | bytes 1474568 | tf_op jit(solution)/shard_map/ppermute | solution.py:201
  66.3 1.1 shard_map.99
  67.4 2.8 %collective-permute-start.13 = (bf16[8,120,128]{2,1,0:T(8,128)(2,1)S(1)}, bf16[8,120,128]{2,1,0:T(8,128)(2,1)S(1)}, u32[]{:S(2)}, u32[]{:S(2)}) collective-permute-start(bf16[8,120,128]{2,1,0:T(8,128)(2,1)S(1)} %get-tuple-element.41), channel_id=1, source_target_pairs={{0,256},{16,272},{32,288},{48,304},{64,320},{80,336},{96,352},{112... | collective-permute-start | bytes 737288 | tf_op jit(solution)/shard_map/ppermute | solution.py:201
  70.2 1.1 shard_map.101
  71.3 2.5 %collective-permute-start.15 = (bf16[8,120,128]{2,1,0:T(8,128)(2,1)S(1)}, bf16[8,120,128]{2,1,0:T(8,128)(2,1)S(1)}, u32[]{:S(2)}, u32[]{:S(2)}) collective-permute-start(bf16[8,120,128]{2,1,0:T(8,128)(2,1)S(1)} %get-tuple-element.45), channel_id=1, source_target_pairs={{0,256},{16,272},{32,288},{48,304},{64,320},{80,336},{96,352},{112... | collective-permute-start | bytes 737288 | tf_op jit(solution)/shard_map/ppermute | solution.py:201
  73.8 3.0 %collective-permute-done.13.refs_1_ = bf16[8,120,128]{2,1,0:T(8,128)(2,1)S(1)} collective-permute-done((bf16[8,120,128]{2,1,0:T(8,128)(2,1)S(1)}, bf16[8,120,128]{2,1,0:T(8,128)(2,1)S(1)}, u32[]{:S(2)}, u32[]{:S(2)}) %collective-permute-start.13) | collective-permute-done | bytes 245792 | tf_op jit(solution)/shard_map/ppermute | solution.py:201
  76.8 5.3 %collective-permute-done.15.refs_3_ = bf16[8,120,128]{2,1,0:T(8,128)(2,1)S(1)} collective-permute-done((bf16[8,120,128]{2,1,0:T(8,128)(2,1)S(1)}, bf16[8,120,128]{2,1,0:T(8,128)(2,1)S(1)}, u32[]{:S(2)}, u32[]{:S(2)}) %collective-permute-start.15) | collective-permute-done | bytes 245792 | tf_op jit(solution)/shard_map/ppermute | solution.py:201
  82.1 25.0 %all_to_all.10.parts = bf16[8,240,128]{2,1,0:T(8,128)(2,1)S(1)} all-to-all(bf16[8,240,128]{2,1,0:T(8,128)(2,1)S(1)} %shard_map.102), channel_id=1, replica_groups={{0,32,64,96,128,160,192,224},{16,48,80,112,144,176,208,240},{256,288,32..., dimensions={0} | all-to-all | bytes 983040 | tf_op jit(solution)/shard_map/all_to_all | solution.py:231
  107.2 26.2 %all_to_all.11.mine = bf16[16,240,128]{2,1,0:T(8,128)(2,1)S(1)} all-to-all(bf16[16,240,128]{2,1,0:T(8,128)(2,1)S(1)} %shard_map.103), channel_id=1, replica_groups={{0,32,64,96,128,160,192,224,256,288,320,352,384,416,448,480},{16,48,80,..., dimensions={0} | all-to-all | bytes 1966080 | tf_op jit(solution)/shard_map/all_to_all | solution.py:231
  133.4 4.6 %collective-permute-start.16 = (bf16[16,240,128]{2,1,0:T(8,128)(2,1)S(1)}, bf16[16,240,128]{2,1,0:T(8,128)(2,1)S(1)}, u32[]{:S(2)}, u32[]{:S(2)}) collective-permute-start(bf16[16,240,128]{2,1,0:T(8,128)(2,1)S(1)} %all_to_all.11.mine), channel_id=1, source_target_pairs={{0,16},{16,0},{32,48},{48,32},{64,80},{80,64},{96,112},{112,96},{1... | collective-permute-start | bytes 2949128 | tf_op jit(solution)/shard_map/ppermute | solution.py:201
  138.1 1.4 shard_map.96
  139.5 4.0 %collective-permute-start.8 = (bf16[128,384]{1,0:T(8,128)(2,1)S(1)}, bf16[128,384]{1,0:T(8,128)(2,1)S(1)}, u32[]{:S(2)}, u32[]{:S(2)}) collective-permute-start(bf16[128,384]{1,0:T(8,128)(2,1)S(1)} %get-tuple-element.34), channel_id=1, source_target_pairs={{0,1},{1,0},{2,3},{3,2},{4,5},{5,4},{6,7},{7,6},{8,9},{9,8},{10,11... | collective-permute-start | bytes 294920 | tf_op jit(solution)/shard_map/ppermute | solution.py:201
  143.5 2.4 %collective-permute-start.9 = (bf16[128,384]{1,0:T(8,128)(2,1)S(1)}, bf16[128,384]{1,0:T(8,128)(2,1)S(1)}, u32[]{:S(2)}, u32[]{:S(2)}) collective-permute-start(bf16[128,384]{1,0:T(8,128)(2,1)S(1)} %get-tuple-element.35), channel_id=1, source_target_pairs={{0,2},{1,3},{2,0},{3,1},{4,6},{5,7},{6,4},{7,5},{8,10},{9,11},{10,... | collective-permute-start | bytes 294920 | tf_op jit(solution)/shard_map/ppermute | solution.py:201
  145.9 3.2 %collective-permute-start.10 = (bf16[128,384]{1,0:T(8,128)(2,1)S(1)}, bf16[128,384]{1,0:T(8,128)(2,1)S(1)}, u32[]{:S(2)}, u32[]{:S(2)}) collective-permute-start(bf16[128,384]{1,0:T(8,128)(2,1)S(1)} %get-tuple-element.36), channel_id=1, source_target_pairs={{0,4},{1,5},{2,6},{3,7},{4,0},{5,1},{6,2},{7,3},{8,12},{9,13},{10,... | collective-permute-start | bytes 294920 | tf_op jit(solution)/shard_map/ppermute | solution.py:201
  149.2 4.4 %collective-permute-start.11 = (bf16[128,384]{1,0:T(8,128)(2,1)S(1)}, bf16[128,384]{1,0:T(8,128)(2,1)S(1)}, u32[]{:S(2)}, u32[]{:S(2)}) collective-permute-start(bf16[128,384]{1,0:T(8,128)(2,1)S(1)} %get-tuple-element.37), channel_id=1, source_target_pairs={{0,8},{1,9},{2,10},{3,11},{4,12},{5,13},{6,14},{7,15},{8,0},{9,1},... | collective-permute-start | bytes 294920 | tf_op jit(solution)/shard_map/ppermute | solution.py:201
  153.6 2.5 %collective-permute-done.11.refs_3_ = bf16[128,384]{1,0:T(8,128)(2,1)S(1)} collective-permute-done((bf16[128,384]{1,0:T(8,128)(2,1)S(1)}, bf16[128,384]{1,0:T(8,128)(2,1)S(1)}, u32[]{:S(2)}, u32[]{:S(2)}) %collective-permute-start.11) | collective-permute-done | bytes 98336 | tf_op jit(solution)/shard_map/ppermute | solution.py:201
  156.7 2.3 %shard_map.95 = bf16[128,384]{1,0:T(8,128)(2,1)} custom-call(s32[3,2,5]{2,1,0:T(2,128)S(1)} %bitcast.22, bf16[30,128,128]{2,1,0:T(8,128)(2,1)S(1)} %bitcast.17, bf16[128,768]{1,0:T(8,128)(2,1)S(1)} %get-tuple-element.31.refs_0_, bf16[128,768]{1,0:T(8,128)(2,1)} %collective-permute-done.4.refs_1_, bf16[128,768]{1,0:T(8,128)(2,1)} %collective-permute-done.5.refs_2_, ...), custom_call_target="tpu_custom_call" | custom-call | tf_op jit(solution)/shard_map/pallas_call | solution.py:48
  159.0 1.4 shard_map.104
  (34 shorter events, 3.4 us)
Async XLA Ops:
  0.6 0.7 copy-start.7
  0.6 33.1 %copy-start = (bf16[1,5,6,128,128]{4,3,2,1,0:T(8,128)(2,1)S(1)}, bf16[1,5,6,128,128]{4,3,2,1,0:T(8,128)(2,1)}, u32[]{:S(2)}) copy-start(bf16[1,5,6,128,128]{4,3,2,1,0:T(8,128)(2,1)} %param.7) | copy-start | bytes 2949124
  1.3 32.4 %copy-start.2 = (bf16[128,384]{1,0:T(8,128)(2,1)S(1)}, bf16[128,384]{1,0:T(8,128)(2,1)}, u32[]{:S(2)}) copy-start(bf16[128,384]{1,0:T(8,128)(2,1)} %refs_0_.1) | copy-start | bytes 294916
  3.3 30.4 %collective-permute-start = (bf16[128,1152]{1,0:T(8,128)(2,1)S(1)}, bf16[128,1152]{1,0:T(8,128)(2,1)S(1)}, u32[]{:S(2)}, u32[]{:S(2)}) collective-permute-start(bf16[128,1152]{1,0:T(8,128)(2,1)S(1)} %get-tuple-element.27), channel_id=1, source_target_pairs={{0,1},{1,0},{2,3},{3,2},{4,5},{5,4},{6,7},{7,6},{8,9},{9,8},{10,11... | collective-permute-start | bytes 884744 | tf_op jit(solution)/shard_map/ppermute | solution.py:201
  8.3 25.4 %collective-permute-start.1 = (bf16[128,1152]{1,0:T(8,128)(2,1)S(1)}, bf16[128,1152]{1,0:T(8,128)(2,1)S(1)}, u32[]{:S(2)}, u32[]{:S(2)}) collective-permute-start(bf16[128,1152]{1,0:T(8,128)(2,1)S(1)} %get-tuple-element.28), channel_id=1, source_target_pairs={{0,2},{1,3},{2,0},{3,1},{4,6},{5,7},{6,4},{7,5},{8,10},{9,11},{10,... | collective-permute-start | bytes 884744 | tf_op jit(solution)/shard_map/ppermute | solution.py:201
  14.0 19.7 %collective-permute-start.2 = (bf16[128,1152]{1,0:T(8,128)(2,1)S(1)}, bf16[128,1152]{1,0:T(8,128)(2,1)S(1)}, u32[]{:S(2)}, u32[]{:S(2)}) collective-permute-start(bf16[128,1152]{1,0:T(8,128)(2,1)S(1)} %get-tuple-element.29), channel_id=1, source_target_pairs={{0,4},{1,5},{2,6},{3,7},{4,0},{5,1},{6,2},{7,3},{8,12},{9,13},{10,... | collective-permute-start | bytes 884744 | tf_op jit(solution)/shard_map/ppermute | solution.py:201
  17.1 16.6 %copy-start.8 = (s32[1,5,6]{2,0,1:T(1,128)S(1)}, s32[1,5,6]{2,0,1:T(1,128)}, u32[]{:S(2)}) copy-start(s32[1,5,6]{2,0,1:T(1,128)} %param.8) | copy-start | bytes 364
  17.1 16.6 %collective-permute-start.3 = (bf16[128,1152]{1,0:T(8,128)(2,1)S(1)}, bf16[128,1152]{1,0:T(8,128)(2,1)S(1)}, u32[]{:S(2)}, u32[]{:S(2)}) collective-permute-start(bf16[128,1152]{1,0:T(8,128)(2,1)S(1)} %get-tuple-element.30), channel_id=1, source_target_pairs={{0,8},{1,9},{2,10},{3,11},{4,12},{5,13},{6,14},{7,15},{8,0},{9,1},... | collective-permute-start | bytes 884744 | tf_op jit(solution)/shard_map/ppermute | solution.py:201
  35.0 0.7 copy-start.3
  35.7 24.1 %collective-permute-start.4 = (bf16[128,768]{1,0:T(8,128)(2,1)S(1)}, bf16[128,768]{1,0:T(8,128)(2,1)}, u32[]{:S(2)}, u32[]{:S(2)}) collective-permute-start(bf16[128,768]{1,0:T(8,128)(2,1)S(1)} %get-tuple-element.31.refs_0_), channel_id=1, source_target_pairs={{0,1},{1,0},{2,3},{3,2},{4,5},{5,4},{6,7},{7,6},{8,9},{9,8},{10,11... | collective-permute-start | bytes 589832 | tf_op jit(solution)/shard_map/ppermute | solution.py:201
  37.6 22.2 %collective-permute-start.5 = (bf16[128,768]{1,0:T(8,128)(2,1)S(1)}, bf16[128,768]{1,0:T(8,128)(2,1)}, u32[]{:S(2)}, u32[]{:S(2)}) collective-permute-start(bf16[128,768]{1,0:T(8,128)(2,1)S(1)} %get-tuple-element.31.refs_0_), channel_id=1, source_target_pairs={{0,2},{1,3},{2,0},{3,1},{4,6},{5,7},{6,4},{7,5},{8,10},{9,11},{10,... | collective-permute-start | bytes 589832 | tf_op jit(solution)/shard_map/ppermute | solution.py:201
  46.0 13.7 %collective-permute-start.6 = (bf16[128,768]{1,0:T(8,128)(2,1)S(1)}, bf16[128,768]{1,0:T(8,128)(2,1)}, u32[]{:S(2)}, u32[]{:S(2)}) collective-permute-start(bf16[128,768]{1,0:T(8,128)(2,1)S(1)} %get-tuple-element.31.refs_0_), channel_id=1, source_target_pairs={{0,4},{1,5},{2,6},{3,7},{4,0},{5,1},{6,2},{7,3},{8,12},{9,13},{10,... | collective-permute-start | bytes 589832 | tf_op jit(solution)/shard_map/ppermute | solution.py:201
  49.2 10.9 %collective-permute-start.7 = (bf16[128,768]{1,0:T(8,128)(2,1)S(1)}, bf16[128,768]{1,0:T(8,128)(2,1)}, u32[]{:S(2)}, u32[]{:S(2)}) collective-permute-start(bf16[128,768]{1,0:T(8,128)(2,1)S(1)} %get-tuple-element.31.refs_0_), channel_id=1, source_target_pairs={{0,8},{1,9},{2,10},{3,11},{4,12},{5,13},{6,14},{7,15},{8,0},{9,1},... | collective-permute-start | bytes 589832 | tf_op jit(solution)/shard_map/ppermute | solution.py:201
  53.5 0.9 copy-start.4
  54.5 5.6 %copy-start.6 = (bf16[128,384]{1,0:T(8,128)(2,1)S(1)}, bf16[128,384]{1,0:T(8,128)(2,1)}, u32[]{:S(2)}) copy-start(bf16[128,384]{1,0:T(8,128)(2,1)} %cot.3) | copy-start | bytes 294916
  56.4 9.9 %collective-permute-start.12 = (bf16[15,128,128]{2,1,0:T(8,128)(2,1)}, bf16[15,128,128]{2,1,0:T(8,128)(2,1)}, u32[]{:S(2)}, u32[]{:S(2)}) collective-permute-start(bf16[15,128,128]{2,1,0:T(8,128)(2,1)} %get-tuple-element.39), channel_id=1, source_target_pairs={{0,16},{16,0},{32,48},{48,32},{64,80},{80,64},{96,112},{112,96},{1... | collective-permute-start | bytes 1474568 | tf_op jit(solution)/shard_map/ppermute | solution.py:201
  62.6 7.6 %collective-permute-start.14 = (bf16[15,128,128]{2,1,0:T(8,128)(2,1)}, bf16[15,128,128]{2,1,0:T(8,128)(2,1)}, u32[]{:S(2)}, u32[]{:S(2)}) collective-permute-start(bf16[15,128,128]{2,1,0:T(8,128)(2,1)} %get-tuple-element.43), channel_id=1, source_target_pairs={{0,16},{16,0},{32,48},{48,32},{64,80},{80,64},{96,112},{112,96},{1... | collective-permute-start | bytes 1474568 | tf_op jit(solution)/shard_map/ppermute | solution.py:201
  67.4 9.4 %collective-permute-start.13 = (bf16[8,120,128]{2,1,0:T(8,128)(2,1)S(1)}, bf16[8,120,128]{2,1,0:T(8,128)(2,1)S(1)}, u32[]{:S(2)}, u32[]{:S(2)}) collective-permute-start(bf16[8,120,128]{2,1,0:T(8,128)(2,1)S(1)} %get-tuple-element.41), channel_id=1, source_target_pairs={{0,256},{16,272},{32,288},{48,304},{64,320},{80,336},{96,352},{112... | collective-permute-start | bytes 737288 | tf_op jit(solution)/shard_map/ppermute | solution.py:201
  71.3 10.7 %collective-permute-start.15 = (bf16[8,120,128]{2,1,0:T(8,128)(2,1)S(1)}, bf16[8,120,128]{2,1,0:T(8,128)(2,1)S(1)}, u32[]{:S(2)}, u32[]{:S(2)}) collective-permute-start(bf16[8,120,128]{2,1,0:T(8,128)(2,1)S(1)} %get-tuple-element.45), channel_id=1, source_target_pairs={{0,256},{16,272},{32,288},{48,304},{64,320},{80,336},{96,352},{112... | collective-permute-start | bytes 737288 | tf_op jit(solution)/shard_map/ppermute | solution.py:201
  107.2 30.8 %copy-start.5 = (bf16[128,768]{1,0:T(8,128)(2,1)S(1)}, bf16[128,768]{1,0:T(8,128)(2,1)}, u32[]{:S(2)}) copy-start(bf16[128,768]{1,0:T(8,128)(2,1)} %copy-done.3) | copy-start | bytes 589828
  133.4 23.3 %copy-start.1 = (bf16[1,5,3,2,128,128]{5,4,3,2,1,0:T(8,128)(2,1)S(1)}, bf16[1,5,3,2,128,128]{5,4,3,2,1,0:T(8,128)(2,1)}, u32[]{:S(2)}) copy-start(bf16[1,5,3,2,128,128]{5,4,3,2,1,0:T(8,128)(2,1)} %param.9) | copy-start | bytes 2949124
  133.4 25.6 %collective-permute-start.16 = (bf16[16,240,128]{2,1,0:T(8,128)(2,1)S(1)}, bf16[16,240,128]{2,1,0:T(8,128)(2,1)S(1)}, u32[]{:S(2)}, u32[]{:S(2)}) collective-permute-start(bf16[16,240,128]{2,1,0:T(8,128)(2,1)S(1)} %all_to_all.11.mine), channel_id=1, source_target_pairs={{0,16},{16,0},{32,48},{48,32},{64,80},{80,64},{96,112},{112,96},{1... | collective-permute-start | bytes 2949128 | tf_op jit(solution)/shard_map/ppermute | solution.py:201
  139.5 14.0 %collective-permute-start.8 = (bf16[128,384]{1,0:T(8,128)(2,1)S(1)}, bf16[128,384]{1,0:T(8,128)(2,1)S(1)}, u32[]{:S(2)}, u32[]{:S(2)}) collective-permute-start(bf16[128,384]{1,0:T(8,128)(2,1)S(1)} %get-tuple-element.34), channel_id=1, source_target_pairs={{0,1},{1,0},{2,3},{3,2},{4,5},{5,4},{6,7},{7,6},{8,9},{9,8},{10,11... | collective-permute-start | bytes 294920 | tf_op jit(solution)/shard_map/ppermute | solution.py:201
  143.5 10.0 %collective-permute-start.9 = (bf16[128,384]{1,0:T(8,128)(2,1)S(1)}, bf16[128,384]{1,0:T(8,128)(2,1)S(1)}, u32[]{:S(2)}, u32[]{:S(2)}) collective-permute-start(bf16[128,384]{1,0:T(8,128)(2,1)S(1)} %get-tuple-element.35), channel_id=1, source_target_pairs={{0,2},{1,3},{2,0},{3,1},{4,6},{5,7},{6,4},{7,5},{8,10},{9,11},{10,... | collective-permute-start | bytes 294920 | tf_op jit(solution)/shard_map/ppermute | solution.py:201
  145.9 7.6 %collective-permute-start.10 = (bf16[128,384]{1,0:T(8,128)(2,1)S(1)}, bf16[128,384]{1,0:T(8,128)(2,1)S(1)}, u32[]{:S(2)}, u32[]{:S(2)}) collective-permute-start(bf16[128,384]{1,0:T(8,128)(2,1)S(1)} %get-tuple-element.36), channel_id=1, source_target_pairs={{0,4},{1,5},{2,6},{3,7},{4,0},{5,1},{6,2},{7,3},{8,12},{9,13},{10,... | collective-permute-start | bytes 294920 | tf_op jit(solution)/shard_map/ppermute | solution.py:201
  149.2 6.9 %collective-permute-start.11 = (bf16[128,384]{1,0:T(8,128)(2,1)S(1)}, bf16[128,384]{1,0:T(8,128)(2,1)S(1)}, u32[]{:S(2)}, u32[]{:S(2)}) collective-permute-start(bf16[128,384]{1,0:T(8,128)(2,1)S(1)} %get-tuple-element.37), channel_id=1, source_target_pairs={{0,8},{1,9},{2,10},{3,11},{4,12},{5,13},{6,14},{7,15},{8,0},{9,1},... | collective-permute-start | bytes 294920 | tf_op jit(solution)/shard_map/ppermute | solution.py:201

commit v7 on v6

--- a/solution.py
+++ b/solution.py
@@ -218,10 +218,14 @@
     core = lax.rem(lax.axis_index("dp"), 2).reshape(1)
     row = lax.div(lax.axis_index("dp"), chips).reshape(1)
     deep_z = chips // 2
-    chip_groups = [[2 * i + c for i in range(chips)] for c in range(2)]
-    column_groups = [
-        [chips * r + 2 * i + c for i in range(deep_z)] for r in range(2) for c in range(2)
-    ]
+    turn = sorted(range(deep_z), key=lambda z: f"{z:08b}"[::-1])
+    column_groups = {
+        (r, c): [chips * r + 2 * ((z + c * deep_z // 2) % deep_z) + c for z in turn]
+        for r in range(2)
+        for c in range(2)
+    }
+    chip_groups = [column_groups[0, c] + column_groups[1, c] for c in range(2)]
+    column_groups = list(column_groups.values())
     row_bit = dp.bit_length() - 2
 
     def over_mp(blocks):

time: 163 us -> 163 us (level)
  blocking collectives: 51.2 us -> 52.9 us
    all_to_all x2, blocking collectives: 51.2 us -> 52.9 us  [exchange(): lax.all_to_all(block, 'dp', split_axis=0, concat_axis=0, axis_index_group...]
where the time goes in v7:
time: 163 us; the launch traced here: 161 us
  starting transfers between devices  66.1 us (41%)
  blocking collectives  52.9 us (32%)
  waiting for transfers between devices  23.2 us (14%)
  Pallas kernels  15.9 us (10%)
  local copies, waits for them, and re-layouts  2.28 us (1%)
    ppermute x17, starting transfers between devices, from_partner(): return lax.ppermute(block, axis, [(i, i ^ 1 << bit) for i in range(count)])  66.1 us
    all_to_all x2, blocking collectives, exchange(): lax.all_to_all(block, 'dp', split_axis=0, concat_axis=0, axis_index_group...  52.9 us
    ppermute x17, waiting for transfers between devices, from_partner(): return lax.ppermute(block, axis, [(i, i ^ 1 << bit) for i in range(count)])  23.2 us
    pallas_call x12, Pallas kernels, invoke(): return run(*placed)  15.9 us
  transfers between devices with their start and end apart: 17, of which 5 were waited for; matrix products, arithmetic and copies ran while one was open for 0% of the time, Pallas kernels for 7%

profile of v7, /device:TPU:1, one launch (start us, length us, event | category | flops | bytes accessed | tf_op | source)
XLA Modules:
  0.0 161.3 jit_solution(415767253280752839)
XLA Ops:
  1.3 2.0 %shard_map.93 = (f32[128,768]{1,0:T(8,128)S(1)}, bf16[128,1152]{1,0:T(8,128)(2,1)S(1)}, bf16[128,1152]{1,0:T(8,128)(2,1)S(1)}, bf16[128,1152]{1,0:T(8,128)(2,1)S(1)}, bf16[128,1152]{1,0:T(8,128)(2,1)S(1)}) custom-call(s32[3,2,5]{2,1,0:T(2,128)S(1)} %bitcast.20, bf16[128,384]{1,0:T(8,128)(2,1)} %cot.3, bf16[30,128,128]{2,1,0:T(8,128)(2,1)} %bitcast.16, ...), custom_call_target="tpu_custom_call" | custom-call | tf_op jit(solution)/shard_map/pallas_call | solution.py:48
  3.3 5.0 %collective-permute-start = (bf16[128,1152]{1,0:T(8,128)(2,1)S(1)}, bf16[128,1152]{1,0:T(8,128)(2,1)S(1)}, u32[]{:S(2)}, u32[]{:S(2)}) collective-permute-start(bf16[128,1152]{1,0:T(8,128)(2,1)S(1)} %get-tuple-element.27), channel_id=1, source_target_pairs={{0,1},{1,0},{2,3},{3,2},{4,5},{5,4},{6,7},{7,6},{8,9},{9,8},{10,11... | collective-permute-start | bytes 884744 | tf_op jit(solution)/shard_map/ppermute | solution.py:201
  8.3 5.7 %collective-permute-start.1 = (bf16[128,1152]{1,0:T(8,128)(2,1)S(1)}, bf16[128,1152]{1,0:T(8,128)(2,1)S(1)}, u32[]{:S(2)}, u32[]{:S(2)}) collective-permute-start(bf16[128,1152]{1,0:T(8,128)(2,1)S(1)} %get-tuple-element.28), channel_id=1, source_target_pairs={{0,2},{1,3},{2,0},{3,1},{4,6},{5,7},{6,4},{7,5},{8,10},{9,11},{10,... | collective-permute-start | bytes 884744 | tf_op jit(solution)/shard_map/ppermute | solution.py:201
  14.0 3.1 %collective-permute-start.2 = (bf16[128,1152]{1,0:T(8,128)(2,1)S(1)}, bf16[128,1152]{1,0:T(8,128)(2,1)S(1)}, u32[]{:S(2)}, u32[]{:S(2)}) collective-permute-start(bf16[128,1152]{1,0:T(8,128)(2,1)S(1)} %get-tuple-element.29), channel_id=1, source_target_pairs={{0,4},{1,5},{2,6},{3,7},{4,0},{5,1},{6,2},{7,3},{8,12},{9,13},{10,... | collective-permute-start | bytes 884744 | tf_op jit(solution)/shard_map/ppermute | solution.py:201
  17.1 4.4 %collective-permute-start.3 = (bf16[128,1152]{1,0:T(8,128)(2,1)S(1)}, bf16[128,1152]{1,0:T(8,128)(2,1)S(1)}, u32[]{:S(2)}, u32[]{:S(2)}) collective-permute-start(bf16[128,1152]{1,0:T(8,128)(2,1)S(1)} %get-tuple-element.30), channel_id=1, source_target_pairs={{0,8},{1,9},{2,10},{3,11},{4,12},{5,13},{6,14},{7,15},{8,0},{9,1},... | collective-permute-start | bytes 884744 | tf_op jit(solution)/shard_map/ppermute | solution.py:201
  21.5 12.2 %collective-permute-done.refs_0_.refs_1_ = bf16[128,1152]{1,0:T(8,128)(2,1)S(1)} collective-permute-done((bf16[128,1152]{1,0:T(8,128)(2,1)S(1)}, bf16[128,1152]{1,0:T(8,128)(2,1)S(1)}, u32[]{:S(2)}, u32[]{:S(2)}) %collective-permute-start) | collective-permute-done | bytes 294944 | tf_op jit(solution)/shard_map/ppermute | solution.py:201
  33.7 1.2 shard_map.94
  35.7 1.9 %collective-permute-start.4 = (bf16[128,768]{1,0:T(8,128)(2,1)S(1)}, bf16[128,768]{1,0:T(8,128)(2,1)}, u32[]{:S(2)}, u32[]{:S(2)}) collective-permute-start(bf16[128,768]{1,0:T(8,128)(2,1)S(1)} %get-tuple-element.31.refs_0_), channel_id=1, source_target_pairs={{0,1},{1,0},{2,3},{3,2},{4,5},{5,4},{6,7},{7,6},{8,9},{9,8},{10,11... | collective-permute-start | bytes 589832 | tf_op jit(solution)/shard_map/ppermute | solution.py:201
  37.6 8.4 %collective-permute-start.5 = (bf16[128,768]{1,0:T(8,128)(2,1)S(1)}, bf16[128,768]{1,0:T(8,128)(2,1)}, u32[]{:S(2)}, u32[]{:S(2)}) collective-permute-start(bf16[128,768]{1,0:T(8,128)(2,1)S(1)} %get-tuple-element.31.refs_0_), channel_id=1, source_target_pairs={{0,2},{1,3},{2,0},{3,1},{4,6},{5,7},{6,4},{7,5},{8,10},{9,11},{10,... | collective-permute-start | bytes 589832 | tf_op jit(solution)/shard_map/ppermute | solution.py:201
  46.0 3.1 %collective-permute-start.6 = (bf16[128,768]{1,0:T(8,128)(2,1)S(1)}, bf16[128,768]{1,0:T(8,128)(2,1)}, u32[]{:S(2)}, u32[]{:S(2)}) collective-permute-start(bf16[128,768]{1,0:T(8,128)(2,1)S(1)} %get-tuple-element.31.refs_0_), channel_id=1, source_target_pairs={{0,4},{1,5},{2,6},{3,7},{4,0},{5,1},{6,2},{7,3},{8,12},{9,13},{10,... | collective-permute-start | bytes 589832 | tf_op jit(solution)/shard_map/ppermute | solution.py:201
  49.2 4.4 %collective-permute-start.7 = (bf16[128,768]{1,0:T(8,128)(2,1)S(1)}, bf16[128,768]{1,0:T(8,128)(2,1)}, u32[]{:S(2)}, u32[]{:S(2)}) collective-permute-start(bf16[128,768]{1,0:T(8,128)(2,1)S(1)} %get-tuple-element.31.refs_0_), channel_id=1, source_target_pairs={{0,8},{1,9},{2,10},{3,11},{4,12},{5,13},{6,14},{7,15},{8,0},{9,1},... | collective-permute-start | bytes 589832 | tf_op jit(solution)/shard_map/ppermute | solution.py:201
  54.5 1.9 %shard_map.98 = (f32[15,128,128]{2,1,0:T(8,128)S(1)}, bf16[15,128,128]{2,1,0:T(8,128)(2,1)}) custom-call(s32[5,1,6]{2,1,0:T(1,128)S(1)} %bitcast.24, s32[1]{0:T(128)} %bitcast.6.core, bf16[128,768]{1,0:T(8,128)(2,1)S(1)} %copy-done.4, bf16[128,384]{1,0:T(8,128)(2,1)S(1)} %copy-done.2, bf16[128,1152]{1,0:T(8,128)(2,1)S(1)} %collective-permute-done.refs_0_.refs_1_, ...), custom_call_target="tpu_custom_call" | custom-call | tf_op jit(solution)/shard_map/pallas_call | solution.py:48
  56.4 3.3 %collective-permute-start.12 = (bf16[15,128,128]{2,1,0:T(8,128)(2,1)}, bf16[15,128,128]{2,1,0:T(8,128)(2,1)}, u32[]{:S(2)}, u32[]{:S(2)}) collective-permute-start(bf16[15,128,128]{2,1,0:T(8,128)(2,1)} %get-tuple-element.39), channel_id=1, source_target_pairs={{0,16},{16,0},{32,48},{48,32},{64,80},{80,64},{96,112},{112,96},{1... | collective-permute-start | bytes 1474568 | tf_op jit(solution)/shard_map/ppermute | solution.py:201
  60.0 2.6 %shard_map.100 = (f32[15,128,128]{2,1,0:T(8,128)S(1)}, bf16[15,128,128]{2,1,0:T(8,128)(2,1)}) custom-call(s32[3,2,5]{2,1,0:T(2,128)S(1)} %bitcast.21, s32[1]{0:T(128)} %bitcast.6.core, bf16[128,384]{1,0:T(8,128)(2,1)S(1)} %copy-done.6, bf16[128,768]{1,0:T(8,128)(2,1)S(1)} %get-tuple-element.31.refs_0_, bf16[128,768]{1,0:T(8,128)(2,1)} %collective-permute-done.4.refs_1_, ...), custom_call_target="tpu_custom_call" | custom-call | tf_op jit(solution)/shard_map/pallas_call | solution.py:48
  62.6 3.6 %collective-permute-start.14 = (bf16[15,128,128]{2,1,0:T(8,128)(2,1)}, bf16[15,128,128]{2,1,0:T(8,128)(2,1)}, u32[]{:S(2)}, u32[]{:S(2)}) collective-permute-start(bf16[15,128,128]{2,1,0:T(8,128)(2,1)} %get-tuple-element.43), channel_id=1, source_target_pairs={{0,16},{16,0},{32,48},{48,32},{64,80},{80,64},{96,112},{112,96},{1... | collective-permute-start | bytes 1474568 | tf_op jit(solution)/shard_map/ppermute | solution.py:201
  66.3 1.1 shard_map.99
  67.4 2.8 %collective-permute-start.13 = (bf16[8,120,128]{2,1,0:T(8,128)(2,1)S(1)}, bf16[8,120,128]{2,1,0:T(8,128)(2,1)S(1)}, u32[]{:S(2)}, u32[]{:S(2)}) collective-permute-start(bf16[8,120,128]{2,1,0:T(8,128)(2,1)S(1)} %get-tuple-element.41), channel_id=1, source_target_pairs={{0,256},{16,272},{32,288},{48,304},{64,320},{80,336},{96,352},{112... | collective-permute-start | bytes 737288 | tf_op jit(solution)/shard_map/ppermute | solution.py:201
  70.2 1.1 shard_map.101
  71.3 2.5 %collective-permute-start.15 = (bf16[8,120,128]{2,1,0:T(8,128)(2,1)S(1)}, bf16[8,120,128]{2,1,0:T(8,128)(2,1)S(1)}, u32[]{:S(2)}, u32[]{:S(2)}) collective-permute-start(bf16[8,120,128]{2,1,0:T(8,128)(2,1)S(1)} %get-tuple-element.45), channel_id=1, source_target_pairs={{0,256},{16,272},{32,288},{48,304},{64,320},{80,336},{96,352},{112... | collective-permute-start | bytes 737288 | tf_op jit(solution)/shard_map/ppermute | solution.py:201
  73.8 3.0 %collective-permute-done.13.refs_1_ = bf16[8,120,128]{2,1,0:T(8,128)(2,1)S(1)} collective-permute-done((bf16[8,120,128]{2,1,0:T(8,128)(2,1)S(1)}, bf16[8,120,128]{2,1,0:T(8,128)(2,1)S(1)}, u32[]{:S(2)}, u32[]{:S(2)}) %collective-permute-start.13) | collective-permute-done | bytes 245792 | tf_op jit(solution)/shard_map/ppermute | solution.py:201
  76.8 5.3 %collective-permute-done.15.refs_3_ = bf16[8,120,128]{2,1,0:T(8,128)(2,1)S(1)} collective-permute-done((bf16[8,120,128]{2,1,0:T(8,128)(2,1)S(1)}, bf16[8,120,128]{2,1,0:T(8,128)(2,1)S(1)}, u32[]{:S(2)}, u32[]{:S(2)}) %collective-permute-start.15) | collective-permute-done | bytes 245792 | tf_op jit(solution)/shard_map/ppermute | solution.py:201
  82.1 24.2 %all_to_all.10.parts = bf16[8,240,128]{2,1,0:T(8,128)(2,1)S(1)} all-to-all(bf16[8,240,128]{2,1,0:T(8,128)(2,1)S(1)} %shard_map.102), channel_id=1, replica_groups={{0,128,64,192,32,160,96,224},{144,16,208,80,176,48,240,112},{256,384,32..., dimensions={0} | all-to-all | bytes 983040 | tf_op jit(solution)/shard_map/all_to_all | solution.py:235
  106.4 28.7 %all_to_all.11.mine = bf16[16,240,128]{2,1,0:T(8,128)(2,1)S(1)} all-to-all(bf16[16,240,128]{2,1,0:T(8,128)(2,1)S(1)} %shard_map.103), channel_id=1, replica_groups={{0,128,64,192,32,160,96,224,256,384,320,448,288,416,352,480},{144,16,20..., dimensions={0} | all-to-all | bytes 1966080 | tf_op jit(solution)/shard_map/all_to_all | solution.py:235
  135.1 3.9 %collective-permute-start.16 = (bf16[16,240,128]{2,1,0:T(8,128)(2,1)S(1)}, bf16[16,240,128]{2,1,0:T(8,128)(2,1)S(1)}, u32[]{:S(2)}, u32[]{:S(2)}) collective-permute-start(bf16[16,240,128]{2,1,0:T(8,128)(2,1)S(1)} %all_to_all.11.mine), channel_id=1, source_target_pairs={{0,16},{16,0},{32,48},{48,32},{64,80},{80,64},{96,112},{112,96},{1... | collective-permute-start | bytes 2949128 | tf_op jit(solution)/shard_map/ppermute | solution.py:201
  139.0 1.4 shard_map.96
  140.4 3.7 %collective-permute-start.8 = (bf16[128,384]{1,0:T(8,128)(2,1)S(1)}, bf16[128,384]{1,0:T(8,128)(2,1)S(1)}, u32[]{:S(2)}, u32[]{:S(2)}) collective-permute-start(bf16[128,384]{1,0:T(8,128)(2,1)S(1)} %get-tuple-element.34), channel_id=1, source_target_pairs={{0,1},{1,0},{2,3},{3,2},{4,5},{5,4},{6,7},{7,6},{8,9},{9,8},{10,11... | collective-permute-start | bytes 294920 | tf_op jit(solution)/shard_map/ppermute | solution.py:201
  144.1 2.7 %collective-permute-start.9 = (bf16[128,384]{1,0:T(8,128)(2,1)S(1)}, bf16[128,384]{1,0:T(8,128)(2,1)S(1)}, u32[]{:S(2)}, u32[]{:S(2)}) collective-permute-start(bf16[128,384]{1,0:T(8,128)(2,1)S(1)} %get-tuple-element.35), channel_id=1, source_target_pairs={{0,2},{1,3},{2,0},{3,1},{4,6},{5,7},{6,4},{7,5},{8,10},{9,11},{10,... | collective-permute-start | bytes 294920 | tf_op jit(solution)/shard_map/ppermute | solution.py:201
  146.8 3.3 %collective-permute-start.10 = (bf16[128,384]{1,0:T(8,128)(2,1)S(1)}, bf16[128,384]{1,0:T(8,128)(2,1)S(1)}, u32[]{:S(2)}, u32[]{:S(2)}) collective-permute-start(bf16[128,384]{1,0:T(8,128)(2,1)S(1)} %get-tuple-element.36), channel_id=1, source_target_pairs={{0,4},{1,5},{2,6},{3,7},{4,0},{5,1},{6,2},{7,3},{8,12},{9,13},{10,... | collective-permute-start | bytes 294920 | tf_op jit(solution)/shard_map/ppermute | solution.py:201
  150.1 4.3 %collective-permute-start.11 = (bf16[128,384]{1,0:T(8,128)(2,1)S(1)}, bf16[128,384]{1,0:T(8,128)(2,1)S(1)}, u32[]{:S(2)}, u32[]{:S(2)}) collective-permute-start(bf16[128,384]{1,0:T(8,128)(2,1)S(1)} %get-tuple-element.37), channel_id=1, source_target_pairs={{0,8},{1,9},{2,10},{3,11},{4,12},{5,13},{6,14},{7,15},{8,0},{9,1},... | collective-permute-start | bytes 294920 | tf_op jit(solution)/shard_map/ppermute | solution.py:201
  154.5 2.5 %collective-permute-done.11.refs_3_ = bf16[128,384]{1,0:T(8,128)(2,1)S(1)} collective-permute-done((bf16[128,384]{1,0:T(8,128)(2,1)S(1)}, bf16[128,384]{1,0:T(8,128)(2,1)S(1)}, u32[]{:S(2)}, u32[]{:S(2)}) %collective-permute-start.11) | collective-permute-done | bytes 98336 | tf_op jit(solution)/shard_map/ppermute | solution.py:201
  157.6 2.3 %shard_map.95 = bf16[128,384]{1,0:T(8,128)(2,1)} custom-call(s32[3,2,5]{2,1,0:T(2,128)S(1)} %bitcast.22, bf16[30,128,128]{2,1,0:T(8,128)(2,1)S(1)} %bitcast.17, bf16[128,768]{1,0:T(8,128)(2,1)S(1)} %get-tuple-element.31.refs_0_, bf16[128,768]{1,0:T(8,128)(2,1)} %collective-permute-done.4.refs_1_, bf16[128,768]{1,0:T(8,128)(2,1)} %collective-permute-done.5.refs_2_, ...), custom_call_target="tpu_custom_call" | custom-call | tf_op jit(solution)/shard_map/pallas_call | solution.py:48
  159.9 1.4 shard_map.104
  (34 shorter events, 3.4 us)
Async XLA Ops:
  0.6 0.7 copy-start.7
  0.6 33.1 %copy-start = (bf16[1,5,6,128,128]{4,3,2,1,0:T(8,128)(2,1)S(1)}, bf16[1,5,6,128,128]{4,3,2,1,0:T(8,128)(2,1)}, u32[]{:S(2)}) copy-start(bf16[1,5,6,128,128]{4,3,2,1,0:T(8,128)(2,1)} %param.7) | copy-start | bytes 2949124
  1.3 32.4 %copy-start.2 = (bf16[128,384]{1,0:T(8,128)(2,1)S(1)}, bf16[128,384]{1,0:T(8,128)(2,1)}, u32[]{:S(2)}) copy-start(bf16[128,384]{1,0:T(8,128)(2,1)} %refs_0_.1) | copy-start | bytes 294916
  3.3 30.4 %collective-permute-start = (bf16[128,1152]{1,0:T(8,128)(2,1)S(1)}, bf16[128,1152]{1,0:T(8,128)(2,1)S(1)}, u32[]{:S(2)}, u32[]{:S(2)}) collective-permute-start(bf16[128,1152]{1,0:T(8,128)(2,1)S(1)} %get-tuple-element.27), channel_id=1, source_target_pairs={{0,1},{1,0},{2,3},{3,2},{4,5},{5,4},{6,7},{7,6},{8,9},{9,8},{10,11... | collective-permute-start | bytes 884744 | tf_op jit(solution)/shard_map/ppermute | solution.py:201
  8.3 25.4 %collective-permute-start.1 = (bf16[128,1152]{1,0:T(8,128)(2,1)S(1)}, bf16[128,1152]{1,0:T(8,128)(2,1)S(1)}, u32[]{:S(2)}, u32[]{:S(2)}) collective-permute-start(bf16[128,1152]{1,0:T(8,128)(2,1)S(1)} %get-tuple-element.28), channel_id=1, source_target_pairs={{0,2},{1,3},{2,0},{3,1},{4,6},{5,7},{6,4},{7,5},{8,10},{9,11},{10,... | collective-permute-start | bytes 884744 | tf_op jit(solution)/shard_map/ppermute | solution.py:201
  14.0 19.7 %collective-permute-start.2 = (bf16[128,1152]{1,0:T(8,128)(2,1)S(1)}, bf16[128,1152]{1,0:T(8,128)(2,1)S(1)}, u32[]{:S(2)}, u32[]{:S(2)}) collective-permute-start(bf16[128,1152]{1,0:T(8,128)(2,1)S(1)} %get-tuple-element.29), channel_id=1, source_target_pairs={{0,4},{1,5},{2,6},{3,7},{4,0},{5,1},{6,2},{7,3},{8,12},{9,13},{10,... | collective-permute-start | bytes 884744 | tf_op jit(solution)/shard_map/ppermute | solution.py:201
  17.1 16.6 %copy-start.8 = (s32[1,5,6]{2,0,1:T(1,128)S(1)}, s32[1,5,6]{2,0,1:T(1,128)}, u32[]{:S(2)}) copy-start(s32[1,5,6]{2,0,1:T(1,128)} %param.8) | copy-start | bytes 364
  17.1 16.6 %collective-permute-start.3 = (bf16[128,1152]{1,0:T(8,128)(2,1)S(1)}, bf16[128,1152]{1,0:T(8,128)(2,1)S(1)}, u32[]{:S(2)}, u32[]{:S(2)}) collective-permute-start(bf16[128,1152]{1,0:T(8,128)(2,1)S(1)} %get-tuple-element.30), channel_id=1, source_target_pairs={{0,8},{1,9},{2,10},{3,11},{4,12},{5,13},{6,14},{7,15},{8,0},{9,1},... | collective-permute-start | bytes 884744 | tf_op jit(solution)/shard_map/ppermute | solution.py:201
  35.0 0.7 copy-start.3
  35.7 24.1 %collective-permute-start.4 = (bf16[128,768]{1,0:T(8,128)(2,1)S(1)}, bf16[128,768]{1,0:T(8,128)(2,1)}, u32[]{:S(2)}, u32[]{:S(2)}) collective-permute-start(bf16[128,768]{1,0:T(8,128)(2,1)S(1)} %get-tuple-element.31.refs_0_), channel_id=1, source_target_pairs={{0,1},{1,0},{2,3},{3,2},{4,5},{5,4},{6,7},{7,6},{8,9},{9,8},{10,11... | collective-permute-start | bytes 589832 | tf_op jit(solution)/shard_map/ppermute | solution.py:201
  37.6 22.2 %collective-permute-start.5 = (bf16[128,768]{1,0:T(8,128)(2,1)S(1)}, bf16[128,768]{1,0:T(8,128)(2,1)}, u32[]{:S(2)}, u32[]{:S(2)}) collective-permute-start(bf16[128,768]{1,0:T(8,128)(2,1)S(1)} %get-tuple-element.31.refs_0_), channel_id=1, source_target_pairs={{0,2},{1,3},{2,0},{3,1},{4,6},{5,7},{6,4},{7,5},{8,10},{9,11},{10,... | collective-permute-start | bytes 589832 | tf_op jit(solution)/shard_map/ppermute | solution.py:201
  46.0 13.7 %collective-permute-start.6 = (bf16[128,768]{1,0:T(8,128)(2,1)S(1)}, bf16[128,768]{1,0:T(8,128)(2,1)}, u32[]{:S(2)}, u32[]{:S(2)}) collective-permute-start(bf16[128,768]{1,0:T(8,128)(2,1)S(1)} %get-tuple-element.31.refs_0_), channel_id=1, source_target_pairs={{0,4},{1,5},{2,6},{3,7},{4,0},{5,1},{6,2},{7,3},{8,12},{9,13},{10,... | collective-permute-start | bytes 589832 | tf_op jit(solution)/shard_map/ppermute | solution.py:201
  49.2 10.9 %collective-permute-start.7 = (bf16[128,768]{1,0:T(8,128)(2,1)S(1)}, bf16[128,768]{1,0:T(8,128)(2,1)}, u32[]{:S(2)}, u32[]{:S(2)}) collective-permute-start(bf16[128,768]{1,0:T(8,128)(2,1)S(1)} %get-tuple-element.31.refs_0_), channel_id=1, source_target_pairs={{0,8},{1,9},{2,10},{3,11},{4,12},{5,13},{6,14},{7,15},{8,0},{9,1},... | collective-permute-start | bytes 589832 | tf_op jit(solution)/shard_map/ppermute | solution.py:201
  53.5 0.9 copy-start.4
  54.5 5.6 %copy-start.6 = (bf16[128,384]{1,0:T(8,128)(2,1)S(1)}, bf16[128,384]{1,0:T(8,128)(2,1)}, u32[]{:S(2)}) copy-start(bf16[128,384]{1,0:T(8,128)(2,1)} %cot.3) | copy-start | bytes 294916
  56.4 9.9 %collective-permute-start.12 = (bf16[15,128,128]{2,1,0:T(8,128)(2,1)}, bf16[15,128,128]{2,1,0:T(8,128)(2,1)}, u32[]{:S(2)}, u32[]{:S(2)}) collective-permute-start(bf16[15,128,128]{2,1,0:T(8,128)(2,1)} %get-tuple-element.39), channel_id=1, source_target_pairs={{0,16},{16,0},{32,48},{48,32},{64,80},{80,64},{96,112},{112,96},{1... | collective-permute-start | bytes 1474568 | tf_op jit(solution)/shard_map/ppermute | solution.py:201
  62.6 7.6 %collective-permute-start.14 = (bf16[15,128,128]{2,1,0:T(8,128)(2,1)}, bf16[15,128,128]{2,1,0:T(8,128)(2,1)}, u32[]{:S(2)}, u32[]{:S(2)}) collective-permute-start(bf16[15,128,128]{2,1,0:T(8,128)(2,1)} %get-tuple-element.43), channel_id=1, source_target_pairs={{0,16},{16,0},{32,48},{48,32},{64,80},{80,64},{96,112},{112,96},{1... | collective-permute-start | bytes 1474568 | tf_op jit(solution)/shard_map/ppermute | solution.py:201
  67.4 9.4 %collective-permute-start.13 = (bf16[8,120,128]{2,1,0:T(8,128)(2,1)S(1)}, bf16[8,120,128]{2,1,0:T(8,128)(2,1)S(1)}, u32[]{:S(2)}, u32[]{:S(2)}) collective-permute-start(bf16[8,120,128]{2,1,0:T(8,128)(2,1)S(1)} %get-tuple-element.41), channel_id=1, source_target_pairs={{0,256},{16,272},{32,288},{48,304},{64,320},{80,336},{96,352},{112... | collective-permute-start | bytes 737288 | tf_op jit(solution)/shard_map/ppermute | solution.py:201
  71.3 10.7 %collective-permute-start.15 = (bf16[8,120,128]{2,1,0:T(8,128)(2,1)S(1)}, bf16[8,120,128]{2,1,0:T(8,128)(2,1)S(1)}, u32[]{:S(2)}, u32[]{:S(2)}) collective-permute-start(bf16[8,120,128]{2,1,0:T(8,128)(2,1)S(1)} %get-tuple-element.45), channel_id=1, source_target_pairs={{0,256},{16,272},{32,288},{48,304},{64,320},{80,336},{96,352},{112... | collective-permute-start | bytes 737288 | tf_op jit(solution)/shard_map/ppermute | solution.py:201
  106.4 32.5 %copy-start.5 = (bf16[128,768]{1,0:T(8,128)(2,1)S(1)}, bf16[128,768]{1,0:T(8,128)(2,1)}, u32[]{:S(2)}) copy-start(bf16[128,768]{1,0:T(8,128)(2,1)} %copy-done.3) | copy-start | bytes 589828
  135.1 22.5 %copy-start.1 = (bf16[1,5,3,2,128,128]{5,4,3,2,1,0:T(8,128)(2,1)S(1)}, bf16[1,5,3,2,128,128]{5,4,3,2,1,0:T(8,128)(2,1)}, u32[]{:S(2)}) copy-start(bf16[1,5,3,2,128,128]{5,4,3,2,1,0:T(8,128)(2,1)} %param.9) | copy-start | bytes 2949124
  135.1 24.8 %collective-permute-start.16 = (bf16[16,240,128]{2,1,0:T(8,128)(2,1)S(1)}, bf16[16,240,128]{2,1,0:T(8,128)(2,1)S(1)}, u32[]{:S(2)}, u32[]{:S(2)}) collective-permute-start(bf16[16,240,128]{2,1,0:T(8,128)(2,1)S(1)} %all_to_all.11.mine), channel_id=1, source_target_pairs={{0,16},{16,0},{32,48},{48,32},{64,80},{80,64},{96,112},{112,96},{1... | collective-permute-start | bytes 2949128 | tf_op jit(solution)/shard_map/ppermute | solution.py:201
  140.4 14.0 %collective-permute-start.8 = (bf16[128,384]{1,0:T(8,128)(2,1)S(1)}, bf16[128,384]{1,0:T(8,128)(2,1)S(1)}, u32[]{:S(2)}, u32[]{:S(2)}) collective-permute-start(bf16[128,384]{1,0:T(8,128)(2,1)S(1)} %get-tuple-element.34), channel_id=1, source_target_pairs={{0,1},{1,0},{2,3},{3,2},{4,5},{5,4},{6,7},{7,6},{8,9},{9,8},{10,11... | collective-permute-start | bytes 294920 | tf_op jit(solution)/shard_map/ppermute | solution.py:201
  144.1 10.4 %collective-permute-start.9 = (bf16[128,384]{1,0:T(8,128)(2,1)S(1)}, bf16[128,384]{1,0:T(8,128)(2,1)S(1)}, u32[]{:S(2)}, u32[]{:S(2)}) collective-permute-start(bf16[128,384]{1,0:T(8,128)(2,1)S(1)} %get-tuple-element.35), channel_id=1, source_target_pairs={{0,2},{1,3},{2,0},{3,1},{4,6},{5,7},{6,4},{7,5},{8,10},{9,11},{10,... | collective-permute-start | bytes 294920 | tf_op jit(solution)/shard_map/ppermute | solution.py:201
  146.8 7.6 %collective-permute-start.10 = (bf16[128,384]{1,0:T(8,128)(2,1)S(1)}, bf16[128,384]{1,0:T(8,128)(2,1)S(1)}, u32[]{:S(2)}, u32[]{:S(2)}) collective-permute-start(bf16[128,384]{1,0:T(8,128)(2,1)S(1)} %get-tuple-element.36), channel_id=1, source_target_pairs={{0,4},{1,5},{2,6},{3,7},{4,0},{5,1},{6,2},{7,3},{8,12},{9,13},{10,... | collective-permute-start | bytes 294920 | tf_op jit(solution)/shard_map/ppermute | solution.py:201
  150.1 6.9 %collective-permute-start.11 = (bf16[128,384]{1,0:T(8,128)(2,1)S(1)}, bf16[128,384]{1,0:T(8,128)(2,1)S(1)}, u32[]{:S(2)}, u32[]{:S(2)}) collective-permute-start(bf16[128,384]{1,0:T(8,128)(2,1)S(1)} %get-tuple-element.37), channel_id=1, source_target_pairs={{0,8},{1,9},{2,10},{3,11},{4,12},{5,13},{6,14},{7,15},{8,0},{9,1},... | collective-permute-start | bytes 294920 | tf_op jit(solution)/shard_map/ppermute | solution.py:201

commit v8 on v6

--- a/solution.py
+++ b/solution.py
@@ -187,13 +187,15 @@
         out[i] = total
 
 
-def join_kernel(core, mine, other, *outs):
-    at = 0
-    for out in outs:
-        rows = out.shape[2]
-        out[core[0]] = mine[:, at : at + rows, :]
-        out[1 - core[0]] = other[:, at : at + rows, :]
-        at += rows
+def join_kernel(places, core, mine, other, *outs):
+    for half, source in ((core[0], mine), (1 - core[0], other)):
+        for p, (first, second) in enumerate(zip(*places)):
+            spot = jnp.where(half == 0, first, second)
+            at = 0
+            for out in outs:
+                rows = out.shape[2]
+                out[half, spot] = source[p, at : at + rows, :]
+                at += rows
 
 
 def from_partner(block, axis, bit):
@@ -218,9 +220,14 @@
     core = lax.rem(lax.axis_index("dp"), 2).reshape(1)
     row = lax.div(lax.axis_index("dp"), chips).reshape(1)
     deep_z = chips // 2
+    turn = sorted(range(deep_z), key=lambda z: f"{z:08b}"[::-1])
+    rings = [[(z + c * deep_z // 2) % deep_z for z in turn] for c in range(2)]
     chip_groups = [[2 * i + c for i in range(chips)] for c in range(2)]
     column_groups = [
-        [chips * r + 2 * i + c for i in range(deep_z)] for r in range(2) for c in range(2)
+        [chips * r + 2 * z + c for z in rings[c]] for r in range(2) for c in range(2)
+    ]
+    places = [
+        [r * deep_z + ring.index(z) for r in range(2) for z in range(deep_z)] for ring in rings
     ]
     row_bit = dp.bit_length() - 2
 
@@ -311,7 +318,10 @@
     mine = exchange(shard, chip_groups)
     other = from_partner(mine, "dp", 0)
     up_out, down_out = call(
-        join_kernel, [hbm((2, chips, r, B), BF16) for r in rows], [SMEM, VMEM, VMEM], ()
+        functools.partial(join_kernel, places),
+        [hbm((2, chips, r, B), BF16) for r in rows],
+        [SMEM, VMEM, VMEM],
+        (),
     )(core, mine, other)
     return (
         output,

time: 163 us -> 164 us (level)
  no operation moved by 1% of the time
where the time goes in v8:
time: 164 us; the launch traced here: 161 us
  starting transfers between devices  66.8 us (41%)
  blocking collectives  51.7 us (32%)
  waiting for transfers between devices  23.2 us (14%)
  Pallas kernels  16 us (10%)
  local copies, waits for them, and re-layouts  2.28 us (1%)
    ppermute x17, starting transfers between devices, from_partner(): return lax.ppermute(block, axis, [(i, i ^ 1 << bit) for i in range(count)])  66.8 us
    all_to_all x2, blocking collectives, exchange(): lax.all_to_all(block, 'dp', split_axis=0, concat_axis=0, axis_index_group...  51.7 us
    ppermute x17, waiting for transfers between devices, from_partner(): return lax.ppermute(block, axis, [(i, i ^ 1 << bit) for i in range(count)])  23.2 us
    pallas_call x12, Pallas kernels, invoke(): return run(*placed)  16 us
  transfers between devices with their start and end apart: 17, of which 5 were waited for; matrix products, arithmetic and copies ran while one was open for 0% of the time, Pallas kernels for 7%

profile of v8, /device:TPU:1, one launch (start us, length us, event | category | flops | bytes accessed | tf_op | source)
XLA Modules:
  0.0 160.9 jit_solution(6349222352874299241)
XLA Ops:
  1.3 2.0 %shard_map.93 = (f32[128,768]{1,0:T(8,128)S(1)}, bf16[128,1152]{1,0:T(8,128)(2,1)S(1)}, bf16[128,1152]{1,0:T(8,128)(2,1)S(1)}, bf16[128,1152]{1,0:T(8,128)(2,1)S(1)}, bf16[128,1152]{1,0:T(8,128)(2,1)S(1)}) custom-call(s32[3,2,5]{2,1,0:T(2,128)S(1)} %bitcast.20, bf16[128,384]{1,0:T(8,128)(2,1)} %cot.3, bf16[30,128,128]{2,1,0:T(8,128)(2,1)} %bitcast.16, ...), custom_call_target="tpu_custom_call" | custom-call | tf_op jit(solution)/shard_map/pallas_call | solution.py:48
  3.3 5.0 %collective-permute-start = (bf16[128,1152]{1,0:T(8,128)(2,1)S(1)}, bf16[128,1152]{1,0:T(8,128)(2,1)S(1)}, u32[]{:S(2)}, u32[]{:S(2)}) collective-permute-start(bf16[128,1152]{1,0:T(8,128)(2,1)S(1)} %get-tuple-element.27), channel_id=1, source_target_pairs={{0,1},{1,0},{2,3},{3,2},{4,5},{5,4},{6,7},{7,6},{8,9},{9,8},{10,11... | collective-permute-start | bytes 884744 | tf_op jit(solution)/shard_map/ppermute | solution.py:203
  8.3 5.7 %collective-permute-start.1 = (bf16[128,1152]{1,0:T(8,128)(2,1)S(1)}, bf16[128,1152]{1,0:T(8,128)(2,1)S(1)}, u32[]{:S(2)}, u32[]{:S(2)}) collective-permute-start(bf16[128,1152]{1,0:T(8,128)(2,1)S(1)} %get-tuple-element.28), channel_id=1, source_target_pairs={{0,2},{1,3},{2,0},{3,1},{4,6},{5,7},{6,4},{7,5},{8,10},{9,11},{10,... | collective-permute-start | bytes 884744 | tf_op jit(solution)/shard_map/ppermute | solution.py:203
  14.0 3.1 %collective-permute-start.2 = (bf16[128,1152]{1,0:T(8,128)(2,1)S(1)}, bf16[128,1152]{1,0:T(8,128)(2,1)S(1)}, u32[]{:S(2)}, u32[]{:S(2)}) collective-permute-start(bf16[128,1152]{1,0:T(8,128)(2,1)S(1)} %get-tuple-element.29), channel_id=1, source_target_pairs={{0,4},{1,5},{2,6},{3,7},{4,0},{5,1},{6,2},{7,3},{8,12},{9,13},{10,... | collective-permute-start | bytes 884744 | tf_op jit(solution)/shard_map/ppermute | solution.py:203
  17.1 4.4 %collective-permute-start.3 = (bf16[128,1152]{1,0:T(8,128)(2,1)S(1)}, bf16[128,1152]{1,0:T(8,128)(2,1)S(1)}, u32[]{:S(2)}, u32[]{:S(2)}) collective-permute-start(bf16[128,1152]{1,0:T(8,128)(2,1)S(1)} %get-tuple-element.30), channel_id=1, source_target_pairs={{0,8},{1,9},{2,10},{3,11},{4,12},{5,13},{6,14},{7,15},{8,0},{9,1},... | collective-permute-start | bytes 884744 | tf_op jit(solution)/shard_map/ppermute | solution.py:203
  21.5 12.2 %collective-permute-done.refs_0_.refs_1_ = bf16[128,1152]{1,0:T(8,128)(2,1)S(1)} collective-permute-done((bf16[128,1152]{1,0:T(8,128)(2,1)S(1)}, bf16[128,1152]{1,0:T(8,128)(2,1)S(1)}, u32[]{:S(2)}, u32[]{:S(2)}) %collective-permute-start) | collective-permute-done | bytes 294944 | tf_op jit(solution)/shard_map/ppermute | solution.py:203
  33.7 1.2 shard_map.94
  35.7 1.9 %collective-permute-start.4 = (bf16[128,768]{1,0:T(8,128)(2,1)S(1)}, bf16[128,768]{1,0:T(8,128)(2,1)}, u32[]{:S(2)}, u32[]{:S(2)}) collective-permute-start(bf16[128,768]{1,0:T(8,128)(2,1)S(1)} %get-tuple-element.31.refs_0_), channel_id=1, source_target_pairs={{0,1},{1,0},{2,3},{3,2},{4,5},{5,4},{6,7},{7,6},{8,9},{9,8},{10,11... | collective-permute-start | bytes 589832 | tf_op jit(solution)/shard_map/ppermute | solution.py:203
  37.6 8.4 %collective-permute-start.5 = (bf16[128,768]{1,0:T(8,128)(2,1)S(1)}, bf16[128,768]{1,0:T(8,128)(2,1)}, u32[]{:S(2)}, u32[]{:S(2)}) collective-permute-start(bf16[128,768]{1,0:T(8,128)(2,1)S(1)} %get-tuple-element.31.refs_0_), channel_id=1, source_target_pairs={{0,2},{1,3},{2,0},{3,1},{4,6},{5,7},{6,4},{7,5},{8,10},{9,11},{10,... | collective-permute-start | bytes 589832 | tf_op jit(solution)/shard_map/ppermute | solution.py:203
  46.0 3.1 %collective-permute-start.6 = (bf16[128,768]{1,0:T(8,128)(2,1)S(1)}, bf16[128,768]{1,0:T(8,128)(2,1)}, u32[]{:S(2)}, u32[]{:S(2)}) collective-permute-start(bf16[128,768]{1,0:T(8,128)(2,1)S(1)} %get-tuple-element.31.refs_0_), channel_id=1, source_target_pairs={{0,4},{1,5},{2,6},{3,7},{4,0},{5,1},{6,2},{7,3},{8,12},{9,13},{10,... | collective-permute-start | bytes 589832 | tf_op jit(solution)/shard_map/ppermute | solution.py:203
  49.2 4.4 %collective-permute-start.7 = (bf16[128,768]{1,0:T(8,128)(2,1)S(1)}, bf16[128,768]{1,0:T(8,128)(2,1)}, u32[]{:S(2)}, u32[]{:S(2)}) collective-permute-start(bf16[128,768]{1,0:T(8,128)(2,1)S(1)} %get-tuple-element.31.refs_0_), channel_id=1, source_target_pairs={{0,8},{1,9},{2,10},{3,11},{4,12},{5,13},{6,14},{7,15},{8,0},{9,1},... | collective-permute-start | bytes 589832 | tf_op jit(solution)/shard_map/ppermute | solution.py:203
  54.5 1.9 %shard_map.98 = (f32[15,128,128]{2,1,0:T(8,128)S(1)}, bf16[15,128,128]{2,1,0:T(8,128)(2,1)}) custom-call(s32[5,1,6]{2,1,0:T(1,128)S(1)} %bitcast.24, s32[1]{0:T(128)} %bitcast.6.core, bf16[128,768]{1,0:T(8,128)(2,1)S(1)} %copy-done.4, bf16[128,384]{1,0:T(8,128)(2,1)S(1)} %copy-done.2, bf16[128,1152]{1,0:T(8,128)(2,1)S(1)} %collective-permute-done.refs_0_.refs_1_, ...), custom_call_target="tpu_custom_call" | custom-call | tf_op jit(solution)/shard_map/pallas_call | solution.py:48
  56.4 3.3 %collective-permute-start.12 = (bf16[15,128,128]{2,1,0:T(8,128)(2,1)}, bf16[15,128,128]{2,1,0:T(8,128)(2,1)}, u32[]{:S(2)}, u32[]{:S(2)}) collective-permute-start(bf16[15,128,128]{2,1,0:T(8,128)(2,1)} %get-tuple-element.39), channel_id=1, source_target_pairs={{0,16},{16,0},{32,48},{48,32},{64,80},{80,64},{96,112},{112,96},{1... | collective-permute-start | bytes 1474568 | tf_op jit(solution)/shard_map/ppermute | solution.py:203
  60.0 2.6 %shard_map.100 = (f32[15,128,128]{2,1,0:T(8,128)S(1)}, bf16[15,128,128]{2,1,0:T(8,128)(2,1)}) custom-call(s32[3,2,5]{2,1,0:T(2,128)S(1)} %bitcast.21, s32[1]{0:T(128)} %bitcast.6.core, bf16[128,384]{1,0:T(8,128)(2,1)S(1)} %copy-done.6, bf16[128,768]{1,0:T(8,128)(2,1)S(1)} %get-tuple-element.31.refs_0_, bf16[128,768]{1,0:T(8,128)(2,1)} %collective-permute-done.4.refs_1_, ...), custom_call_target="tpu_custom_call" | custom-call | tf_op jit(solution)/shard_map/pallas_call | solution.py:48
  62.6 3.6 %collective-permute-start.14 = (bf16[15,128,128]{2,1,0:T(8,128)(2,1)}, bf16[15,128,128]{2,1,0:T(8,128)(2,1)}, u32[]{:S(2)}, u32[]{:S(2)}) collective-permute-start(bf16[15,128,128]{2,1,0:T(8,128)(2,1)} %get-tuple-element.43), channel_id=1, source_target_pairs={{0,16},{16,0},{32,48},{48,32},{64,80},{80,64},{96,112},{112,96},{1... | collective-permute-start | bytes 1474568 | tf_op jit(solution)/shard_map/ppermute | solution.py:203
  66.3 1.1 shard_map.99
  67.4 2.8 %collective-permute-start.13 = (bf16[8,120,128]{2,1,0:T(8,128)(2,1)S(1)}, bf16[8,120,128]{2,1,0:T(8,128)(2,1)S(1)}, u32[]{:S(2)}, u32[]{:S(2)}) collective-permute-start(bf16[8,120,128]{2,1,0:T(8,128)(2,1)S(1)} %get-tuple-element.41), channel_id=1, source_target_pairs={{0,256},{16,272},{32,288},{48,304},{64,320},{80,336},{96,352},{112... | collective-permute-start | bytes 737288 | tf_op jit(solution)/shard_map/ppermute | solution.py:203
  70.2 1.1 shard_map.101
  71.3 2.5 %collective-permute-start.15 = (bf16[8,120,128]{2,1,0:T(8,128)(2,1)S(1)}, bf16[8,120,128]{2,1,0:T(8,128)(2,1)S(1)}, u32[]{:S(2)}, u32[]{:S(2)}) collective-permute-start(bf16[8,120,128]{2,1,0:T(8,128)(2,1)S(1)} %get-tuple-element.45), channel_id=1, source_target_pairs={{0,256},{16,272},{32,288},{48,304},{64,320},{80,336},{96,352},{112... | collective-permute-start | bytes 737288 | tf_op jit(solution)/shard_map/ppermute | solution.py:203
  73.8 3.0 %collective-permute-done.13.refs_1_ = bf16[8,120,128]{2,1,0:T(8,128)(2,1)S(1)} collective-permute-done((bf16[8,120,128]{2,1,0:T(8,128)(2,1)S(1)}, bf16[8,120,128]{2,1,0:T(8,128)(2,1)S(1)}, u32[]{:S(2)}, u32[]{:S(2)}) %collective-permute-start.13) | collective-permute-done | bytes 245792 | tf_op jit(solution)/shard_map/ppermute | solution.py:203
  76.8 5.3 %collective-permute-done.15.refs_3_ = bf16[8,120,128]{2,1,0:T(8,128)(2,1)S(1)} collective-permute-done((bf16[8,120,128]{2,1,0:T(8,128)(2,1)S(1)}, bf16[8,120,128]{2,1,0:T(8,128)(2,1)S(1)}, u32[]{:S(2)}, u32[]{:S(2)}) %collective-permute-start.15) | collective-permute-done | bytes 245792 | tf_op jit(solution)/shard_map/ppermute | solution.py:203
  82.1 24.2 %all_to_all.10.parts = bf16[8,240,128]{2,1,0:T(8,128)(2,1)S(1)} all-to-all(bf16[8,240,128]{2,1,0:T(8,128)(2,1)S(1)} %shard_map.102), channel_id=1, replica_groups={{0,128,64,192,32,160,96,224},{144,16,208,80,176,48,240,112},{256,384,32..., dimensions={0} | all-to-all | bytes 983040 | tf_op jit(solution)/shard_map/all_to_all | solution.py:238
  106.4 27.5 %all_to_all.11.mine = bf16[16,240,128]{2,1,0:T(8,128)(2,1)S(1)} all-to-all(bf16[16,240,128]{2,1,0:T(8,128)(2,1)S(1)} %shard_map.103), channel_id=1, replica_groups={{0,32,64,96,128,160,192,224,256,288,320,352,384,416,448,480},{16,48,80,..., dimensions={0} | all-to-all | bytes 1966080 | tf_op jit(solution)/shard_map/all_to_all | solution.py:238
  134.0 4.5 %collective-permute-start.16 = (bf16[16,240,128]{2,1,0:T(8,128)(2,1)S(1)}, bf16[16,240,128]{2,1,0:T(8,128)(2,1)S(1)}, u32[]{:S(2)}, u32[]{:S(2)}) collective-permute-start(bf16[16,240,128]{2,1,0:T(8,128)(2,1)S(1)} %all_to_all.11.mine), channel_id=1, source_target_pairs={{0,16},{16,0},{32,48},{48,32},{64,80},{80,64},{96,112},{112,96},{1... | collective-permute-start | bytes 2949128 | tf_op jit(solution)/shard_map/ppermute | solution.py:203
  138.5 1.4 shard_map.96
  139.9 3.8 %collective-permute-start.8 = (bf16[128,384]{1,0:T(8,128)(2,1)S(1)}, bf16[128,384]{1,0:T(8,128)(2,1)S(1)}, u32[]{:S(2)}, u32[]{:S(2)}) collective-permute-start(bf16[128,384]{1,0:T(8,128)(2,1)S(1)} %get-tuple-element.34), channel_id=1, source_target_pairs={{0,1},{1,0},{2,3},{3,2},{4,5},{5,4},{6,7},{7,6},{8,9},{9,8},{10,11... | collective-permute-start | bytes 294920 | tf_op jit(solution)/shard_map/ppermute | solution.py:203
  143.8 2.6 %collective-permute-start.9 = (bf16[128,384]{1,0:T(8,128)(2,1)S(1)}, bf16[128,384]{1,0:T(8,128)(2,1)S(1)}, u32[]{:S(2)}, u32[]{:S(2)}) collective-permute-start(bf16[128,384]{1,0:T(8,128)(2,1)S(1)} %get-tuple-element.35), channel_id=1, source_target_pairs={{0,2},{1,3},{2,0},{3,1},{4,6},{5,7},{6,4},{7,5},{8,10},{9,11},{10,... | collective-permute-start | bytes 294920 | tf_op jit(solution)/shard_map/ppermute | solution.py:203
  146.3 3.2 %collective-permute-start.10 = (bf16[128,384]{1,0:T(8,128)(2,1)S(1)}, bf16[128,384]{1,0:T(8,128)(2,1)S(1)}, u32[]{:S(2)}, u32[]{:S(2)}) collective-permute-start(bf16[128,384]{1,0:T(8,128)(2,1)S(1)} %get-tuple-element.36), channel_id=1, source_target_pairs={{0,4},{1,5},{2,6},{3,7},{4,0},{5,1},{6,2},{7,3},{8,12},{9,13},{10,... | collective-permute-start | bytes 294920 | tf_op jit(solution)/shard_map/ppermute | solution.py:203
  149.6 4.4 %collective-permute-start.11 = (bf16[128,384]{1,0:T(8,128)(2,1)S(1)}, bf16[128,384]{1,0:T(8,128)(2,1)S(1)}, u32[]{:S(2)}, u32[]{:S(2)}) collective-permute-start(bf16[128,384]{1,0:T(8,128)(2,1)S(1)} %get-tuple-element.37), channel_id=1, source_target_pairs={{0,8},{1,9},{2,10},{3,11},{4,12},{5,13},{6,14},{7,15},{8,0},{9,1},... | collective-permute-start | bytes 294920 | tf_op jit(solution)/shard_map/ppermute | solution.py:203
  154.0 2.5 %collective-permute-done.11.refs_3_ = bf16[128,384]{1,0:T(8,128)(2,1)S(1)} collective-permute-done((bf16[128,384]{1,0:T(8,128)(2,1)S(1)}, bf16[128,384]{1,0:T(8,128)(2,1)S(1)}, u32[]{:S(2)}, u32[]{:S(2)}) %collective-permute-start.11) | collective-permute-done | bytes 98336 | tf_op jit(solution)/shard_map/ppermute | solution.py:203
  157.2 2.3 %shard_map.95 = bf16[128,384]{1,0:T(8,128)(2,1)} custom-call(s32[3,2,5]{2,1,0:T(2,128)S(1)} %bitcast.22, bf16[30,128,128]{2,1,0:T(8,128)(2,1)S(1)} %bitcast.17, bf16[128,768]{1,0:T(8,128)(2,1)S(1)} %get-tuple-element.31.refs_0_, bf16[128,768]{1,0:T(8,128)(2,1)} %collective-permute-done.4.refs_1_, bf16[128,768]{1,0:T(8,128)(2,1)} %collective-permute-done.5.refs_2_, ...), custom_call_target="tpu_custom_call" | custom-call | tf_op jit(solution)/shard_map/pallas_call | solution.py:48
  159.5 1.4 shard_map.104
  (34 shorter events, 3.4 us)
Async XLA Ops:
  0.6 0.7 copy-start.7
  0.6 33.1 %copy-start = (bf16[1,5,6,128,128]{4,3,2,1,0:T(8,128)(2,1)S(1)}, bf16[1,5,6,128,128]{4,3,2,1,0:T(8,128)(2,1)}, u32[]{:S(2)}) copy-start(bf16[1,5,6,128,128]{4,3,2,1,0:T(8,128)(2,1)} %param.7) | copy-start | bytes 2949124
  1.3 32.4 %copy-start.2 = (bf16[128,384]{1,0:T(8,128)(2,1)S(1)}, bf16[128,384]{1,0:T(8,128)(2,1)}, u32[]{:S(2)}) copy-start(bf16[128,384]{1,0:T(8,128)(2,1)} %refs_0_.1) | copy-start | bytes 294916
  3.3 30.4 %collective-permute-start = (bf16[128,1152]{1,0:T(8,128)(2,1)S(1)}, bf16[128,1152]{1,0:T(8,128)(2,1)S(1)}, u32[]{:S(2)}, u32[]{:S(2)}) collective-permute-start(bf16[128,1152]{1,0:T(8,128)(2,1)S(1)} %get-tuple-element.27), channel_id=1, source_target_pairs={{0,1},{1,0},{2,3},{3,2},{4,5},{5,4},{6,7},{7,6},{8,9},{9,8},{10,11... | collective-permute-start | bytes 884744 | tf_op jit(solution)/shard_map/ppermute | solution.py:203
  8.3 25.4 %collective-permute-start.1 = (bf16[128,1152]{1,0:T(8,128)(2,1)S(1)}, bf16[128,1152]{1,0:T(8,128)(2,1)S(1)}, u32[]{:S(2)}, u32[]{:S(2)}) collective-permute-start(bf16[128,1152]{1,0:T(8,128)(2,1)S(1)} %get-tuple-element.28), channel_id=1, source_target_pairs={{0,2},{1,3},{2,0},{3,1},{4,6},{5,7},{6,4},{7,5},{8,10},{9,11},{10,... | collective-permute-start | bytes 884744 | tf_op jit(solution)/shard_map/ppermute | solution.py:203
  14.0 19.7 %collective-permute-start.2 = (bf16[128,1152]{1,0:T(8,128)(2,1)S(1)}, bf16[128,1152]{1,0:T(8,128)(2,1)S(1)}, u32[]{:S(2)}, u32[]{:S(2)}) collective-permute-start(bf16[128,1152]{1,0:T(8,128)(2,1)S(1)} %get-tuple-element.29), channel_id=1, source_target_pairs={{0,4},{1,5},{2,6},{3,7},{4,0},{5,1},{6,2},{7,3},{8,12},{9,13},{10,... | collective-permute-start | bytes 884744 | tf_op jit(solution)/shard_map/ppermute | solution.py:203
  17.1 16.6 %copy-start.8 = (s32[1,5,6]{2,0,1:T(1,128)S(1)}, s32[1,5,6]{2,0,1:T(1,128)}, u32[]{:S(2)}) copy-start(s32[1,5,6]{2,0,1:T(1,128)} %param.8) | copy-start | bytes 364
  17.1 16.6 %collective-permute-start.3 = (bf16[128,1152]{1,0:T(8,128)(2,1)S(1)}, bf16[128,1152]{1,0:T(8,128)(2,1)S(1)}, u32[]{:S(2)}, u32[]{:S(2)}) collective-permute-start(bf16[128,1152]{1,0:T(8,128)(2,1)S(1)} %get-tuple-element.30), channel_id=1, source_target_pairs={{0,8},{1,9},{2,10},{3,11},{4,12},{5,13},{6,14},{7,15},{8,0},{9,1},... | collective-permute-start | bytes 884744 | tf_op jit(solution)/shard_map/ppermute | solution.py:203
  35.0 0.7 copy-start.3
  35.7 24.1 %collective-permute-start.4 = (bf16[128,768]{1,0:T(8,128)(2,1)S(1)}, bf16[128,768]{1,0:T(8,128)(2,1)}, u32[]{:S(2)}, u32[]{:S(2)}) collective-permute-start(bf16[128,768]{1,0:T(8,128)(2,1)S(1)} %get-tuple-element.31.refs_0_), channel_id=1, source_target_pairs={{0,1},{1,0},{2,3},{3,2},{4,5},{5,4},{6,7},{7,6},{8,9},{9,8},{10,11... | collective-permute-start | bytes 589832 | tf_op jit(solution)/shard_map/ppermute | solution.py:203
  37.6 22.2 %collective-permute-start.5 = (bf16[128,768]{1,0:T(8,128)(2,1)S(1)}, bf16[128,768]{1,0:T(8,128)(2,1)}, u32[]{:S(2)}, u32[]{:S(2)}) collective-permute-start(bf16[128,768]{1,0:T(8,128)(2,1)S(1)} %get-tuple-element.31.refs_0_), channel_id=1, source_target_pairs={{0,2},{1,3},{2,0},{3,1},{4,6},{5,7},{6,4},{7,5},{8,10},{9,11},{10,... | collective-permute-start | bytes 589832 | tf_op jit(solution)/shard_map/ppermute | solution.py:203
  46.0 13.7 %collective-permute-start.6 = (bf16[128,768]{1,0:T(8,128)(2,1)S(1)}, bf16[128,768]{1,0:T(8,128)(2,1)}, u32[]{:S(2)}, u32[]{:S(2)}) collective-permute-start(bf16[128,768]{1,0:T(8,128)(2,1)S(1)} %get-tuple-element.31.refs_0_), channel_id=1, source_target_pairs={{0,4},{1,5},{2,6},{3,7},{4,0},{5,1},{6,2},{7,3},{8,12},{9,13},{10,... | collective-permute-start | bytes 589832 | tf_op jit(solution)/shard_map/ppermute | solution.py:203
  49.2 10.9 %collective-permute-start.7 = (bf16[128,768]{1,0:T(8,128)(2,1)S(1)}, bf16[128,768]{1,0:T(8,128)(2,1)}, u32[]{:S(2)}, u32[]{:S(2)}) collective-permute-start(bf16[128,768]{1,0:T(8,128)(2,1)S(1)} %get-tuple-element.31.refs_0_), channel_id=1, source_target_pairs={{0,8},{1,9},{2,10},{3,11},{4,12},{5,13},{6,14},{7,15},{8,0},{9,1},... | collective-permute-start | bytes 589832 | tf_op jit(solution)/shard_map/ppermute | solution.py:203
  53.5 0.9 copy-start.4
  54.5 5.6 %copy-start.6 = (bf16[128,384]{1,0:T(8,128)(2,1)S(1)}, bf16[128,384]{1,0:T(8,128)(2,1)}, u32[]{:S(2)}) copy-start(bf16[128,384]{1,0:T(8,128)(2,1)} %cot.3) | copy-start | bytes 294916
  56.4 9.9 %collective-permute-start.12 = (bf16[15,128,128]{2,1,0:T(8,128)(2,1)}, bf16[15,128,128]{2,1,0:T(8,128)(2,1)}, u32[]{:S(2)}, u32[]{:S(2)}) collective-permute-start(bf16[15,128,128]{2,1,0:T(8,128)(2,1)} %get-tuple-element.39), channel_id=1, source_target_pairs={{0,16},{16,0},{32,48},{48,32},{64,80},{80,64},{96,112},{112,96},{1... | collective-permute-start | bytes 1474568 | tf_op jit(solution)/shard_map/ppermute | solution.py:203
  62.6 7.6 %collective-permute-start.14 = (bf16[15,128,128]{2,1,0:T(8,128)(2,1)}, bf16[15,128,128]{2,1,0:T(8,128)(2,1)}, u32[]{:S(2)}, u32[]{:S(2)}) collective-permute-start(bf16[15,128,128]{2,1,0:T(8,128)(2,1)} %get-tuple-element.43), channel_id=1, source_target_pairs={{0,16},{16,0},{32,48},{48,32},{64,80},{80,64},{96,112},{112,96},{1... | collective-permute-start | bytes 1474568 | tf_op jit(solution)/shard_map/ppermute | solution.py:203
  67.4 9.4 %collective-permute-start.13 = (bf16[8,120,128]{2,1,0:T(8,128)(2,1)S(1)}, bf16[8,120,128]{2,1,0:T(8,128)(2,1)S(1)}, u32[]{:S(2)}, u32[]{:S(2)}) collective-permute-start(bf16[8,120,128]{2,1,0:T(8,128)(2,1)S(1)} %get-tuple-element.41), channel_id=1, source_target_pairs={{0,256},{16,272},{32,288},{48,304},{64,320},{80,336},{96,352},{112... | collective-permute-start | bytes 737288 | tf_op jit(solution)/shard_map/ppermute | solution.py:203
  71.3 10.7 %collective-permute-start.15 = (bf16[8,120,128]{2,1,0:T(8,128)(2,1)S(1)}, bf16[8,120,128]{2,1,0:T(8,128)(2,1)S(1)}, u32[]{:S(2)}, u32[]{:S(2)}) collective-permute-start(bf16[8,120,128]{2,1,0:T(8,128)(2,1)S(1)} %get-tuple-element.45), channel_id=1, source_target_pairs={{0,256},{16,272},{32,288},{48,304},{64,320},{80,336},{96,352},{112... | collective-permute-start | bytes 737288 | tf_op jit(solution)/shard_map/ppermute | solution.py:203
  106.4 32.1 %copy-start.5 = (bf16[128,768]{1,0:T(8,128)(2,1)S(1)}, bf16[128,768]{1,0:T(8,128)(2,1)}, u32[]{:S(2)}) copy-start(bf16[128,768]{1,0:T(8,128)(2,1)} %copy-done.3) | copy-start | bytes 589828
  134.0 23.2 %copy-start.1 = (bf16[1,5,3,2,128,128]{5,4,3,2,1,0:T(8,128)(2,1)S(1)}, bf16[1,5,3,2,128,128]{5,4,3,2,1,0:T(8,128)(2,1)}, u32[]{:S(2)}) copy-start(bf16[1,5,3,2,128,128]{5,4,3,2,1,0:T(8,128)(2,1)} %param.9) | copy-start | bytes 2949124
  134.0 25.5 %collective-permute-start.16 = (bf16[16,240,128]{2,1,0:T(8,128)(2,1)S(1)}, bf16[16,240,128]{2,1,0:T(8,128)(2,1)S(1)}, u32[]{:S(2)}, u32[]{:S(2)}) collective-permute-start(bf16[16,240,128]{2,1,0:T(8,128)(2,1)S(1)} %all_to_all.11.mine), channel_id=1, source_target_pairs={{0,16},{16,0},{32,48},{48,32},{64,80},{80,64},{96,112},{112,96},{1... | collective-permute-start | bytes 2949128 | tf_op jit(solution)/shard_map/ppermute | solution.py:203
  139.9 14.0 %collective-permute-start.8 = (bf16[128,384]{1,0:T(8,128)(2,1)S(1)}, bf16[128,384]{1,0:T(8,128)(2,1)S(1)}, u32[]{:S(2)}, u32[]{:S(2)}) collective-permute-start(bf16[128,384]{1,0:T(8,128)(2,1)S(1)} %get-tuple-element.34), channel_id=1, source_target_pairs={{0,1},{1,0},{2,3},{3,2},{4,5},{5,4},{6,7},{7,6},{8,9},{9,8},{10,11... | collective-permute-start | bytes 294920 | tf_op jit(solution)/shard_map/ppermute | solution.py:203
  143.8 10.2 %collective-permute-start.9 = (bf16[128,384]{1,0:T(8,128)(2,1)S(1)}, bf16[128,384]{1,0:T(8,128)(2,1)S(1)}, u32[]{:S(2)}, u32[]{:S(2)}) collective-permute-start(bf16[128,384]{1,0:T(8,128)(2,1)S(1)} %get-tuple-element.35), channel_id=1, source_target_pairs={{0,2},{1,3},{2,0},{3,1},{4,6},{5,7},{6,4},{7,5},{8,10},{9,11},{10,... | collective-permute-start | bytes 294920 | tf_op jit(solution)/shard_map/ppermute | solution.py:203
  146.3 7.6 %collective-permute-start.10 = (bf16[128,384]{1,0:T(8,128)(2,1)S(1)}, bf16[128,384]{1,0:T(8,128)(2,1)S(1)}, u32[]{:S(2)}, u32[]{:S(2)}) collective-permute-start(bf16[128,384]{1,0:T(8,128)(2,1)S(1)} %get-tuple-element.36), channel_id=1, source_target_pairs={{0,4},{1,5},{2,6},{3,7},{4,0},{5,1},{6,2},{7,3},{8,12},{9,13},{10,... | collective-permute-start | bytes 294920 | tf_op jit(solution)/shard_map/ppermute | solution.py:203
  149.6 6.9 %collective-permute-start.11 = (bf16[128,384]{1,0:T(8,128)(2,1)S(1)}, bf16[128,384]{1,0:T(8,128)(2,1)S(1)}, u32[]{:S(2)}, u32[]{:S(2)}) collective-permute-start(bf16[128,384]{1,0:T(8,128)(2,1)S(1)} %get-tuple-element.37), channel_id=1, source_target_pairs={{0,8},{1,9},{2,10},{3,11},{4,12},{5,13},{6,14},{7,15},{8,0},{9,1},... | collective-permute-start | bytes 294920 | tf_op jit(solution)/shard_map/ppermute | solution.py:203

commit v9 on v8

--- a/solution.py
+++ b/solution.py
@@ -62,10 +62,10 @@
     return lax.dot_general(a, b, (((0,), (0,)), ((), ())), preferred_element_type=F32)
 
 
-def back_kernel(levels, db, hb, kd, pick, cot, w, x, *refs):
+def back_kernel(levels, db, hb, kd, early, pick, cot, w, x, *refs):
     own, sends, acc = refs[0], refs[1:levels], refs[levels]
     wide = db * B
-    for send in sends:
+    for send in sends[early:]:
         send[:, :wide] = x[...]
     for lvl in range(levels):
         acc[...] = jnp.zeros_like(acc)
@@ -79,12 +79,13 @@
             if lvl == 0:
                 own[:, h * B : (h + 1) * B] = acc[h]
             else:
-                sends[lvl - 1][:, wide + h * B : wide + (h + 1) * B] = acc[h].astype(BF16)
-
-
-def mid_kernel(levels, db, hb, pick, w, x, own, *refs):
-    got, hg, act = refs[: levels - 1], refs[levels - 1], refs[levels]
-    xs = (x,) + got
+                at = h * B + (wide if lvl > early else 0)
+                sends[lvl - 1][:, at : at + B] = acc[h].astype(BF16)
+
+
+def mid_kernel(levels, db, hb, early, pick, w, *refs):
+    xs, own, got = refs[:levels], refs[levels], refs[levels + 1 : 2 * levels]
+    hg, act = refs[2 * levels :]
     wide = db * B
     for o in range(hb):
         here = slice(o * B, (o + 1) * B)
@@ -100,8 +101,9 @@
         inner = GELU_C * (1.0 + (3.0 * GELU_A) * sq)
         slope = half + 0.5 * v * (1.0 - t * t) * inner
         grad = own[:, here]
-        for ref in got:
-            grad = grad + ref[:, wide + o * B : wide + (o + 1) * B].astype(F32)
+        for b, ref in enumerate(got):
+            at = o * B + (0 if b < early else wide)
+            grad = grad + ref[:, at : at + B].astype(F32)
         hg[:, here] = (grad * slope).astype(BF16)
 
 
@@ -232,7 +234,7 @@
     row_bit = dp.bit_length() - 2
 
     def over_mp(blocks):
-        return [from_partner(blocks[b], "mp", b) for b in range(bits)]
+        return [from_partner(blocks[b], "mp", b) for b in range(len(blocks))]
 
     def exchange(block, groups):
         return lax.all_to_all(
@@ -252,20 +254,25 @@
         return keep_y, from_partner(send_y, "dp", row_bit)
 
     wide, deep = db * B, hb * B
+    early = bits // 2
+    xs = [inputs] + over_mp([inputs] * early)
     own, *first = call(
-        functools.partial(back_kernel, levels, db, hb, kd),
-        [sds((tokens, deep), F32)] + [sds((tokens, wide + deep), BF16)] * bits,
+        functools.partial(back_kernel, levels, db, hb, kd, early),
+        [sds((tokens, deep), F32)]
+        + [sds((tokens, deep), BF16)] * early
+        + [sds((tokens, wide + deep), BF16)] * (bits - early),
         [SMEM, ARG, ARG, ARG],
         [pltpu.VMEM((hb, tokens, B), F32)],
     )(down_ids, cotangent, down_w, inputs)
     got = over_mp(first)
+    xs = xs + got[early:]
 
     hg, act = call(
-        functools.partial(mid_kernel, levels, db, hb),
+        functools.partial(mid_kernel, levels, db, hb, early),
         [sds((tokens, deep), BF16)] * 2,
-        [SMEM] + [VMEM] * (levels + 2),
+        [SMEM] + [VMEM] * (2 * levels + 1),
         (),
-    )(up_ids, up_w, inputs, own, *got)
+    )(up_ids, up_w, *xs, own, *got)
     acts = [act] + over_mp([act] * bits)
 
     in0, *in_terms = call(
@@ -286,7 +293,7 @@
         grad_outs(n_up),
         [SMEM, SMEM, VMEM] + [VMEM] * levels,
         [pltpu.VMEM((n_up, B, B), F32)],
-    )(up_ids, core, hg, inputs, *got)
+    )(up_ids, core, hg, *xs)
     up_parts = partials(up_keep, up_send)
 
     down_keep, down_send = call(

time: 164 us -> 182 us (1.11)
  waiting for transfers between devices: 23.2 us -> 38.9 us
  local copies, waits for them, and re-layouts: 2.28 us -> 9.38 us
    ppermute x17 -> x19, waiting for transfers between devices: 23.2 us -> 38.9 us  [from_partner(): return lax.ppermute(block, axis, [(i, i ^ 1 << bit) for i in range(count)])]
    unnamed x18 -> x46, local copies, waits for them, and re-layouts: 2.28 us -> 9.38 us
    ppermute x17 -> x19, starting transfers between devices: 66.8 us -> 65.2 us  [from_partner(): return lax.ppermute(block, axis, [(i, i ^ 1 << bit) for i in range(count)])]
  transfers between devices with their start and end apart: 17 -> 19, of which waited for: 5 -> 6; matrix products, arithmetic and copies ran while one was open for 0% -> 0% of each run, Pallas kernels for 7% -> 5%
where the time goes in v9:
time: 182 us; the launch traced here: 179 us
  starting transfers between devices  65.2 us (36%)
  blocking collectives  50.3 us (28%)
  waiting for transfers between devices  38.9 us (21%)
  Pallas kernels  14.4 us (8%)
  local copies, waits for them, and re-layouts  9.38 us (5%)
    ppermute x19, starting transfers between devices, from_partner(): return lax.ppermute(block, axis, [(i, i ^ 1 << bit) for i in range(count)])  65.2 us
    all_to_all x2, blocking collectives, exchange(): lax.all_to_all(block, 'dp', split_axis=0, concat_axis=0, axis_index_group...  50.3 us
    ppermute x19, waiting for transfers between devices, from_partner(): return lax.ppermute(block, axis, [(i, i ^ 1 << bit) for i in range(count)])  38.9 us
    pallas_call x12, Pallas kernels, invoke(): return run(*placed)  14.4 us
    unnamed x46, local copies, waits for them, and re-layouts  9.38 us
  transfers between devices with their start and end apart: 19, of which 6 were waited for; matrix products, arithmetic and copies ran while one was open for 0% of the time, Pallas kernels for 5%

profile of v9, /device:TPU:1, one launch (start us, length us, event | category | flops | bytes accessed | tf_op | source)
XLA Modules:
  0.0 179.2 jit_solution(17096329099065223232)
XLA Ops:
  1.3 2.0 %shard_map.93 = (f32[128,768]{1,0:T(8,128)S(1)}, bf16[128,768]{1,0:T(8,128)(2,1)S(1)}, bf16[128,768]{1,0:T(8,128)(2,1)S(1)}, bf16[128,1152]{1,0:T(8,128)(2,1)S(1)}, bf16[128,1152]{1,0:T(8,128)(2,1)S(1)}) custom-call(s32[3,2,5]{2,1,0:T(2,128)S(1)} %bitcast.21, bf16[128,384]{1,0:T(8,128)(2,1)} %cot.3, bf16[30,128,128]{2,1,0:T(8,128)(2,1)} %bitcast.16, ...), custom_call_target="tpu_custom_call" | custom-call | tf_op jit(solution)/shard_map/pallas_call | solution.py:48
  3.3 3.9 %collective-permute-start.2 = (bf16[128,1152]{1,0:T(8,128)(2,1)S(1)}, bf16[128,1152]{1,0:T(8,128)(2,1)S(1)}, u32[]{:S(2)}, u32[]{:S(2)}) collective-permute-start(bf16[128,1152]{1,0:T(8,128)(2,1)S(1)} %get-tuple-element.26), channel_id=1, source_target_pairs={{0,4},{1,5},{2,6},{3,7},{4,0},{5,1},{6,2},{7,3},{8,12},{9,13},{10,... | collective-permute-start | bytes 884744 | tf_op jit(solution)/shard_map/ppermute | solution.py:205
  7.3 4.4 %collective-permute-start.3 = (bf16[128,1152]{1,0:T(8,128)(2,1)S(1)}, bf16[128,1152]{1,0:T(8,128)(2,1)S(1)}, u32[]{:S(2)}, u32[]{:S(2)}) collective-permute-start(bf16[128,1152]{1,0:T(8,128)(2,1)S(1)} %get-tuple-element.27), channel_id=1, source_target_pairs={{0,8},{1,9},{2,10},{3,11},{4,12},{5,13},{6,14},{7,15},{8,0},{9,1},... | collective-permute-start | bytes 884744 | tf_op jit(solution)/shard_map/ppermute | solution.py:205
  11.6 7.5 %collective-permute-start.1 = (bf16[128,384]{1,0:T(8,128)(2,1)S(1)}, bf16[128,384]{1,0:T(8,128)(2,1)S(1)}, u32[]{:S(2)}, u32[]{:S(2)}) collective-permute-start(bf16[128,384]{1,0:T(8,128)(2,1)S(1)} %copy-done.2), channel_id=1, source_target_pairs={{0,2},{1,3},{2,0},{3,1},{4,6},{5,7},{6,4},{7,5},{8,10},{9,11},{10,... | collective-permute-start | bytes 294920 | tf_op jit(solution)/shard_map/ppermute | solution.py:205
  19.1 2.4 %collective-permute-start.4 = (bf16[128,768]{1,0:T(8,128)(2,1)S(1)}, bf16[128,768]{1,0:T(8,128)(2,1)S(1)}, u32[]{:S(2)}, u32[]{:S(2)}) collective-permute-start(bf16[128,768]{1,0:T(8,128)(2,1)S(1)} %get-tuple-element.29), channel_id=1, source_target_pairs={{0,1},{1,0},{2,3},{3,2},{4,5},{5,4},{6,7},{7,6},{8,9},{9,8},{10,11... | collective-permute-start | bytes 589832 | tf_op jit(solution)/shard_map/ppermute | solution.py:205
  21.5 3.5 %collective-permute-start.5 = (bf16[128,768]{1,0:T(8,128)(2,1)S(1)}, bf16[128,768]{1,0:T(8,128)(2,1)S(1)}, u32[]{:S(2)}, u32[]{:S(2)}) collective-permute-start(bf16[128,768]{1,0:T(8,128)(2,1)S(1)} %get-tuple-element.30), channel_id=1, source_target_pairs={{0,2},{1,3},{2,0},{3,1},{4,6},{5,7},{6,4},{7,5},{8,10},{9,11},{10,... | collective-permute-start | bytes 589832 | tf_op jit(solution)/shard_map/ppermute | solution.py:205
  25.1 2.2 %collective-permute-start = (bf16[128,384]{1,0:T(8,128)(2,1)S(1)}, bf16[128,384]{1,0:T(8,128)(2,1)S(1)}, u32[]{:S(2)}, u32[]{:S(2)}) collective-permute-start(bf16[128,384]{1,0:T(8,128)(2,1)S(1)} %copy-done.2), channel_id=1, source_target_pairs={{0,1},{1,0},{2,3},{3,2},{4,5},{5,4},{6,7},{7,6},{8,9},{9,8},{10,11... | collective-permute-start | bytes 294920 | tf_op jit(solution)/shard_map/ppermute | solution.py:205
  27.2 18.8 %collective-permute-done.refs_1_ = bf16[128,384]{1,0:T(8,128)(2,1)S(1)} collective-permute-done((bf16[128,384]{1,0:T(8,128)(2,1)S(1)}, bf16[128,384]{1,0:T(8,128)(2,1)S(1)}, u32[]{:S(2)}, u32[]{:S(2)}) %collective-permute-start) | collective-permute-done | bytes 98336 | tf_op jit(solution)/shard_map/ppermute | solution.py:205
  48.1 2.4 %collective-permute-start.9 = (bf16[128,768]{1,0:T(8,128)(2,1)S(1)}, bf16[128,768]{1,0:T(8,128)(2,1)S(1)}, u32[]{:S(2)}, u32[]{:S(2)}) collective-permute-start(bf16[128,768]{1,0:T(8,128)(2,1)S(1)} %get-tuple-element.31.refs_0_), channel_id=1, source_target_pairs={{0,8},{1,9},{2,10},{3,11},{4,12},{5,13},{6,14},{7,15},{8,0},{9,1},... | collective-permute-start | bytes 589832 | tf_op jit(solution)/shard_map/ppermute | solution.py:205
  50.5 2.2 %collective-permute-start.8 = (bf16[128,768]{1,0:T(8,128)(2,1)S(1)}, bf16[128,768]{1,0:T(8,128)(2,1)S(1)}, u32[]{:S(2)}, u32[]{:S(2)}) collective-permute-start(bf16[128,768]{1,0:T(8,128)(2,1)S(1)} %get-tuple-element.31.refs_0_), channel_id=1, source_target_pairs={{0,4},{1,5},{2,6},{3,7},{4,0},{5,1},{6,2},{7,3},{8,12},{9,13},{10,... | collective-permute-start | bytes 589832 | tf_op jit(solution)/shard_map/ppermute | solution.py:205
  52.6 4.0 %collective-permute-start.7 = (bf16[128,768]{1,0:T(8,128)(2,1)S(1)}, bf16[128,768]{1,0:T(8,128)(2,1)S(1)}, u32[]{:S(2)}, u32[]{:S(2)}) collective-permute-start(bf16[128,768]{1,0:T(8,128)(2,1)S(1)} %get-tuple-element.31.refs_0_), channel_id=1, source_target_pairs={{0,2},{1,3},{2,0},{3,1},{4,6},{5,7},{6,4},{7,5},{8,10},{9,11},{10,... | collective-permute-start | bytes 589832 | tf_op jit(solution)/shard_map/ppermute | solution.py:205
  56.7 1.9 %collective-permute-start.6 = (bf16[128,768]{1,0:T(8,128)(2,1)S(1)}, bf16[128,768]{1,0:T(8,128)(2,1)}, u32[]{:S(2)}, u32[]{:S(2)}) collective-permute-start(bf16[128,768]{1,0:T(8,128)(2,1)S(1)} %get-tuple-element.31.refs_0_), channel_id=1, source_target_pairs={{0,1},{1,0},{2,3},{3,2},{4,5},{5,4},{6,7},{7,6},{8,9},{9,8},{10,11... | collective-permute-start | bytes 589832 | tf_op jit(solution)/shard_map/ppermute | solution.py:205
  60.4 1.9 %shard_map.98 = (f32[15,128,128]{2,1,0:T(8,128)S(1)}, bf16[15,128,128]{2,1,0:T(8,128)(2,1)}) custom-call(s32[5,1,6]{2,1,0:T(1,128)S(1)} %bitcast.25, s32[1]{0:T(128)} %bitcast.6.core, bf16[128,768]{1,0:T(8,128)(2,1)S(1)} %copy-done.16, bf16[128,384]{1,0:T(8,128)(2,1)S(1)} %copy-done.2, bf16[128,384]{1,0:T(8,128)(2,1)S(1)} %copy-done.19, ...), custom_call_target="tpu_custom_call" | custom-call | tf_op jit(solution)/shard_map/pallas_call | solution.py:48
  62.4 3.8 %collective-permute-start.14 = (bf16[15,128,128]{2,1,0:T(8,128)(2,1)}, bf16[15,128,128]{2,1,0:T(8,128)(2,1)S(1)}, u32[]{:S(2)}, u32[]{:S(2)}) collective-permute-start(bf16[15,128,128]{2,1,0:T(8,128)(2,1)} %get-tuple-element.39), channel_id=1, source_target_pairs={{0,16},{16,0},{32,48},{48,32},{64,80},{80,64},{96,112},{112,96},{1... | collective-permute-start | bytes 1474568 | tf_op jit(solution)/shard_map/ppermute | solution.py:205
  69.2 8.4 %collective-permute-done.6.refs_1_ = bf16[128,768]{1,0:T(8,128)(2,1)} collective-permute-done((bf16[128,768]{1,0:T(8,128)(2,1)S(1)}, bf16[128,768]{1,0:T(8,128)(2,1)}, u32[]{:S(2)}, u32[]{:S(2)}) %collective-permute-start.6) | collective-permute-done | bytes 196640 | tf_op jit(solution)/shard_map/ppermute | solution.py:205
  81.3 2.3 %shard_map.100 = (f32[15,128,128]{2,1,0:T(8,128)S(1)}, bf16[15,128,128]{2,1,0:T(8,128)(2,1)}) custom-call(s32[3,2,5]{2,1,0:T(2,128)S(1)} %bitcast.22, s32[1]{0:T(128)} %bitcast.6.core, bf16[128,384]{1,0:T(8,128)(2,1)S(1)} %copy-done.20, bf16[128,768]{1,0:T(8,128)(2,1)S(1)} %copy-done.4, bf16[128,768]{1,0:T(8,128)(2,1)} %collective-permute-done.6.refs_1_, ...), custom_call_target="tpu_custom_call" | custom-call | tf_op jit(solution)/shard_map/pallas_call | solution.py:48
  83.6 2.4 %collective-permute-start.16 = (bf16[15,128,128]{2,1,0:T(8,128)(2,1)}, bf16[15,128,128]{2,1,0:T(8,128)(2,1)}, u32[]{:S(2)}, u32[]{:S(2)}) collective-permute-start(bf16[15,128,128]{2,1,0:T(8,128)(2,1)} %get-tuple-element.43), channel_id=1, source_target_pairs={{0,16},{16,0},{32,48},{48,32},{64,80},{80,64},{96,112},{112,96},{1... | collective-permute-start | bytes 1474568 | tf_op jit(solution)/shard_map/ppermute | solution.py:205
  86.1 1.9 %collective-permute-start.15 = (bf16[8,120,128]{2,1,0:T(8,128)(2,1)S(1)}, bf16[8,120,128]{2,1,0:T(8,128)(2,1)S(1)}, u32[]{:S(2)}, u32[]{:S(2)}) collective-permute-start(bf16[8,120,128]{2,1,0:T(8,128)(2,1)S(1)} %get-tuple-element.41), channel_id=1, source_target_pairs={{0,256},{16,272},{32,288},{48,304},{64,320},{80,336},{96,352},{112... | collective-permute-start | bytes 737288 | tf_op jit(solution)/shard_map/ppermute | solution.py:205
  89.1 3.4 %collective-permute-start.17 = (bf16[8,120,128]{2,1,0:T(8,128)(2,1)S(1)}, bf16[8,120,128]{2,1,0:T(8,128)(2,1)S(1)}, u32[]{:S(2)}, u32[]{:S(2)}) collective-permute-start(bf16[8,120,128]{2,1,0:T(8,128)(2,1)S(1)} %get-tuple-element.45), channel_id=1, source_target_pairs={{0,256},{16,272},{32,288},{48,304},{64,320},{80,336},{96,352},{112... | collective-permute-start | bytes 737288 | tf_op jit(solution)/shard_map/ppermute | solution.py:205
  92.5 3.0 %collective-permute-done.15.refs_1_ = bf16[8,120,128]{2,1,0:T(8,128)(2,1)S(1)} collective-permute-done((bf16[8,120,128]{2,1,0:T(8,128)(2,1)S(1)}, bf16[8,120,128]{2,1,0:T(8,128)(2,1)S(1)}, u32[]{:S(2)}, u32[]{:S(2)}) %collective-permute-start.15) | collective-permute-done | bytes 245792 | tf_op jit(solution)/shard_map/ppermute | solution.py:205
  95.5 5.3 %collective-permute-done.17.refs_3_ = bf16[8,120,128]{2,1,0:T(8,128)(2,1)S(1)} collective-permute-done((bf16[8,120,128]{2,1,0:T(8,128)(2,1)S(1)}, bf16[8,120,128]{2,1,0:T(8,128)(2,1)S(1)}, u32[]{:S(2)}, u32[]{:S(2)}) %collective-permute-start.17) | collective-permute-done | bytes 245792 | tf_op jit(solution)/shard_map/ppermute | solution.py:205
  100.8 23.4 %all_to_all.10.parts = bf16[8,240,128]{2,1,0:T(8,128)(2,1)S(1)} all-to-all(bf16[8,240,128]{2,1,0:T(8,128)(2,1)S(1)} %shard_map.102), channel_id=1, replica_groups={{0,128,64,192,32,160,96,224},{144,16,208,80,176,48,240,112},{256,384,32..., dimensions={0} | all-to-all | bytes 983040 | tf_op jit(solution)/shard_map/all_to_all | solution.py:240
  124.4 26.8 %all_to_all.11.mine = bf16[16,240,128]{2,1,0:T(8,128)(2,1)S(1)} all-to-all(bf16[16,240,128]{2,1,0:T(8,128)(2,1)S(1)} %shard_map.103), channel_id=1, replica_groups={{0,32,64,96,128,160,192,224,256,288,320,352,384,416,448,480},{16,48,80,..., dimensions={0} | all-to-all | bytes 1966080 | tf_op jit(solution)/shard_map/all_to_all | solution.py:240
  151.2 4.8 %collective-permute-start.18 = (bf16[16,240,128]{2,1,0:T(8,128)(2,1)S(1)}, bf16[16,240,128]{2,1,0:T(8,128)(2,1)S(1)}, u32[]{:S(2)}, u32[]{:S(2)}) collective-permute-start(bf16[16,240,128]{2,1,0:T(8,128)(2,1)S(1)} %all_to_all.11.mine), channel_id=1, source_target_pairs={{0,16},{16,0},{32,48},{48,32},{64,80},{80,64},{96,112},{112,96},{1... | collective-permute-start | bytes 2949128 | tf_op jit(solution)/shard_map/ppermute | solution.py:205
  156.0 1.4 shard_map.96
  157.4 3.0 %collective-permute-start.10 = (bf16[128,384]{1,0:T(8,128)(2,1)S(1)}, bf16[128,384]{1,0:T(8,128)(2,1)S(1)}, u32[]{:S(2)}, u32[]{:S(2)}) collective-permute-start(bf16[128,384]{1,0:T(8,128)(2,1)S(1)} %get-tuple-element.34), channel_id=1, source_target_pairs={{0,1},{1,0},{2,3},{3,2},{4,5},{5,4},{6,7},{7,6},{8,9},{9,8},{10,11... | collective-permute-start | bytes 294920 | tf_op jit(solution)/shard_map/ppermute | solution.py:205
  160.4 4.2 %collective-permute-start.11 = (bf16[128,384]{1,0:T(8,128)(2,1)S(1)}, bf16[128,384]{1,0:T(8,128)(2,1)S(1)}, u32[]{:S(2)}, u32[]{:S(2)}) collective-permute-start(bf16[128,384]{1,0:T(8,128)(2,1)S(1)} %get-tuple-element.35), channel_id=1, source_target_pairs={{0,2},{1,3},{2,0},{3,1},{4,6},{5,7},{6,4},{7,5},{8,10},{9,11},{10,... | collective-permute-start | bytes 294920 | tf_op jit(solution)/shard_map/ppermute | solution.py:205
  164.6 3.1 %collective-permute-start.12 = (bf16[128,384]{1,0:T(8,128)(2,1)S(1)}, bf16[128,384]{1,0:T(8,128)(2,1)S(1)}, u32[]{:S(2)}, u32[]{:S(2)}) collective-permute-start(bf16[128,384]{1,0:T(8,128)(2,1)S(1)} %get-tuple-element.36), channel_id=1, source_target_pairs={{0,4},{1,5},{2,6},{3,7},{4,0},{5,1},{6,2},{7,3},{8,12},{9,13},{10,... | collective-permute-start | bytes 294920 | tf_op jit(solution)/shard_map/ppermute | solution.py:205
  167.7 4.4 %collective-permute-start.13 = (bf16[128,384]{1,0:T(8,128)(2,1)S(1)}, bf16[128,384]{1,0:T(8,128)(2,1)S(1)}, u32[]{:S(2)}, u32[]{:S(2)}) collective-permute-start(bf16[128,384]{1,0:T(8,128)(2,1)S(1)} %get-tuple-element.37), channel_id=1, source_target_pairs={{0,8},{1,9},{2,10},{3,11},{4,12},{5,13},{6,14},{7,15},{8,0},{9,1},... | collective-permute-start | bytes 294920 | tf_op jit(solution)/shard_map/ppermute | solution.py:205
  172.1 2.5 %collective-permute-done.13.refs_3_ = bf16[128,384]{1,0:T(8,128)(2,1)S(1)} collective-permute-done((bf16[128,384]{1,0:T(8,128)(2,1)S(1)}, bf16[128,384]{1,0:T(8,128)(2,1)S(1)}, u32[]{:S(2)}, u32[]{:S(2)}) %collective-permute-start.13) | collective-permute-done | bytes 98336 | tf_op jit(solution)/shard_map/ppermute | solution.py:205
  175.7 2.0 %shard_map.95 = bf16[128,384]{1,0:T(8,128)(2,1)} custom-call(s32[3,2,5]{2,1,0:T(2,128)S(1)} %bitcast.23, bf16[30,128,128]{2,1,0:T(8,128)(2,1)S(1)} %bitcast.17, bf16[128,768]{1,0:T(8,128)(2,1)S(1)} %copy-done.5, bf16[128,768]{1,0:T(8,128)(2,1)} %collective-permute-done.6.refs_1_, bf16[128,768]{1,0:T(8,128)(2,1)S(1)} %copy-done.14, ...), custom_call_target="tpu_custom_call" | custom-call | tf_op jit(solution)/shard_map/pallas_call | solution.py:48
  177.7 1.4 shard_map.104
  (66 shorter events, 13.7 us)
Async XLA Ops:
  0.6 45.5 %copy-start = (bf16[1,5,6,128,128]{4,3,2,1,0:T(8,128)(2,1)S(1)}, bf16[1,5,6,128,128]{4,3,2,1,0:T(8,128)(2,1)}, u32[]{:S(2)}) copy-start(bf16[1,5,6,128,128]{4,3,2,1,0:T(8,128)(2,1)} %param.7) | copy-start | bytes 2949124
  1.3 10.3 %copy-start.2 = (bf16[128,384]{1,0:T(8,128)(2,1)S(1)}, bf16[128,384]{1,0:T(8,128)(2,1)}, u32[]{:S(2)}) copy-start(bf16[128,384]{1,0:T(8,128)(2,1)} %refs_0_.3) | copy-start | bytes 294916
  3.3 42.8 %collective-permute-start.2 = (bf16[128,1152]{1,0:T(8,128)(2,1)S(1)}, bf16[128,1152]{1,0:T(8,128)(2,1)S(1)}, u32[]{:S(2)}, u32[]{:S(2)}) collective-permute-start(bf16[128,1152]{1,0:T(8,128)(2,1)S(1)} %get-tuple-element.26), channel_id=1, source_target_pairs={{0,4},{1,5},{2,6},{3,7},{4,0},{5,1},{6,2},{7,3},{8,12},{9,13},{10,... | collective-permute-start | bytes 884744 | tf_op jit(solution)/shard_map/ppermute | solution.py:205
  7.3 38.8 %collective-permute-start.3 = (bf16[128,1152]{1,0:T(8,128)(2,1)S(1)}, bf16[128,1152]{1,0:T(8,128)(2,1)S(1)}, u32[]{:S(2)}, u32[]{:S(2)}) collective-permute-start(bf16[128,1152]{1,0:T(8,128)(2,1)S(1)} %get-tuple-element.27), channel_id=1, source_target_pairs={{0,8},{1,9},{2,10},{3,11},{4,12},{5,13},{6,14},{7,15},{8,0},{9,1},... | collective-permute-start | bytes 884744 | tf_op jit(solution)/shard_map/ppermute | solution.py:205
  11.6 13.4 %collective-permute-start.1 = (bf16[128,384]{1,0:T(8,128)(2,1)S(1)}, bf16[128,384]{1,0:T(8,128)(2,1)S(1)}, u32[]{:S(2)}, u32[]{:S(2)}) collective-permute-start(bf16[128,384]{1,0:T(8,128)(2,1)S(1)} %copy-done.2), channel_id=1, source_target_pairs={{0,2},{1,3},{2,0},{3,1},{4,6},{5,7},{6,4},{7,5},{8,10},{9,11},{10,... | collective-permute-start | bytes 294920 | tf_op jit(solution)/shard_map/ppermute | solution.py:205
  19.1 27.0 %collective-permute-start.4 = (bf16[128,768]{1,0:T(8,128)(2,1)S(1)}, bf16[128,768]{1,0:T(8,128)(2,1)S(1)}, u32[]{:S(2)}, u32[]{:S(2)}) collective-permute-start(bf16[128,768]{1,0:T(8,128)(2,1)S(1)} %get-tuple-element.29), channel_id=1, source_target_pairs={{0,1},{1,0},{2,3},{3,2},{4,5},{5,4},{6,7},{7,6},{8,9},{9,8},{10,11... | collective-permute-start | bytes 589832 | tf_op jit(solution)/shard_map/ppermute | solution.py:205
  21.5 24.6 %copy-start.22 = (s32[1,5,6]{2,0,1:T(1,128)S(1)}, s32[1,5,6]{2,0,1:T(1,128)}, u32[]{:S(2)}) copy-start(s32[1,5,6]{2,0,1:T(1,128)} %param.8) | copy-start | bytes 364
  21.5 24.5 %collective-permute-start.5 = (bf16[128,768]{1,0:T(8,128)(2,1)S(1)}, bf16[128,768]{1,0:T(8,128)(2,1)S(1)}, u32[]{:S(2)}, u32[]{:S(2)}) collective-permute-start(bf16[128,768]{1,0:T(8,128)(2,1)S(1)} %get-tuple-element.30), channel_id=1, source_target_pairs={{0,2},{1,3},{2,0},{3,1},{4,6},{5,7},{6,4},{7,5},{8,10},{9,11},{10,... | collective-permute-start | bytes 589832 | tf_op jit(solution)/shard_map/ppermute | solution.py:205
  25.1 21.0 %collective-permute-start = (bf16[128,384]{1,0:T(8,128)(2,1)S(1)}, bf16[128,384]{1,0:T(8,128)(2,1)S(1)}, u32[]{:S(2)}, u32[]{:S(2)}) collective-permute-start(bf16[128,384]{1,0:T(8,128)(2,1)S(1)} %copy-done.2), channel_id=1, source_target_pairs={{0,1},{1,0},{2,3},{3,2},{4,5},{5,4},{6,7},{7,6},{8,9},{9,8},{10,11... | collective-permute-start | bytes 294920 | tf_op jit(solution)/shard_map/ppermute | solution.py:205
  46.1 1.3 copy-start.18
  48.1 14.3 %copy-start.3 = (bf16[128,768]{1,0:T(8,128)(2,1)}, bf16[128,768]{1,0:T(8,128)(2,1)S(1)}, u32[]{:S(2)}) copy-start(bf16[128,768]{1,0:T(8,128)(2,1)S(1)} %get-tuple-element.31.refs_0_) | copy-start | bytes 589828
  48.1 18.1 %collective-permute-start.9 = (bf16[128,768]{1,0:T(8,128)(2,1)S(1)}, bf16[128,768]{1,0:T(8,128)(2,1)S(1)}, u32[]{:S(2)}, u32[]{:S(2)}) collective-permute-start(bf16[128,768]{1,0:T(8,128)(2,1)S(1)} %get-tuple-element.31.refs_0_), channel_id=1, source_target_pairs={{0,8},{1,9},{2,10},{3,11},{4,12},{5,13},{6,14},{7,15},{8,0},{9,1},... | collective-permute-start | bytes 589832 | tf_op jit(solution)/shard_map/ppermute | solution.py:205
  50.5 16.4 %collective-permute-start.8 = (bf16[128,768]{1,0:T(8,128)(2,1)S(1)}, bf16[128,768]{1,0:T(8,128)(2,1)S(1)}, u32[]{:S(2)}, u32[]{:S(2)}) collective-permute-start(bf16[128,768]{1,0:T(8,128)(2,1)S(1)} %get-tuple-element.31.refs_0_), channel_id=1, source_target_pairs={{0,4},{1,5},{2,6},{3,7},{4,0},{5,1},{6,2},{7,3},{8,12},{9,13},{10,... | collective-permute-start | bytes 589832 | tf_op jit(solution)/shard_map/ppermute | solution.py:205
  52.6 15.9 %collective-permute-start.7 = (bf16[128,768]{1,0:T(8,128)(2,1)S(1)}, bf16[128,768]{1,0:T(8,128)(2,1)S(1)}, u32[]{:S(2)}, u32[]{:S(2)}) collective-permute-start(bf16[128,768]{1,0:T(8,128)(2,1)S(1)} %get-tuple-element.31.refs_0_), channel_id=1, source_target_pairs={{0,2},{1,3},{2,0},{3,1},{4,6},{5,7},{6,4},{7,5},{8,10},{9,11},{10,... | collective-permute-start | bytes 589832 | tf_op jit(solution)/shard_map/ppermute | solution.py:205
  56.7 20.9 %collective-permute-start.6 = (bf16[128,768]{1,0:T(8,128)(2,1)S(1)}, bf16[128,768]{1,0:T(8,128)(2,1)}, u32[]{:S(2)}, u32[]{:S(2)}) collective-permute-start(bf16[128,768]{1,0:T(8,128)(2,1)S(1)} %get-tuple-element.31.refs_0_), channel_id=1, source_target_pairs={{0,1},{1,0},{2,3},{3,2},{4,5},{5,4},{6,7},{7,6},{8,9},{9,8},{10,11... | collective-permute-start | bytes 589832 | tf_op jit(solution)/shard_map/ppermute | solution.py:205
  58.6 0.9 copy-start.16
  60.4 17.1 %copy-start.20 = (bf16[128,384]{1,0:T(8,128)(2,1)S(1)}, bf16[128,384]{1,0:T(8,128)(2,1)}, u32[]{:S(2)}) copy-start(bf16[128,384]{1,0:T(8,128)(2,1)} %cot.3) | copy-start | bytes 294916
  62.4 23.6 %collective-permute-start.14 = (bf16[15,128,128]{2,1,0:T(8,128)(2,1)}, bf16[15,128,128]{2,1,0:T(8,128)(2,1)S(1)}, u32[]{:S(2)}, u32[]{:S(2)}) collective-permute-start(bf16[15,128,128]{2,1,0:T(8,128)(2,1)} %get-tuple-element.39), channel_id=1, source_target_pairs={{0,16},{16,0},{32,48},{48,32},{64,80},{80,64},{96,112},{112,96},{1... | collective-permute-start | bytes 1474568 | tf_op jit(solution)/shard_map/ppermute | solution.py:205
  83.6 4.4 %collective-permute-start.16 = (bf16[15,128,128]{2,1,0:T(8,128)(2,1)}, bf16[15,128,128]{2,1,0:T(8,128)(2,1)}, u32[]{:S(2)}, u32[]{:S(2)}) collective-permute-start(bf16[15,128,128]{2,1,0:T(8,128)(2,1)} %get-tuple-element.43), channel_id=1, source_target_pairs={{0,16},{16,0},{32,48},{48,32},{64,80},{80,64},{96,112},{112,96},{1... | collective-permute-start | bytes 1474568 | tf_op jit(solution)/shard_map/ppermute | solution.py:205
  86.1 9.4 %collective-permute-start.15 = (bf16[8,120,128]{2,1,0:T(8,128)(2,1)S(1)}, bf16[8,120,128]{2,1,0:T(8,128)(2,1)S(1)}, u32[]{:S(2)}, u32[]{:S(2)}) collective-permute-start(bf16[8,120,128]{2,1,0:T(8,128)(2,1)S(1)} %get-tuple-element.41), channel_id=1, source_target_pairs={{0,256},{16,272},{32,288},{48,304},{64,320},{80,336},{96,352},{112... | collective-permute-start | bytes 737288 | tf_op jit(solution)/shard_map/ppermute | solution.py:205
  89.1 11.6 %collective-permute-start.17 = (bf16[8,120,128]{2,1,0:T(8,128)(2,1)S(1)}, bf16[8,120,128]{2,1,0:T(8,128)(2,1)S(1)}, u32[]{:S(2)}, u32[]{:S(2)}) collective-permute-start(bf16[8,120,128]{2,1,0:T(8,128)(2,1)S(1)} %get-tuple-element.45), channel_id=1, source_target_pairs={{0,256},{16,272},{32,288},{48,304},{64,320},{80,336},{96,352},{112... | collective-permute-start | bytes 737288 | tf_op jit(solution)/shard_map/ppermute | solution.py:205
  124.3 31.6 %copy-start.17 = (bf16[128,768]{1,0:T(8,128)(2,1)S(1)}, bf16[128,768]{1,0:T(8,128)(2,1)}, u32[]{:S(2)}) copy-start(bf16[128,768]{1,0:T(8,128)(2,1)} %copy-done.15) | copy-start | bytes 589828
  151.2 24.1 %copy-start.1 = (bf16[1,5,3,2,128,128]{5,4,3,2,1,0:T(8,128)(2,1)S(1)}, bf16[1,5,3,2,128,128]{5,4,3,2,1,0:T(8,128)(2,1)}, u32[]{:S(2)}) copy-start(bf16[1,5,3,2,128,128]{5,4,3,2,1,0:T(8,128)(2,1)} %param.9) | copy-start | bytes 2949124
  151.2 26.6 %collective-permute-start.18 = (bf16[16,240,128]{2,1,0:T(8,128)(2,1)S(1)}, bf16[16,240,128]{2,1,0:T(8,128)(2,1)S(1)}, u32[]{:S(2)}, u32[]{:S(2)}) collective-permute-start(bf16[16,240,128]{2,1,0:T(8,128)(2,1)S(1)} %all_to_all.11.mine), channel_id=1, source_target_pairs={{0,16},{16,0},{32,48},{48,32},{64,80},{80,64},{96,112},{112,96},{1... | collective-permute-start | bytes 2949128 | tf_op jit(solution)/shard_map/ppermute | solution.py:205
  156.0 19.3 %copy-start.14 = (bf16[128,768]{1,0:T(8,128)(2,1)S(1)}, bf16[128,768]{1,0:T(8,128)(2,1)}, u32[]{:S(2)}) copy-start(bf16[128,768]{1,0:T(8,128)(2,1)} %copy-done.12) | copy-start | bytes 589828
  157.4 14.7 %collective-permute-start.10 = (bf16[128,384]{1,0:T(8,128)(2,1)S(1)}, bf16[128,384]{1,0:T(8,128)(2,1)S(1)}, u32[]{:S(2)}, u32[]{:S(2)}) collective-permute-start(bf16[128,384]{1,0:T(8,128)(2,1)S(1)} %get-tuple-element.34), channel_id=1, source_target_pairs={{0,1},{1,0},{2,3},{3,2},{4,5},{5,4},{6,7},{7,6},{8,9},{9,8},{10,11... | collective-permute-start | bytes 294920 | tf_op jit(solution)/shard_map/ppermute | solution.py:205
  160.4 11.7 %collective-permute-start.11 = (bf16[128,384]{1,0:T(8,128)(2,1)S(1)}, bf16[128,384]{1,0:T(8,128)(2,1)S(1)}, u32[]{:S(2)}, u32[]{:S(2)}) collective-permute-start(bf16[128,384]{1,0:T(8,128)(2,1)S(1)} %get-tuple-element.35), channel_id=1, source_target_pairs={{0,2},{1,3},{2,0},{3,1},{4,6},{5,7},{6,4},{7,5},{8,10},{9,11},{10,... | collective-permute-start | bytes 294920 | tf_op jit(solution)/shard_map/ppermute | solution.py:205
  164.6 7.5 %collective-permute-start.12 = (bf16[128,384]{1,0:T(8,128)(2,1)S(1)}, bf16[128,384]{1,0:T(8,128)(2,1)S(1)}, u32[]{:S(2)}, u32[]{:S(2)}) collective-permute-start(bf16[128,384]{1,0:T(8,128)(2,1)S(1)} %get-tuple-element.36), channel_id=1, source_target_pairs={{0,4},{1,5},{2,6},{3,7},{4,0},{5,1},{6,2},{7,3},{8,12},{9,13},{10,... | collective-permute-start | bytes 294920 | tf_op jit(solution)/shard_map/ppermute | solution.py:205
  167.7 6.9 %collective-permute-start.13 = (bf16[128,384]{1,0:T(8,128)(2,1)S(1)}, bf16[128,384]{1,0:T(8,128)(2,1)S(1)}, u32[]{:S(2)}, u32[]{:S(2)}) collective-permute-start(bf16[128,384]{1,0:T(8,128)(2,1)S(1)} %get-tuple-element.37), channel_id=1, source_target_pairs={{0,8},{1,9},{2,10},{3,11},{4,12},{5,13},{6,14},{7,15},{8,0},{9,1},... | collective-permute-start | bytes 294920 | tf_op jit(solution)/shard_map/ppermute | solution.py:205
  174.6 1.0 copy-start.5
  174.6 1.1 copy-start.8
  174.6 1.1 copy-start.11
  (10 other events, 8.0 us)
